TPU v7x, 32 devices: a whole 2x2x4 slice. The times are simulated.
32 devices in a mesh: gx: 8 (over z, core), gy: 4 (over y, x).
Axes of the slice: x: 2, y: 2, z: 4, core: 2. Of those that a mesh axis runs over, the one named last changes fastest.
Arguments:
- adjoint_forcing: float32 [16, 1536, 1536], P(None, 'gx', 'gy'), may hold values from -6 to 6
- courant_x: bfloat16 [16, 1536, 1536], P(None, 'gx', 'gy'), may hold values from -0.44921875 to 0.44921875
- courant_y: bfloat16 [16, 1536, 1536], P(None, 'gx', 'gy'), may hold values from -0.44921875 to 0.44921875
- vertical_mix: bfloat16 [16, 1536, 1536], P(None, 'gx', 'gy'), may hold values from 0.019897461 to 0.23925781
- tile_block: int32 [8192], replicated, may hold values from 0 to 36863, as said below
- injection_level: int32 [8192], P(('gx', 'gy')), may hold values from 0 to 15
- plume_profile: float32 [16, 16], replicated, may hold values from 0 to 1
- burn_weight: bfloat16 [8192, 6400], P(('gx', 'gy')), may hold values from 0.19921875 to 1
Outputs:
- adjoint_start: float32 [16, 1536, 1536], P(None, 'gx', 'gy')
- emission_gradient: bfloat16 [8192, 6400], P(('gx', 'gy'))
Inputs may be any that keep to these rules, and one draw needn't show every extreme that they name: `tile_block`: the tiles of one device lie on the columns of exactly 16 different devices, exactly 16 of them on each of those.
All inputs are finite; a program needn't handle non-finite values.
Results may differ from a plain program's by a relative error of at most 0.001.
Values sent between devices are 32-bit elements; how exact they have to be, the bound alone decides.
No kernel may reach another device: no remote copies, remote signals or barrier semaphores. Data moves between devices by JAX's collectives and lax.ppermute only.
A program may use at most 192 MiB of HBM per device.

v0:
```python
import functools

import jax
import jax.numpy as jnp
from jax import lax
from jax.experimental import pallas as pl
from jax.experimental.pallas import tpu as pltpu
from jax.sharding import PartitionSpec as P

ITERS = 4
TB = 8
SUB = 100
LANES = 128
SUBL = 8
ROWS = 16
FRONT = 2 * ROWS
HALO = ITERS

F32 = jnp.float32
BF16 = jnp.bfloat16
I32 = jnp.int32
ANY = pl.BlockSpec(memory_space=pl.ANY)
VMEM = pl.BlockSpec(memory_space=pltpu.VMEM)
SMEM = pl.BlockSpec(memory_space=pltpu.SMEM)


def params(mib, **kw):
    return pltpu.CompilerParams(vmem_limit_bytes=mib << 20, **kw)


def cost(flops, nbytes):
    return pl.CostEstimate(flops=flops, bytes_accessed=nbytes, transcendentals=0)


def lane_id(shape):
    return lax.broadcasted_iota(I32, shape, 1)


def pack_x_kernel(vt, vb, cut, cub, cvt, cvb, kt, kb, up, dn):
    h, b = (HALO, ROWS)

    def level(l, _):
        up[0, l] = jnp.concatenate([vt[l, :h], cut[l].astype(F32)[:h]], 0)
        up[1, l] = jnp.concatenate([cvt[l].astype(F32)[:h], kt[l].astype(F32)[:h]], 0)
        dn[0, l] = jnp.concatenate([vb[l, SUBL - h :], cub[l].astype(F32)[b - h :]], 0)
        dn[1, l] = jnp.concatenate([cvb[l].astype(F32)[b - h :], kb[l].astype(F32)[b - h :]], 0)
        return 0

    lax.fori_loop(0, vt.shape[0], level, 0)


def pack_x(v, cu, cv, k):
    lev, nx, ny = v.shape

    def ends(x, rows):
        last = nx // rows - 1
        return (
            pl.BlockSpec((lev, rows, ny), lambda i: (0, 0, 0)),
            pl.BlockSpec((lev, rows, ny), lambda i: (0, last, 0)),
        )

    specs = [s for x, r in ((v, SUBL), (cu, ROWS), (cv, ROWS), (k, ROWS)) for s in ends(x, r)]
    out = jax.ShapeDtypeStruct((2, lev, 2 * HALO, ny), F32)
    whole = pl.BlockSpec((2, lev, 2 * HALO, ny), lambda i: (0, 0, 0, 0))
    return pl.pallas_call(
        pack_x_kernel,
        grid=(1,),
        out_shape=(out, out),
        in_specs=specs,
        out_specs=(whole, whole),
        compiler_params=params(12),
        cost_estimate=cost(0, 3 << 20),
        name="pack_x",
    )(v, v, cu, cu, cv, cv, k, k)


def edge_lanes(rows, lev, right):
    per = LANES // lev
    lane = lane_id((rows, LANES))
    take = lane // lev + (LANES - per if right else 0)
    return take, lane % lev


def pack_edge(slabs, take, level):
    acc = None
    for l, slab in enumerate(slabs):
        got = jnp.take_along_axis(slab, take, axis=1)
        acc = got if acc is None else jnp.where(level == l, got, acc)
    return acc


def store_edges(packed, own, send, at, right):
    v, cu, cv, k = packed
    for i, x in enumerate(packed):
        own[i, at, :] = x
    low = lane_id(v.shape) < LANES // 2
    half = LANES // 2
    for i, (a, b) in enumerate(((v, cu), (cv, k))):
        if right:
            send[i, at, :] = jnp.where(low, pltpu.roll(a, half, 1), b)
        else:
            send[i, at, :] = jnp.where(low, a, pltpu.roll(b, half, 1))


def pack_y_kernel(*refs):
    ins, outs = (refs[:8], refs[8:])
    lev, rows, _ = ins[0].shape
    for side in range(2):
        take, level = edge_lanes(ROWS, lev, side == 1)
        for r in range(rows // ROWS):
            at = slice(r * ROWS, (r + 1) * ROWS)
            packed = [
                pack_edge([ins[2 * a + side][l, at, :].astype(F32) for l in range(lev)], take, level)
                for a in range(4)
            ]
            store_edges(packed, outs[2 * side], outs[2 * side + 1], at, side == 1)


def pack_y(v, cu, cv, k):
    lev, nx, ny = v.shape
    nt = ny // LANES
    rows = 2 * ROWS
    left = pl.BlockSpec((lev, rows, LANES), lambda i: (0, i, 0))
    right = pl.BlockSpec((lev, rows, LANES), lambda i: (0, i, nt - 1))
    own = jax.ShapeDtypeStruct((4, nx + SUBL, LANES), F32)
    send = jax.ShapeDtypeStruct((2, nx + SUBL, LANES), F32)
    own_spec = pl.BlockSpec((4, rows, LANES), lambda i: (0, i, 0))
    send_spec = pl.BlockSpec((2, rows, LANES), lambda i: (0, i, 0))
    return pl.pallas_call(
        pack_y_kernel,
        grid=(nx // rows,),
        out_shape=(own, send, own, send),
        in_specs=[left, right] * 4,
        out_specs=(own_spec, send_spec, own_spec, send_spec),
        compiler_params=params(12),
        cost_estimate=cost(0, 10 << 20),
        name="pack_y",
    )(v, v, cu, cu, cv, cv, k, k)


def pack_corner_kernel(above, below, *refs):
    outs = refs[4:]
    lev, ny = (above.shape[1], above.shape[3])
    for side in range(2):
        take, level = edge_lanes(SUBL, lev, side == 1)
        lanes = slice(ny - LANES, ny) if side else slice(0, LANES)
        packed = []
        for q, o in ((0, 0), (0, HALO), (1, 0), (1, HALO)):
            slabs = [
                jnp.concatenate([below[q, l, o : o + HALO, lanes], above[q, l, o : o + HALO, lanes]], 0)
                for l in range(lev)
            ]
            packed.append(pack_edge(slabs, take, level))
        store_edges(packed, outs[2 * side], outs[2 * side + 1], slice(0, SUBL), side == 1)


def pack_corner(above, below, edges):
    last = edges[0].shape[1] // SUBL - 1
    specs = [
        pl.BlockSpec((x.shape[0], SUBL, LANES), lambda i: (0, last, 0)) for x in edges
    ]
    full = pl.BlockSpec(above.shape, lambda i: (0, 0, 0, 0))
    return pl.pallas_call(
        pack_corner_kernel,
        grid=(1,),
        out_shape=tuple(jax.ShapeDtypeStruct(x.shape, x.dtype) for x in edges),
        in_specs=[full, full] + [ANY] * 4,
        out_specs=tuple(specs),
        input_output_aliases={2 + i: i for i in range(4)},
        compiler_params=params(8),
        cost_estimate=cost(0, 1 << 20),
        name="pack_corner",
    )(above, below, *edges)


def stencil_kernel(v_hbm, cu_hbm, cv_hbm, k_hbm, ab, be, out_hbm, wa, wb, cub, cvb, kb, sem, osem, *, lev, nx, nt):
    srcs = ((v_hbm, wa), (k_hbm, kb), (cu_hbm, cub), (cv_hbm, cvb))
    copies = [
        [
            pltpu.make_async_copy(
                s.at[:, :, pl.ds(LANES * j, LANES)], d.at[:, j, pl.ds(FRONT, nx), :], sem.at[i, j]
            )
            for j in range(nt)
        ]
        for i, (s, d) in enumerate(srcs)
    ]
    for group in copies:
        for c in group:
            c.start()
    rest = jnp.zeros((ROWS - HALO, LANES), F32)

    def halo(l, _):
        for j in range(nt):
            lanes = slice(LANES * j, LANES * (j + 1))
            for buf, q, o in ((wa, 0, 0), (cub, 0, HALO), (cvb, 1, 0), (kb, 1, HALO)):
                top = ab[q, l, o : o + HALO, lanes]
                low = be[q, l, o : o + HALO, lanes]
                buf[l, j, FRONT - ROWS : FRONT, :] = jnp.concatenate([rest, top], 0).astype(buf.dtype)
                buf[l, j, FRONT + nx : FRONT + nx + ROWS, :] = jnp.concatenate([low, rest], 0).astype(buf.dtype)
        return 0

    lax.fori_loop(0, lev, halo, 0)
    lane = lane_id((ROWS, LANES))
    first, last = (lane == 0, lane == LANES - 1)

    def load(ref, l, j, r, off=0):
        if off:
            return ref[l, j, pl.ds(r * ROWS + off, ROWS), :]
        return ref[l, j, pl.ds(pl.multiple_of(r * ROWS, ROWS), ROWS), :]

    def advect(src, l, r):
        mid = [load(src, l, j, r) for j in range(nt)]
        nxt = [pltpu.roll(x, LANES - 1, 1) for x in mid]
        prv = [pltpu.roll(x, 1, 1) for x in mid]
        out = []
        for j in range(nt):
            yp = jnp.where(last, nxt[j + 1], nxt[j]) if j + 1 < nt else nxt[j]
            ym = jnp.where(first, prv[j - 1], prv[j]) if j > 0 else prv[j]
            cu = load(cub, l, j, r).astype(F32)
            cv = load(cvb, l, j, r).astype(F32)
            wx = jnp.where(cu > 0, load(src, l, j, r, 1), load(src, l, j, r, -1))
            wy = jnp.where(cv > 0, yp, ym)
            out.append(mid[j] + jnp.abs(cu) * (wx - mid[j]) + jnp.abs(cv) * (wy - mid[j]))
        return out

    def block(src, dst, do_b, do_d, r):
        def get(l):
            if l >= lev:
                return None
            return advect(src, l, r) if do_b else [load(src, l, j, r) for j in range(nt)]

        at = pl.ds(pl.multiple_of(r * ROWS, ROWS), ROWS)
        cur, below = (get(0), None)
        for l in range(lev):
            nxt = get(l + 1)
            flux = []
            for j in range(nt):
                w = cur[j]
                if do_d:
                    if nxt is not None:
                        f = load(kb, l, j, r).astype(F32) * (nxt[j] - cur[j])
                        flux.append(f)
                        w = w + (f - below[j]) if below else w + f
                    else:
                        w = w - below[j]
                dst[l, j, at, :] = w
            cur, below = (nxt, flux)

    def sweep(src, dst, do_b, do_d, lo, hi):
        def body(r, _):
            block(src, dst, do_b, do_d, r)
            return 0

        lax.fori_loop(lo, hi, body, 0)

    begin, end = (FRONT // ROWS, (FRONT + nx) // ROWS)
    for group in copies[:2]:
        for c in group:
            c.wait()
    sweep(wa, wb, False, True, begin - 1, end + 1)
    for group in copies[2:]:
        for c in group:
            c.wait()
    src, dst = (wb, wa)
    for _ in range(1, ITERS):
        sweep(src, dst, True, True, begin - 1, end + 1)
        src, dst = (dst, src)
    sweep(src, dst, True, False, begin, end)
    done = pltpu.make_async_copy(dst.at[:, :, pl.ds(FRONT, nx), :], out_hbm, osem)
    done.start()
    done.wait()


def stencil(v, cu, cv, k, above, below):
    lev, nx, ny = v.shape
    nt = ny // LANES
    shape = (lev, nt, nx + 2 * FRONT, LANES)
    return pl.pallas_call(
        functools.partial(stencil_kernel, lev=lev, nx=nx, nt=nt),
        out_shape=jax.ShapeDtypeStruct((lev, nt, nx, LANES), F32),
        in_specs=[ANY] * 4 + [VMEM] * 2,
        out_specs=ANY,
        scratch_shapes=[
            pltpu.VMEM(shape, F32),
            pltpu.VMEM(shape, F32),
            pltpu.VMEM(shape, BF16),
            pltpu.VMEM(shape, BF16),
            pltpu.VMEM(shape, BF16),
            pltpu.SemaphoreType.DMA((4, nt)),
            pltpu.SemaphoreType.DMA,
        ],
        compiler_params=params(40),
        cost_estimate=cost(90 * lev * nx * ny, 60 << 20),
        name="stencil",
    )(v, cu, cv, k, above, below)


def index_kernel(me_ref, blocks, row, shift, pos, src_col, slot_col, *, per_x, per_y, gy, cap, nx):
    procs, tiles = blocks.shape
    me = me_ref[0]
    per_tile = LANES // TB

    def owner(b):
        br, bc = (b // (per_y * gy), b % (per_y * gy))
        return br // per_x * gy + bc // per_y, br % per_x, bc % per_y

    src, lr, lc = owner(blocks[...])
    mine = src == me
    t = lane_id((procs, tiles))
    upper = lax.broadcasted_iota(I32, (tiles, tiles), 0) <= lane_id((tiles, tiles))
    rank = jnp.dot(
        mine.astype(F32).astype(BF16), upper.astype(F32).astype(BF16), preferred_element_type=F32
    ).astype(I32)
    code = ((lc // per_tile * nx + lr * TB) * per_tile + lc % per_tile) * tiles + t + 1
    lane = lane_id((procs, LANES))
    found = jnp.zeros((procs, LANES), I32)
    for s in range(cap):
        hit = mine & (rank == s + 1)
        one = jnp.sum(jnp.where(hit, code, 0).astype(F32), axis=1, keepdims=True).astype(I32)
        found = jnp.where(lane == s, one, found)
    value = found - 1
    spot = value // tiles
    row[...] = jnp.where(found > 0, spot // per_tile, -1)
    shift[...] = (lane * TB - spot % per_tile * TB) & (LANES - 1)
    pos[...] = value % tiles
    own = owner(blocks[pl.ds(me, 1), :])[0]
    i = lax.broadcasted_iota(I32, (tiles, tiles), 0)
    j = lane_id((tiles, tiles))
    own_all = jnp.broadcast_to(own, (tiles, tiles)).astype(F32)
    col = jnp.sum(jnp.where(i == j, own_all, 0.0), axis=1, keepdims=True)
    same = (own_all == col) & (j < i)
    src_col[...] = col.astype(I32)
    slot_col[...] = jnp.sum(jnp.where(same, 1.0, 0.0), axis=1, keepdims=True).astype(I32)


def tile_indices(me, blocks, cap, per_x, per_y, gy, nx):
    procs, tiles = blocks.shape
    table = jax.ShapeDtypeStruct((procs, LANES), I32)
    column = jax.ShapeDtypeStruct((tiles, 1), I32)
    return pl.pallas_call(
        functools.partial(index_kernel, per_x=per_x, per_y=per_y, gy=gy, cap=cap, nx=nx),
        out_shape=(table, table, table, column, column),
        in_specs=[SMEM, VMEM],
        out_specs=(VMEM,) * 5,
        compiler_params=params(8),
        cost_estimate=cost(0, 1 << 20),
        name="tile_indices",
    )(me, blocks)


def finish_kernel(
    me_ref, row, shift, pos, inj, prof, mid_hbm, own_l, own_r, got_l, got_r, state, send,
    field, strip, other, coef, sem, osem, *, lev, nx, nt, cap, procs,
):
    fetch = [
        pltpu.make_async_copy(mid_hbm.at[:, j], field.at[:, pl.ds(j * nx, nx), :], sem.at[j])
        for j in range(nt)
    ]
    for c in fetch:
        c.start()
    rows = nx + 2 * HALO
    step = rows // 5 if rows % 40 == 0 else SUBL
    half = LANES // 2
    lane = lane_id((step, LANES))
    low = lane < half
    top_level = lane % lev == lev - 1
    head, tail = (lane < lev, lane >= LANES - lev)

    def turn(x):
        return pltpu.roll(x, half, 1)

    def gather(n, _):
        at = pl.ds(pl.multiple_of(n * step, SUBL), step)
        put = pl.ds(pl.multiple_of(n * step + SUBL, SUBL), step)
        for a in range(4):
            q = a // 2
            ol, orr = (own_l[a, at, :], own_r[a, at, :])
            gl, gr = (got_l[q, at, :], got_r[q, at, :])
            if a % 2:
                gl = turn(gl)
            else:
                gr = turn(gr)
            parts = (
                jnp.where(low, gl, turn(ol)),
                turn(jnp.where(low, orr, ol)),
                jnp.where(low, turn(orr), gr),
            )
            for i, x in enumerate(parts):
                if a == 0:
                    strip[i, put, :] = x
                elif a == 3:
                    coef[2, i, at, :] = jnp.where(top_level, 0.0, x)
                else:
                    coef[a - 1, i, at, :] = x
        return 0

    lax.fori_loop(0, rows // step, gather, 0)

    def diffuse(n, _):
        at = pl.ds(pl.multiple_of(n * step, SUBL), step)
        put = pl.ds(pl.multiple_of(n * step + SUBL, SUBL), step)
        for i in range(3):
            x = strip[i, put, :]
            f = coef[2, i, at, :] * (pltpu.roll(x, LANES - 1, 1) - x)
            other[i, put, :] = x + f - pltpu.roll(f, 1, 1)
        return 0

    def advect(n, _):
        at = pl.ds(pl.multiple_of(n * step, SUBL), step)
        put = pl.ds(pl.multiple_of(n * step + SUBL, SUBL), step)
        mid = [other[i, put, :] for i in range(3)]
        nxt = [pltpu.roll(x, LANES - lev, 1) for x in mid]
        prv = [pltpu.roll(x, lev, 1) for x in mid]
        yps = (jnp.where(tail, nxt[1], nxt[0]), jnp.where(tail, nxt[2], nxt[1]), nxt[2])
        yms = (prv[0], jnp.where(head, prv[0], prv[1]), jnp.where(head, prv[1], prv[2]))
        for i in range(3):
            cu, cv = (coef[0, i, at, :], coef[1, i, at, :])
            wx = jnp.where(
                cu > 0,
                other[i, pl.ds(n * step + SUBL + 1, step), :],
                other[i, pl.ds(n * step + SUBL - 1, step), :],
            )
            wy = jnp.where(cv > 0, yps[i], yms[i])
            strip[i, put, :] = mid[i] + jnp.abs(cu) * (wx - mid[i]) + jnp.abs(cv) * (wy - mid[i])
        return 0

    for _ in range(ITERS):
        lax.fori_loop(0, rows // step, diffuse, 0)
        for i in range(3):
            other[i, SUBL - 1 : SUBL, :] = other[i, SUBL + rows - 1 : SUBL + rows, :]
            other[i, SUBL + rows : SUBL + rows + 1, :] = other[i, SUBL : SUBL + 1, :]
        lax.fori_loop(0, rows // step, advect, 0)

    for c in fetch:
        c.wait()
    lane16 = lane_id((ROWS, LANES))
    width = HALO

    def patch(n, _):
        put = pl.ds(pl.multiple_of(n * ROWS + SUBL, SUBL), ROWS)
        left, right = (strip[0, put, :], strip[2, put, :])
        for l in range(lev):
            take_l = (lane16 * lev + (half + l)) & (LANES - 1)
            take_r = ((lane16 - (LANES - width)) * lev + l) & (LANES - 1)
            a = pl.ds(pl.multiple_of(n * ROWS, ROWS), ROWS)
            b = pl.ds(pl.multiple_of((nt - 1) * nx + n * ROWS, ROWS), ROWS)
            field[l, a, :] = jnp.where(lane16 < width, jnp.take_along_axis(left, take_l, axis=1), field[l, a, :])
            field[l, b, :] = jnp.where(
                lane16 >= LANES - width, jnp.take_along_axis(right, take_r, axis=1), field[l, b, :]
            )
        return 0

    lax.fori_loop(0, nx // ROWS, patch, 0)
    puts = [
        pltpu.make_async_copy(
            field.at[:, pl.ds(j * nx, nx), :], state.at[:, :, pl.ds(j * LANES, LANES)], osem.at[j]
        )
        for j in range(nt)
    ]
    for c in puts:
        c.start()
    me = me_ref[0]
    slot_of = lane_id((TB, LANES)) // TB

    def handler(h, _):
        @pl.when(row[h, 0] >= 0)
        def _():
            out = jnp.zeros((TB, LANES), F32)
            source = h ^ me
            for s in range(cap):
                at = pl.ds(pl.multiple_of(row[h, s], TB), TB)
                level = inj[source, pos[h, s]]
                acc = prof[level, 0] * field[0, at, :]
                for l in range(1, lev):
                    acc = acc + prof[level, l] * field[l, at, :]
                out = jnp.where(slot_of == s, pltpu.roll(acc, shift[h, s], 1), out)
            send[h] = out

        @pl.when(row[h, 0] < 0)
        def _():
            send[h] = jnp.zeros((TB, LANES), F32)

        return 0

    lax.fori_loop(0, procs, handler, 0)
    for c in puts:
        c.wait()


def finish(me, row, shift, pos, inj, prof, mid, own_l, own_r, got_l, got_r, cap):
    lev, nt, nx, _ = mid.shape
    procs = row.shape[0]
    rows = nx + 2 * HALO
    return pl.pallas_call(
        functools.partial(finish_kernel, lev=lev, nx=nx, nt=nt, cap=cap, procs=procs),
        out_shape=(
            jax.ShapeDtypeStruct((lev, nx, nt * LANES), F32),
            jax.ShapeDtypeStruct((procs, TB, LANES), F32),
        ),
        in_specs=[SMEM] * 6 + [ANY] + [VMEM] * 4,
        out_specs=(ANY, VMEM),
        scratch_shapes=[
            pltpu.VMEM((lev, nt * nx, LANES), F32),
            pltpu.VMEM((3, rows + 2 * SUBL, LANES), F32),
            pltpu.VMEM((3, rows + 2 * SUBL, LANES), F32),
            pltpu.VMEM((3, 3, rows, LANES), F32),
            pltpu.SemaphoreType.DMA((nt,)),
            pltpu.SemaphoreType.DMA((nt,)),
        ],
        compiler_params=params(20),
        cost_estimate=cost(30 << 20, 20 << 20),
        name="finish",
    )(me, row, shift, pos, inj, prof, mid, own_l, own_r, got_l, got_r)


def split3(x):
    hi = x.astype(BF16)
    rest = x - hi.astype(F32)
    mid = rest.astype(BF16)
    return hi, mid, (rest - mid.astype(F32)).astype(BF16)


def gradient_kernel(src, slot, got, burn, out, cols, *, cells):
    tiles, width = burn.shape
    procs = got.shape[0]
    step = pl.program_id(0)

    @pl.when(step == 0)
    def _():
        pick = (src[...] == lane_id((tiles, procs))).astype(F32).astype(BF16)
        pick3 = jnp.concatenate([pick] * 3, 1)
        lane = lane_id((tiles, LANES))
        keep = lane // TB == slot[...]
        col = jnp.zeros((tiles, LANES), F32)
        for a in range(TB):
            parts = jnp.concatenate(split3(got[:, a, :]), 0)
            t = jnp.where(keep, jnp.dot(pick3, parts, preferred_element_type=F32), 0.0)
            w = LANES // 2
            while w >= TB:
                t = t + pltpu.roll(t, w, 1)
                w //= 2
            col = jnp.where(lane // TB == a, t, col)
        hi, mid, lo = split3(col[:, :cells])
        cols[...] = jnp.concatenate([hi, mid, lo], 1)

    q = step * width + lane_id((cells, width))
    c = lax.broadcasted_iota(I32, (cells, width), 0) * SUB
    spread = ((q >= c) & (q < c + SUB)).astype(F32).astype(BF16)
    wide = jnp.dot(cols[...], jnp.concatenate([spread] * 3, 0), preferred_element_type=F32)
    out[...] = (burn[...].astype(F32) * wide).astype(BF16)


def gradient(src, slot, got, burn):
    tiles, fire = burn.shape
    cells = TB * TB
    width = max(w for w in range(LANES, 11 * LANES, LANES) if fire % w == 0)
    block = pl.BlockSpec((tiles, width), lambda i: (0, i))
    return pl.pallas_call(
        functools.partial(gradient_kernel, cells=cells),
        grid=(fire // width,),
        out_shape=jax.ShapeDtypeStruct((tiles, fire), BF16),
        in_specs=[
            pl.BlockSpec((tiles, 1), lambda i: (0, 0)),
            pl.BlockSpec((tiles, 1), lambda i: (0, 0)),
            pl.BlockSpec(got.shape, lambda i: (0, 0, 0)),
            block,
        ],
        out_specs=block,
        scratch_shapes=[pltpu.VMEM((tiles, 3 * cells), BF16)],
        compiler_params=params(16),
        cost_estimate=cost(2 * tiles * fire * 3 * cells, 7 << 20),
        name="gradient",
    )(src, slot, got, burn)


def shifts(axis):
    count = lax.axis_size(axis)
    up = [(i, i + 1) for i in range(count - 1)]
    return up, [(j, i) for i, j in up]


def on_device(
    adjoint_forcing,
    courant_x,
    courant_y,
    vertical_mix,
    tile_block,
    injection_level,
    plume_profile,
    burn_weight,
):
    lev, nx, ny = adjoint_forcing.shape
    gx, gy = (lax.axis_size("gx"), lax.axis_size("gy"))
    procs = gx * gy
    tiles = injection_level.shape[0]
    sources = min(tiles // 4, procs // 2)
    cap = tiles // sources
    me = lax.axis_index(("gx", "gy"))
    me1 = me.astype(I32).reshape(1)
    fields = (adjoint_forcing, courant_x, courant_y, vertical_mix)

    fwd, back = shifts("gx")
    up, down = pack_x(*fields)
    above = lax.ppermute(down, "gx", fwd)
    below = lax.ppermute(up, "gx", back)
    edges = pack_y(*fields)
    own_l, send_l, own_r, send_r = pack_corner(above, below, edges)
    fwd, back = shifts("gy")
    got_l = lax.ppermute(send_r, "gy", fwd)
    got_r = lax.ppermute(send_l, "gy", back)

    levels_all = injection_level.reshape(1, tiles)
    for axis, count in (("gy", gy), ("gx", gx)):
        bit = 1
        while bit < count:
            pairs = [(i, i ^ bit) for i in range(count)]
            levels_all = jnp.concatenate([levels_all, lax.ppermute(levels_all, axis, pairs)], 0)
            bit *= 2

    row, shift, pos, src, slot = tile_indices(
        me1, tile_block.reshape(procs, tiles), cap, nx // TB, ny // TB, gy, nx
    )
    mid = stencil(*fields, above, below)
    state, columns = finish(
        me1, row, shift, pos, levels_all, plume_profile, mid, own_l, own_r, got_l, got_r, cap
    )
    columns = lax.all_to_all(columns, ("gx", "gy"), split_axis=0, concat_axis=0, tiled=True)
    return state, gradient(src, slot, columns, burn_weight)


def solution(mesh):
    return jax.shard_map(
        on_device,
        mesh=mesh,
        in_specs=(
            P(None, "gx", "gy"),
            P(None, "gx", "gy"),
            P(None, "gx", "gy"),
            P(None, "gx", "gy"),
            P(),
            P(("gx", "gy")),
            P(),
            P(("gx", "gy"), None),
        ),
        out_specs=(P(None, "gx", "gy"), P(("gx", "gy"), None)),
        check_vma=False,
    )
```

profile of v0, /device:TPU:0, one launch (start us, length us, event | category | flops | bytes accessed | tf_op | source)
XLA Modules:
  0.0 112.6 jit_solution(4269363730375498107)
XLA Ops:
  0.6 0.0 copy-start
  0.6 2.3 %copy-done = f32[16,192,384]{2,1,0:T(8,128)S(1)} copy-done((f32[16,192,384]{2,1,0:T(8,128)S(1)}, f32[16,192,384]{2,1,0:T(8,128)}, u32[]{:S(2)}) %copy-start) | copy-done | bytes 4718616
  3.0 0.0 copy-start.1
  3.0 1.7 %copy-done.1 = bf16[16,192,384]{2,1,0:T(8,128)(2,1)S(1)} copy-done((bf16[16,192,384]{2,1,0:T(8,128)(2,1)S(1)}, bf16[16,192,384]{2,1,0:T(8,128)(2,1)}, u32[]{:S(2)}) %copy-start.1) | copy-done | bytes 2359320
  4.6 0.0 copy-start.3
  4.6 1.7 %copy-done.3 = bf16[16,192,384]{2,1,0:T(8,128)(2,1)S(1)} copy-done((bf16[16,192,384]{2,1,0:T(8,128)(2,1)S(1)}, bf16[16,192,384]{2,1,0:T(8,128)(2,1)}, u32[]{:S(2)}) %copy-start.3) | copy-done | bytes 2359320
  6.3 0.0 copy-start.5
  6.3 1.7 %copy-done.5 = bf16[16,192,384]{2,1,0:T(8,128)(2,1)S(1)} copy-done((bf16[16,192,384]{2,1,0:T(8,128)(2,1)S(1)}, bf16[16,192,384]{2,1,0:T(8,128)(2,1)}, u32[]{:S(2)}) %copy-start.5) | copy-done | bytes 2359320
  8.0 0.0 copy-start.23
  8.0 0.3 pack_x.1
  8.3 2.4 %collective-permute-start.5 = (f32[2,16,8,384]{3,2,1,0:T(8,128)S(1)}, f32[2,16,8,384]{3,2,1,0:T(8,128)S(1)}, u32[]{:S(2)}, u32[]{:S(2)}) collective-permute-start(f32[2,16,8,384]{3,2,1,0:T(8,128)S(1)} %get-tuple-element.22), channel_id=1, source_target_pairs={{0,4},{4,8},{8,12},{12,16},{16,20},{20,24},{24,28},{1,5},{5,9},{9,... | collective-permute-start | bytes 1179656 | tf_op jit(solution)/shard_map/ppermute | solution.py:604
  10.7 1.3 %collective-permute-start.6 = (f32[2,16,8,384]{3,2,1,0:T(8,128)S(1)}, f32[2,16,8,384]{3,2,1,0:T(8,128)S(1)}, u32[]{:S(2)}, u32[]{:S(2)}) collective-permute-start(f32[2,16,8,384]{3,2,1,0:T(8,128)S(1)} %get-tuple-element.23), channel_id=1, source_target_pairs={{4,0},{8,4},{12,8},{16,12},{20,16},{24,20},{28,24},{5,1},{9,5},{13... | collective-permute-start | bytes 1179656 | tf_op jit(solution)/shard_map/ppermute | solution.py:605
  12.0 0.0 copy-done.23
  12.0 2.4 %collective-permute-start = (s32[1,256]{1,0:T(1,128)S(1)}, s32[1,256]{1,0:T(1,128)S(1)}, u32[]{:S(2)}, u32[]{:S(2)}) collective-permute-start(s32[1,256]{1,0:T(1,128)S(1)} %bitcast.3), channel_id=1, source_target_pairs={{0,1},{1,0},{2,3},{3,2},{4,5},{5,4},{6,7},{7,6},{8,9},{9,8},{10,11... | collective-permute-start | bytes 3080 | tf_op jit(solution)/shard_map/ppermute | solution.py:617
  14.4 1.6 %collective-permute-done = s32[1,256]{1,0:T(1,128)S(1)} collective-permute-done((s32[1,256]{1,0:T(1,128)S(1)}, s32[1,256]{1,0:T(1,128)S(1)}, u32[]{:S(2)}, u32[]{:S(2)}) %collective-permute-start) | collective-permute-done | bytes 1056 | tf_op jit(solution)/shard_map/ppermute | solution.py:617
  15.9 0.0 copy-start.24
  16.0 0.0 copy-start.21
  16.0 2.1 %collective-permute-start.1 = (s32[2,256]{1,0:T(2,128)S(1)}, s32[2,256]{1,0:T(2,128)S(1)}, u32[]{:S(2)}, u32[]{:S(2)}) collective-permute-start(s32[2,256]{1,0:T(2,128)S(1)} %pad_add_fusion.2), channel_id=1, source_target_pairs={{0,2},{1,3},{2,0},{3,1},{4,6},{5,7},{6,4},{7,5},{8,10},{9,11},{10,... | collective-permute-start | bytes 6152 | tf_op jit(solution)/shard_map/ppermute | solution.py:617
  18.1 6.1 %pack_y.1 = (f32[4,200,128]{2,1,0:T(8,128)S(1)}, f32[2,200,128]{2,1,0:T(8,128)}, f32[4,200,128]{2,1,0:T(8,128)S(1)}, f32[2,200,128]{2,1,0:T(8,128)}) custom-call(f32[16,192,384]{2,1,0:T(8,128)S(1)} %copy-done, f32[16,192,384]{2,1,0:T(8,128)S(1)} %copy-done, bf16[16,192,384]{2,1,0:T(8,128)(2,1)S(1)} %copy-done.1, bf16[16,192,384]{2,1,0:T(8,128)(2,1)S(1)} %copy-done.1, ...), custom_call_target="tpu_custom_call" | custom-call | bytes 10485760 | tf_op jit(solution)/shard_map/pack_y/pallas_call | solution.py:129
  24.1 0.0 collective-permute-done.5.ab.above
  24.1 0.0 collective-permute-done.6.be.below
  24.1 0.0 copy-start.10
  24.2 0.9 pack_corner.1
  25.1 0.0 copy-done.8
  25.1 0.0 copy-done.10
  25.1 3.4 %collective-permute-start.7 = (f32[2,200,128]{2,1,0:T(8,128)}, f32[2,200,128]{2,1,0:T(8,128)S(1)}, u32[]{:S(2)}, u32[]{:S(2)}) collective-permute-start(f32[2,200,128]{2,1,0:T(8,128)} %get-tuple-element.30), channel_id=1, source_target_pairs={{0,1},{1,2},{2,3},{4,5},{5,6},{6,7},{8,9},{9,10},{10,11},{12,13},{... | collective-permute-start | bytes 614408 | tf_op jit(solution)/shard_map/ppermute | solution.py:609
  28.5 1.3 %collective-permute-start.8 = (f32[2,200,128]{2,1,0:T(8,128)}, f32[2,200,128]{2,1,0:T(8,128)}, u32[]{:S(2)}, u32[]{:S(2)}) collective-permute-start(f32[2,200,128]{2,1,0:T(8,128)} %get-tuple-element.31), channel_id=1, source_target_pairs={{1,0},{2,1},{3,2},{5,4},{6,5},{7,6},{9,8},{10,9},{11,10},{13,12},{... | collective-permute-start | bytes 614408 | tf_op jit(solution)/shard_map/ppermute | solution.py:610
  29.8 0.0 collective-permute-done.1
  29.8 0.8 collective-permute-start.2
  30.6 0.8 collective-permute-done.2
  31.5 3.7 %collective-permute-start.3 = (s32[8,256]{1,0:T(8,128)S(1)}, s32[8,256]{1,0:T(8,128)S(1)}, u32[]{:S(2)}, u32[]{:S(2)}) collective-permute-start(s32[8,256]{1,0:T(8,128)S(1)} %pad_add_fusion), channel_id=1, source_target_pairs={{0,8},{4,12},{8,0},{12,4},{16,24},{20,28},{24,16},{28,20},{1,9},{5... | collective-permute-start | bytes 24584 | tf_op jit(solution)/shard_map/ppermute | solution.py:617
  35.2 1.6 %collective-permute-done.3 = s32[8,256]{1,0:T(8,128)S(1)} collective-permute-done((s32[8,256]{1,0:T(8,128)S(1)}, s32[8,256]{1,0:T(8,128)S(1)}, u32[]{:S(2)}, u32[]{:S(2)}) %collective-permute-start.3) | collective-permute-done | bytes 8224 | tf_op jit(solution)/shard_map/ppermute | solution.py:617
  36.8 0.0 copy-done.24
  36.8 1.2 %concatenate.22 = s32[16,256]{1,0:T(8,128)} concatenate(s32[1,256]{1,0:T(1,128)S(1)} %bitcast.7, s32[1,256]{1,0:T(1,128)S(1)} %collective-permute-done, s32[2,256]{1,0:T(2,128)S(1)} %collective-permute-done.1, s32[4,256]{1,0:T(4,128)S(1)} %collective-permute-done.2, s32[8,256]{1,0:T(8,128)S(1)} %collective-permute-done.3), dimensions={0} | concatenate | bytes 32768 | tf_op jit(solution)/shard_map/concatenate | solution.py:617
  38.0 3.0 %collective-permute-start.4 = (s32[16,256]{1,0:T(8,128)}, s32[16,256]{1,0:T(8,128)}, u32[]{:S(2)}, u32[]{:S(2)}) collective-permute-start(s32[16,256]{1,0:T(8,128)} %concatenate.22), channel_id=1, source_target_pairs={{0,16},{4,20},{8,24},{12,28},{16,0},{20,4},{24,8},{28,12},{1,17},{... | collective-permute-start | bytes 49160 | tf_op jit(solution)/shard_map/ppermute | solution.py:617
  41.1 0.0 copy-done.22
  41.1 0.0 copy-done.21
  41.1 0.4 tile_indices.1
  41.5 0.0 copy-start.12
  41.5 0.6 copy-done.12
  42.2 0.6 copy-done.14
  42.8 0.6 copy-done.16
  43.4 0.6 copy-done.18
  44.0 0.0 collective-permute-done.4
  44.0 2.1 %concatenate.23.inj = s32[32,256]{1,0:T(8,128)S(1)} concatenate(s32[1,256]{1,0:T(1,128)} %bitcast.2, s32[1,256]{1,0:T(1,128)} %copy-done.24, s32[2,256]{1,0:T(2,128)S(1)} %collective-permute-done.1, s32[4,256]{1,0:T(4,128)S(1)} %collective-permute-done.2, s32[8,256]{1,0:T(8,128)} %copy-done.22, s32[16,256]{1,0:T(8,128)} %collective-permute-done.4), dimensions={0} | concatenate | bytes 65536 | tf_op jit(solution)/shard_map/concatenate | solution.py:617
  46.1 0.0 copy-done.2
  46.1 1.7 %copy-done.4 = bf16[16,192,384]{2,1,0:T(8,128)(2,1)S(1)} copy-done((bf16[16,192,384]{2,1,0:T(8,128)(2,1)S(1)}, bf16[16,192,384]{2,1,0:T(8,128)(2,1)}, u32[]{:S(2)}) %copy-start.4) | copy-done | bytes 2359320
  47.8 1.7 %copy-done.6 = bf16[16,192,384]{2,1,0:T(8,128)(2,1)S(1)} copy-done((bf16[16,192,384]{2,1,0:T(8,128)(2,1)S(1)}, bf16[16,192,384]{2,1,0:T(8,128)(2,1)}, u32[]{:S(2)}) %copy-start.6) | copy-done | bytes 2359320
  49.4 1.0 copy-done.9
  50.4 1.0 copy-done.11
  51.4 21.8 %stencil.1.mid_hbm = f32[16,3,192,128]{3,2,1,0:T(8,128)S(1)} custom-call(f32[16,192,384]{2,1,0:T(8,128)} %refs_1_.1, bf16[16,192,384]{2,1,0:T(8,128)(2,1)S(1)} %copy-done.2, bf16[16,192,384]{2,1,0:T(8,128)(2,1)S(1)} %copy-done.4, bf16[16,192,384]{2,1,0:T(8,128)(2,1)S(1)} %copy-done.6, f32[2,16,8,384]{3,2,1,0:T(8,128)S(1)} %copy-done.9, ...), custom_call_target="tpu_custom_call" | custom-call | flops 106168320 | bytes 62914560 | tf_op jit(solution)/shard_map/stencil/pallas_call | solution.py:278
  73.3 0.0 copy-start.7
  73.3 0.0 copy-start.13
  73.3 0.0 collective-permute-done.7.got_l
  73.3 0.0 collective-permute-done.8.got_r
  73.3 0.0 copy-done.15
  73.3 0.0 copy-done.17
  73.3 0.0 copy-done.19
  73.4 0.0 copy-done.20
  73.4 15.8 %finish.1 = (f32[16,192,384]{2,1,0:T(8,128)}, f32[32,8,128]{2,1,0:T(8,128)S(1)}) custom-call(s32[1]{0:T(128)} %bitcast.me_ref, s32[32,128]{1,0:T(8,128)S(1)} %copy-done.15, s32[32,128]{1,0:T(8,128)S(1)} %copy-done.17, s32[32,128]{1,0:T(8,128)S(1)} %copy-done.19, s32[32,256]{1,0:T(8,128)S(1)} %concatenate.23.inj, f32[16,16]{1,0:T(8,128)S(1)} %copy-done.20, ...), custom_call_target="tpu_custom_call" | custom-call | flops 31457280 | bytes 20971520 | tf_op jit(solution)/shard_map/finish/pallas_call | solution.py:494
  89.1 17.3 %all_to_all.5.got = f32[32,8,128]{2,1,0:T(8,128)S(1)} all-to-all(f32[32,8,128]{2,1,0:T(8,128)S(1)} %get-tuple-element.35), channel_id=1, replica_groups=mesh['gx'=8,'gy'=4] {'gx','gy'}, dimensions={0} | all-to-all | bytes 262144 | tf_op jit(solution)/shard_map/all_to_all | solution.py:627
  106.5 0.0 copy-done.7
  106.5 0.0 copy-done.13
  106.5 6.1 %gradient.1 = bf16[256,6400]{1,0:T(8,128)(2,1)} custom-call(s32[256,1]{1,0:T(8,128)S(1)} %get-tuple-element.33.src, s32[256,1]{1,0:T(8,128)S(1)} %copy-done.13, f32[32,8,128]{2,1,0:T(8,128)S(1)} %all_to_all.5.got, bf16[256,6400]{1,0:T(8,128)(2,1)S(1)} %copy-done.7), custom_call_target="tpu_custom_call" | custom-call | flops 629145600 | bytes 7340032 | tf_op jit(solution)/shard_map/gradient/pallas_call | solution.py:558
  (18 shorter events, 0.1 us)
Async XLA Ops:
  0.6 2.3 %copy-start = (f32[16,192,384]{2,1,0:T(8,128)S(1)}, f32[16,192,384]{2,1,0:T(8,128)}, u32[]{:S(2)}) copy-start(f32[16,192,384]{2,1,0:T(8,128)} %refs_1_.1) | copy-start | bytes 14155780
  3.0 1.7 %copy-start.1 = (bf16[16,192,384]{2,1,0:T(8,128)(2,1)S(1)}, bf16[16,192,384]{2,1,0:T(8,128)(2,1)}, u32[]{:S(2)}) copy-start(bf16[16,192,384]{2,1,0:T(8,128)(2,1)} %refs_3_.1) | copy-start | bytes 7077892
  4.6 1.7 %copy-start.3 = (bf16[16,192,384]{2,1,0:T(8,128)(2,1)S(1)}, bf16[16,192,384]{2,1,0:T(8,128)(2,1)}, u32[]{:S(2)}) copy-start(bf16[16,192,384]{2,1,0:T(8,128)(2,1)} %refs_5_.1) | copy-start | bytes 7077892
  6.3 1.7 %copy-start.5 = (bf16[16,192,384]{2,1,0:T(8,128)(2,1)S(1)}, bf16[16,192,384]{2,1,0:T(8,128)(2,1)}, u32[]{:S(2)}) copy-start(bf16[16,192,384]{2,1,0:T(8,128)(2,1)} %refs_7_.1) | copy-start | bytes 7077892
  8.0 4.0 %copy-start.23 = (s32[256]{0:T(256)S(1)}, s32[256]{0:T(256)}, u32[]{:S(2)}) copy-start(s32[256]{0:T(256)} %param.13) | copy-start | bytes 3076
  8.3 15.9 %collective-permute-start.5 = (f32[2,16,8,384]{3,2,1,0:T(8,128)S(1)}, f32[2,16,8,384]{3,2,1,0:T(8,128)S(1)}, u32[]{:S(2)}, u32[]{:S(2)}) collective-permute-start(f32[2,16,8,384]{3,2,1,0:T(8,128)S(1)} %get-tuple-element.22), channel_id=1, source_target_pairs={{0,4},{4,8},{8,12},{12,16},{16,20},{20,24},{24,28},{1,5},{5,9},{9,... | collective-permute-start | bytes 1179656 | tf_op jit(solution)/shard_map/ppermute | solution.py:604
  10.7 13.4 %collective-permute-start.6 = (f32[2,16,8,384]{3,2,1,0:T(8,128)S(1)}, f32[2,16,8,384]{3,2,1,0:T(8,128)S(1)}, u32[]{:S(2)}, u32[]{:S(2)}) collective-permute-start(f32[2,16,8,384]{3,2,1,0:T(8,128)S(1)} %get-tuple-element.23), channel_id=1, source_target_pairs={{4,0},{8,4},{12,8},{16,12},{20,16},{24,20},{28,24},{5,1},{9,5},{13... | collective-permute-start | bytes 1179656 | tf_op jit(solution)/shard_map/ppermute | solution.py:605
  12.0 3.9 %collective-permute-start = (s32[1,256]{1,0:T(1,128)S(1)}, s32[1,256]{1,0:T(1,128)S(1)}, u32[]{:S(2)}, u32[]{:S(2)}) collective-permute-start(s32[1,256]{1,0:T(1,128)S(1)} %bitcast.3), channel_id=1, source_target_pairs={{0,1},{1,0},{2,3},{3,2},{4,5},{5,4},{6,7},{7,6},{8,9},{9,8},{10,11... | collective-permute-start | bytes 3080 | tf_op jit(solution)/shard_map/ppermute | solution.py:617
  15.9 20.9 %copy-start.24 = (s32[1,256]{1,0:T(1,128)}, s32[1,256]{1,0:T(1,128)S(1)}, u32[]{:S(2)}) copy-start(s32[1,256]{1,0:T(1,128)S(1)} %collective-permute-done) | copy-start | bytes 3076
  16.0 25.1 %copy-start.21 = (s32[8192]{0:T(1024)S(1)}, s32[8192]{0:T(1024)}, u32[]{:S(2)}) copy-start(s32[8192]{0:T(1024)} %param.12) | copy-start | bytes 98308
  16.0 13.8 %collective-permute-start.1 = (s32[2,256]{1,0:T(2,128)S(1)}, s32[2,256]{1,0:T(2,128)S(1)}, u32[]{:S(2)}, u32[]{:S(2)}) collective-permute-start(s32[2,256]{1,0:T(2,128)S(1)} %pad_add_fusion.2), channel_id=1, source_target_pairs={{0,2},{1,3},{2,0},{3,1},{4,6},{5,7},{6,4},{7,5},{8,10},{9,11},{10,... | collective-permute-start | bytes 6152 | tf_op jit(solution)/shard_map/ppermute | solution.py:617
  18.1 28.0 %copy-start.2 = (bf16[16,192,384]{2,1,0:T(8,128)(2,1)S(1)}, bf16[16,192,384]{2,1,0:T(8,128)(2,1)}, u32[]{:S(2)}) copy-start(bf16[16,192,384]{2,1,0:T(8,128)(2,1)} %refs_3_.1) | copy-start | bytes 7077892
  24.1 0.9 copy-start.8
  24.1 0.9 copy-start.10
  25.1 48.2 %collective-permute-start.7 = (f32[2,200,128]{2,1,0:T(8,128)}, f32[2,200,128]{2,1,0:T(8,128)S(1)}, u32[]{:S(2)}, u32[]{:S(2)}) collective-permute-start(f32[2,200,128]{2,1,0:T(8,128)} %get-tuple-element.30), channel_id=1, source_target_pairs={{0,1},{1,2},{2,3},{4,5},{5,6},{6,7},{8,9},{9,10},{10,11},{12,13},{... | collective-permute-start | bytes 614408 | tf_op jit(solution)/shard_map/ppermute | solution.py:609
  28.5 44.8 %collective-permute-start.8 = (f32[2,200,128]{2,1,0:T(8,128)}, f32[2,200,128]{2,1,0:T(8,128)}, u32[]{:S(2)}, u32[]{:S(2)}) collective-permute-start(f32[2,200,128]{2,1,0:T(8,128)} %get-tuple-element.31), channel_id=1, source_target_pairs={{1,0},{2,1},{3,2},{5,4},{6,5},{7,6},{9,8},{10,9},{11,10},{13,12},{... | collective-permute-start | bytes 614408 | tf_op jit(solution)/shard_map/ppermute | solution.py:610
  29.8 1.6 %collective-permute-start.2 = (s32[4,256]{1,0:T(4,128)S(1)}, s32[4,256]{1,0:T(4,128)S(1)}, u32[]{:S(2)}, u32[]{:S(2)}) collective-permute-start(s32[4,256]{1,0:T(4,128)S(1)} %pad_add_fusion.1), channel_id=1, source_target_pairs={{0,4},{4,0},{8,12},{12,8},{16,20},{20,16},{24,28},{28,24},{1,5},{5... | collective-permute-start | bytes 12296 | tf_op jit(solution)/shard_map/ppermute | solution.py:617
  31.5 5.4 %collective-permute-start.3 = (s32[8,256]{1,0:T(8,128)S(1)}, s32[8,256]{1,0:T(8,128)S(1)}, u32[]{:S(2)}, u32[]{:S(2)}) collective-permute-start(s32[8,256]{1,0:T(8,128)S(1)} %pad_add_fusion), channel_id=1, source_target_pairs={{0,8},{4,12},{8,0},{12,4},{16,24},{20,28},{24,16},{28,20},{1,9},{5... | collective-permute-start | bytes 24584 | tf_op jit(solution)/shard_map/ppermute | solution.py:617
  36.8 4.2 %copy-start.22 = (s32[8,256]{1,0:T(8,128)}, s32[8,256]{1,0:T(8,128)S(1)}, u32[]{:S(2)}) copy-start(s32[8,256]{1,0:T(8,128)S(1)} %collective-permute-done.3) | copy-start | bytes 24580
  38.0 5.9 %collective-permute-start.4 = (s32[16,256]{1,0:T(8,128)}, s32[16,256]{1,0:T(8,128)}, u32[]{:S(2)}, u32[]{:S(2)}) collective-permute-start(s32[16,256]{1,0:T(8,128)} %concatenate.22), channel_id=1, source_target_pairs={{0,16},{4,20},{8,24},{12,28},{16,0},{20,4},{24,8},{28,12},{1,17},{... | collective-permute-start | bytes 49160 | tf_op jit(solution)/shard_map/ppermute | solution.py:617
  41.5 0.6 copy-start.12
  42.2 0.6 copy-start.14
  42.8 0.6 copy-start.16
  43.4 0.6 copy-start.18
  46.1 1.7 %copy-start.4 = (bf16[16,192,384]{2,1,0:T(8,128)(2,1)S(1)}, bf16[16,192,384]{2,1,0:T(8,128)(2,1)}, u32[]{:S(2)}) copy-start(bf16[16,192,384]{2,1,0:T(8,128)(2,1)} %refs_5_.1) | copy-start | bytes 7077892
  47.8 1.7 %copy-start.6 = (bf16[16,192,384]{2,1,0:T(8,128)(2,1)S(1)}, bf16[16,192,384]{2,1,0:T(8,128)(2,1)}, u32[]{:S(2)}) copy-start(bf16[16,192,384]{2,1,0:T(8,128)(2,1)} %refs_7_.1) | copy-start | bytes 7077892
  49.4 1.0 copy-start.9
  50.4 1.0 copy-start.11
  51.4 21.9 %copy-start.15 = (s32[32,128]{1,0:T(8,128)S(1)}, s32[32,128]{1,0:T(8,128)}, u32[]{:S(2)}) copy-start(s32[32,128]{1,0:T(8,128)} %copy-done.14) | copy-start | bytes 49156
  51.4 21.9 %copy-start.17 = (s32[32,128]{1,0:T(8,128)S(1)}, s32[32,128]{1,0:T(8,128)}, u32[]{:S(2)}) copy-start(s32[32,128]{1,0:T(8,128)} %copy-done.16) | copy-start | bytes 49156
  51.4 21.9 %copy-start.19 = (s32[32,128]{1,0:T(8,128)S(1)}, s32[32,128]{1,0:T(8,128)}, u32[]{:S(2)}) copy-start(s32[32,128]{1,0:T(8,128)} %copy-done.18) | copy-start | bytes 49156
  51.4 21.9 %copy-start.20 = (f32[16,16]{1,0:T(8,128)S(1)}, f32[16,16]{1,0:T(8,128)}, u32[]{:S(2)}) copy-start(f32[16,16]{1,0:T(8,128)} %prof.1) | copy-start | bytes 3076
  73.3 33.2 %copy-start.7 = (bf16[256,6400]{1,0:T(8,128)(2,1)S(1)}, bf16[256,6400]{1,0:T(8,128)(2,1)}, u32[]{:S(2)}) copy-start(bf16[256,6400]{1,0:T(8,128)(2,1)} %burn.1) | copy-start | bytes 9830404
  73.3 33.2 %copy-start.13 = (s32[256,1]{1,0:T(8,128)S(1)}, s32[256,1]{1,0:T(8,128)}, u32[]{:S(2)}) copy-start(s32[256,1]{1,0:T(8,128)} %copy-done.12) | copy-start | bytes 3076
where the time goes:
time: 113 us
  Pallas kernels  51.4 us (45%)
  starting transfers between devices  20.5 us (18%)
  local copies, waits for them, and re-layouts  18.5 us (16%)
  blocking collectives  17.3 us (15%)
  waiting for transfers between devices  4.02 us (4%)
    pallas_call x1, Pallas kernels, stencil(): pl.pallas_call(functools.partial(stencil_kernel, lev=lev, nx=nx, nt=nt),...  21.8 us
    all_to_all x1, blocking collectives, on_device(): lax.all_to_all(columns, ('gx', 'gy'), split_axis=0, concat_axis=0, tiled=...  17.3 us
    pallas_call x1, Pallas kernels, finish(): pl.pallas_call(functools.partial(finish_kernel, lev=lev, nx=nx, nt=nt, ca...  15.8 us
    unnamed x50, local copies, waits for them, and re-layouts  15.1 us
    ppermute x5, starting transfers between devices, on_device(): lax.ppermute(levels_all, axis, pairs)  12.1 us
    pallas_call x1, Pallas kernels, gradient(): pl.pallas_call(functools.partial(gradient_kernel, cells=cells), grid=(fir...  6.11 us
    pallas_call x1, Pallas kernels, pack_y(): pl.pallas_call(pack_y_kernel, grid=(nx // rows,), out_shape=(own, send, o...  6.05 us
    ppermute x5, waiting for transfers between devices, on_device(): lax.ppermute(levels_all, axis, pairs)  4.01 us
  transfers between devices with their start and end apart: 9, of which 3 were waited for; matrix products, arithmetic and copies ran while one was open for 3% of the time, Pallas kernels for 26%

commit v1 on v0

v1 whole, which is shorter than its diff:
```python
import functools

import jax
import jax.numpy as jnp
from jax import lax
from jax.experimental import pallas as pl
from jax.experimental.pallas import tpu as pltpu
from jax.sharding import PartitionSpec as P

ITERS = 4
TB = 8
SUB = 100
LANES = 128
SUBL = 8
ROWS = 16
FRONT = 2 * SUBL
EDGE = SUBL
HALO = ITERS
UNROLL = 8

F32 = jnp.float32
BF16 = jnp.bfloat16
I32 = jnp.int32
ANY = pl.BlockSpec(memory_space=pl.ANY)
HBM = pl.BlockSpec(memory_space=pltpu.HBM)
VMEM = pl.BlockSpec(memory_space=pltpu.VMEM)
SMEM = pl.BlockSpec(memory_space=pltpu.SMEM)


def params(mib, **kw):
    return pltpu.CompilerParams(vmem_limit_bytes=mib << 20, **kw)


def cost(flops, nbytes):
    return pl.CostEstimate(flops=flops, bytes_accessed=nbytes, transcendentals=0)


def lane_id(shape):
    return lax.broadcasted_iota(I32, shape, 1)


def pack_x_kernel(vt, vb, cut, cub, cvt, cvb, kt, kb, up, dn):
    h, b = (HALO, ROWS)

    def level(l, _):
        up[0, l] = jnp.concatenate([vt[l, :h], cut[l].astype(F32)[:h]], 0)
        up[1, l] = jnp.concatenate([cvt[l].astype(F32)[:h], kt[l].astype(F32)[:h]], 0)
        dn[0, l] = jnp.concatenate([vb[l, SUBL - h :], cub[l].astype(F32)[b - h :]], 0)
        dn[1, l] = jnp.concatenate([cvb[l].astype(F32)[b - h :], kb[l].astype(F32)[b - h :]], 0)
        return 0

    lax.fori_loop(0, vt.shape[0], level, 0)


def pack_x(v, cu, cv, k):
    lev, nx, ny = v.shape

    def ends(x, rows):
        last = nx // rows - 1
        return (
            pl.BlockSpec((lev, rows, ny), lambda i: (0, 0, 0)),
            pl.BlockSpec((lev, rows, ny), lambda i: (0, last, 0)),
        )

    specs = [s for x, r in ((v, SUBL), (cu, ROWS), (cv, ROWS), (k, ROWS)) for s in ends(x, r)]
    out = jax.ShapeDtypeStruct((2, lev, 2 * HALO, ny), F32)
    whole = pl.BlockSpec((2, lev, 2 * HALO, ny), lambda i: (0, 0, 0, 0))
    return pl.pallas_call(
        pack_x_kernel,
        grid=(1,),
        out_shape=(out, out),
        in_specs=specs,
        out_specs=(whole, whole),
        compiler_params=params(12),
        cost_estimate=cost(0, 3 << 20),
        name="pack_x",
    )(v, v, cu, cu, cv, cv, k, k)


def edge_lanes(rows, lev, right):
    per = LANES // lev
    lane = lane_id((rows, LANES))
    take = lane // lev + (LANES - per if right else 0)
    return take, lane % lev


def pack_edge(slabs, take, level):
    acc = None
    for l, slab in enumerate(slabs):
        got = jnp.take_along_axis(slab, take, axis=1)
        acc = got if acc is None else jnp.where(level == l, got, acc)
    return acc


def store_edges(packed, own, send, at, right):
    v, cu, cv, k = packed
    for i, x in enumerate(packed):
        own[i, at, :] = x
    low = lane_id(v.shape) < LANES // 2
    half = LANES // 2
    for i, (a, b) in enumerate(((v, cu), (cv, k))):
        if right:
            send[i, at, :] = jnp.where(low, pltpu.roll(a, half, 1), b)
        else:
            send[i, at, :] = jnp.where(low, a, pltpu.roll(b, half, 1))


def load_group(ref, l, j, g, off=0):
    if off:
        return ref[l, j, pl.ds(g * SUBL + (FRONT - EDGE) + off, SUBL), :]
    return ref[l, j, pl.ds(pl.multiple_of(g * SUBL + (FRONT - EDGE), SUBL), SUBL), :]


def load_coef(ref, l, j, g):
    return ref[l, j, pl.ds(pl.multiple_of(g * SUBL, SUBL), SUBL), :]


def diffuse(get, mix, put, lev, nt):
    cur, below = (get(0), None)
    for l in range(lev):
        nxt = get(l + 1) if l + 1 < lev else None
        flux = []
        for j in range(nt):
            w = cur[j]
            if nxt is not None:
                f = mix(l, j) * (nxt[j] - cur[j])
                flux.append(f)
                w = w + (f - below[j]) if below else w + f
            elif below:
                w = w - below[j]
            put(l, j, w)
        cur, below = (nxt, flux)


def prepare_kernel(
    v_hbm, cu_hbm, cv_hbm, k_hbm, w, cuf, cvf, kf, own_l, send_l, own_r, send_r, vs, cus, cvs, ks, sem,
    *, lev, nx, nt, chunks,
):
    part = nx // chunks
    copies = []
    for c in range(chunks):
        at = pl.ds(c * part, part)
        pairs = ((v_hbm, vs), (k_hbm, ks), (cu_hbm, cus), (cv_hbm, cvs))
        copies.append(
            [
                pltpu.make_async_copy(src.at[:, at, :], dst.at[:, at, :], sem.at[c, i])
                for i, (src, dst) in enumerate(pairs)
            ]
        )
    for group in copies:
        for c in group:
            c.start()
    takes = [edge_lanes(ROWS, lev, side == 1) for side in range(2)]

    def rows(r, _):
        at = pl.ds(pl.multiple_of(r * ROWS, ROWS), ROWS)
        put = pl.ds(pl.multiple_of(r * ROWS + EDGE, SUBL), ROWS)
        here = pl.ds(pl.multiple_of(r * ROWS + FRONT, SUBL), ROWS)
        lanes = [slice(LANES * j, LANES * (j + 1)) for j in range(nt)]
        for l in range(lev):
            for j in range(nt):
                for buf, raw in ((cuf, cus), (cvf, cvs), (kf, ks)):
                    buf[l, j, put, :] = raw[l, at, lanes[j]].astype(F32)

        def store(l, j, x):
            w[l, j, here, :] = x

        diffuse(
            lambda l: [vs[l, at, lanes[j]] for j in range(nt)],
            lambda l, j: ks[l, at, lanes[j]].astype(F32),
            store,
            lev,
            nt,
        )
        for side, (own, send) in enumerate(((own_l, send_l), (own_r, send_r))):
            edge = lanes[-1] if side else lanes[0]
            packed = [
                pack_edge([x[l, at, edge].astype(F32) for l in range(lev)], *takes[side])
                for x in (vs, cus, cvs, ks)
            ]
            store_edges(packed, own, send, at, side == 1)
        return 0

    for c in range(chunks):
        for x in copies[c]:
            x.wait()
        lax.fori_loop(c * part // ROWS, (c + 1) * part // ROWS, rows, 0)


def prepare(v, cu, cv, k):
    lev, nx, ny = v.shape
    nt = ny // LANES
    chunks = max(c for c in (1, 2, 3, 4) if nx % (c * ROWS) == 0)
    wide = jax.ShapeDtypeStruct((lev, nt, nx + 2 * EDGE, LANES), F32)
    own = jax.ShapeDtypeStruct((4, nx + SUBL, LANES), F32)
    send = jax.ShapeDtypeStruct((2, nx + SUBL, LANES), F32)
    return pl.pallas_call(
        functools.partial(prepare_kernel, lev=lev, nx=nx, nt=nt, chunks=chunks),
        out_shape=(jax.ShapeDtypeStruct((lev, nt, nx + 2 * FRONT, LANES), F32), wide, wide, wide, own, send, own, send),
        in_specs=[HBM] * 4,
        out_specs=(VMEM,) * 8,
        scratch_shapes=[pltpu.VMEM((lev, nx, ny), F32)]
        + [pltpu.VMEM((lev, nx, ny), BF16)] * 3
        + [pltpu.SemaphoreType.DMA((chunks, 4))],
        compiler_params=params(14),
        cost_estimate=cost(20 * lev * nx * ny, 34 << 20),
        name="prepare",
    )(v, cu, cv, k)


def fill_kernel(above, below, *refs, lev, nx, nt):
    w, cuf, cvf, kf = refs[8:12]
    outs = refs[12:]
    rest = jnp.zeros((SUBL - HALO, LANES), F32)

    def pair(l, j, q, o):
        lanes = slice(LANES * j, LANES * (j + 1))
        top = jnp.concatenate([rest, above[q, l, o : o + HALO, lanes]], 0)
        return top, jnp.concatenate([below[q, l, o : o + HALO, lanes], rest], 0)

    for end in range(2):
        to = (FRONT + nx) if end else (FRONT - SUBL)
        at = (EDGE + nx) if end else (EDGE - SUBL)

        def store(l, j, x):
            w[l, j, to : to + SUBL, :] = x

        diffuse(
            lambda l: [pair(l, j, 0, 0)[end] for j in range(nt)],
            lambda l, j: pair(l, j, 1, HALO)[end],
            store,
            lev,
            nt,
        )
        for l in range(lev):
            for j in range(nt):
                for buf, q, o in ((cuf, 0, HALO), (cvf, 1, 0), (kf, 1, HALO)):
                    buf[l, j, at : at + SUBL, :] = pair(l, j, q, o)[end]
    for side in range(2):
        take, level = edge_lanes(SUBL, lev, side == 1)
        lanes = slice(LANES * (nt - 1), LANES * nt) if side else slice(0, LANES)
        packed = []
        for q, o in ((0, 0), (0, HALO), (1, 0), (1, HALO)):
            slabs = [
                jnp.concatenate([below[q, l, o : o + HALO, lanes], above[q, l, o : o + HALO, lanes]], 0)
                for l in range(lev)
            ]
            packed.append(pack_edge(slabs, take, level))
        store_edges(packed, outs[2 * side], outs[2 * side + 1], slice(nx, nx + SUBL), side == 1)


def fill(above, below, arrays):
    lev, _, _, ny = above.shape
    nt = ny // LANES
    nx = arrays[4].shape[1] - SUBL
    return pl.pallas_call(
        functools.partial(fill_kernel, lev=above.shape[1], nx=nx, nt=nt),
        out_shape=tuple(jax.ShapeDtypeStruct(x.shape, x.dtype) for x in arrays),
        in_specs=[VMEM] * 10,
        out_specs=(VMEM,) * 8,
        input_output_aliases={2 + i: i for i in range(8)},
        compiler_params=params(3),
        cost_estimate=cost(0, 4 << 20),
        name="fill",
    )(above, below, *arrays)


def sweep_kernel(src, cuf, cvf, *refs, lev, nx, nt, last_step):
    dst = refs[-1]
    lane = lane_id((SUBL, LANES))
    first, last = (lane == 0, lane == LANES - 1)

    def advect(l, g):
        mid = [load_group(src, l, j, g) for j in range(nt)]
        nxt = [pltpu.roll(x, LANES - 1, 1) for x in mid]
        prv = [pltpu.roll(x, 1, 1) for x in mid]
        out = []
        for j in range(nt):
            yp = jnp.where(last, nxt[j + 1], nxt[j]) if j + 1 < nt else nxt[j]
            ym = jnp.where(first, prv[j - 1], prv[j]) if j > 0 else prv[j]
            cu, cv = (load_coef(cuf, l, j, g), load_coef(cvf, l, j, g))
            wx = jnp.where(cu > 0, load_group(src, l, j, g, 1), load_group(src, l, j, g, -1))
            wy = jnp.where(cv > 0, yp, ym)
            out.append(mid[j] + jnp.abs(cu) * (wx - mid[j]) + jnp.abs(cv) * (wy - mid[j]))
        return out

    def body(g, _):
        if last_step:
            at = pl.ds(pl.multiple_of(g * SUBL - EDGE, SUBL), SUBL)
            for l in range(lev):
                for j, x in enumerate(advect(l, g)):
                    dst[l, j, at, :] = x
            return 0
        at = pl.ds(pl.multiple_of(g * SUBL + (FRONT - EDGE), SUBL), SUBL)

        def store(l, j, x):
            dst[l, j, at, :] = x

        diffuse(lambda l: advect(l, g), lambda l, j: load_coef(refs[0], l, j, g), store, lev, nt)
        return 0

    groups = nx // SUBL
    lo, hi = (1, groups + 1) if last_step else (0, groups + 2)
    whole = (hi - lo) // UNROLL

    def several(i, _):
        for n in range(UNROLL):
            body(lo + i * UNROLL + n, 0)
        return 0

    lax.fori_loop(0, whole, several, 0)
    for g in range(lo + whole * UNROLL, hi):
        body(g, 0)


def sweep(src, cuf, cvf, kf, last_step):
    lev, nt, rows, _ = src.shape
    nx = rows - 2 * FRONT
    ins = (src, cuf, cvf) if last_step else (src, cuf, cvf, kf)
    shape = (lev, nt, nx, LANES) if last_step else src.shape
    return pl.pallas_call(
        functools.partial(sweep_kernel, lev=lev, nx=nx, nt=nt, last_step=last_step),
        out_shape=jax.ShapeDtypeStruct(shape, F32),
        in_specs=[VMEM] * len(ins),
        out_specs=VMEM,
        compiler_params=params(3),
        cost_estimate=cost(18 * lev * nt * nx * LANES, 16 << 20),
        name="sweep_last" if last_step else "sweep",
    )(*ins)


def index_kernel(me_ref, blocks, row, shift, pos, src_col, slot_col, *, tiles, per_x, per_y, gy, cap, nx):
    per = tiles // LANES
    procs = blocks.shape[0] // per
    me = me_ref[0]
    per_tile = LANES // TB

    def lines(start, count, stride):
        return jnp.concatenate([blocks[pl.ds(start + i, count, stride), :] for i in range(per)], 1)

    def owner(b):
        br, bc = (b // (per_y * gy), b % (per_y * gy))
        return br // per_x * gy + bc // per_y, br % per_x, bc % per_y

    src, lr, lc = owner(lines(0, procs, per))
    mine = src == me
    t = lane_id((procs, tiles))
    upper = lax.broadcasted_iota(I32, (tiles, tiles), 0) <= lane_id((tiles, tiles))
    rank = jnp.dot(
        mine.astype(F32).astype(BF16), upper.astype(F32).astype(BF16), preferred_element_type=F32
    ).astype(I32)
    code = ((lc // per_tile * nx + lr * TB) * per_tile + lc % per_tile) * tiles + t + 1
    lane = lane_id((procs, LANES))
    found = jnp.zeros((procs, LANES), I32)
    for s in range(cap):
        hit = mine & (rank == s + 1)
        one = jnp.sum(jnp.where(hit, code, 0).astype(F32), axis=1, keepdims=True).astype(I32)
        found = jnp.where(lane == s, one, found)
    value = found - 1
    spot = value // tiles
    row[...] = jnp.where(found > 0, spot // per_tile, -1)
    shift[...] = (lane * TB - spot % per_tile * TB) & (LANES - 1)
    pos[...] = value % tiles
    own = owner(lines(me * per, 1, 1))[0]
    i = lax.broadcasted_iota(I32, (tiles, tiles), 0)
    j = lane_id((tiles, tiles))
    own_all = jnp.broadcast_to(own, (tiles, tiles)).astype(F32)
    col = jnp.sum(jnp.where(i == j, own_all, 0.0), axis=1, keepdims=True)
    same = (own_all == col) & (j < i)
    src_col[...] = col.astype(I32)
    slot_col[...] = jnp.sum(jnp.where(same, 1.0, 0.0), axis=1, keepdims=True).astype(I32)


def tile_indices(me, blocks, procs, cap, per_x, per_y, gy, nx):
    tiles = blocks.shape[0] // procs
    blocks = blocks.reshape(-1, LANES)
    table = jax.ShapeDtypeStruct((procs, LANES), I32)
    column = jax.ShapeDtypeStruct((tiles, 1), I32)
    return pl.pallas_call(
        functools.partial(index_kernel, tiles=tiles, per_x=per_x, per_y=per_y, gy=gy, cap=cap, nx=nx),
        out_shape=(table, table, table, column, column),
        in_specs=[SMEM, VMEM],
        out_specs=(VMEM,) * 5,
        compiler_params=params(8),
        cost_estimate=cost(0, 1 << 20),
        name="tile_indices",
    )(me, blocks)


def strips_kernel(own_l, own_r, got_l, got_r, out_l, out_r, strip, other, coef, *, lev, nx):
    rows = nx + 2 * HALO
    step = rows
    half = LANES // 2
    lane = lane_id((step, LANES))
    low = lane < half
    top_level = lane % lev == lev - 1
    head, tail = (lane < lev, lane >= LANES - lev)

    def turn(x):
        return pltpu.roll(x, half, 1)

    def gather(n, _):
        at = pl.ds(pl.multiple_of(n * step, SUBL), step)
        put = pl.ds(pl.multiple_of(n * step + SUBL, SUBL), step)
        for a in range(4):
            q = a // 2
            ol, orr = (own_l[a, at, :], own_r[a, at, :])
            gl, gr = (got_l[q, at, :], got_r[q, at, :])
            if a % 2:
                gl = turn(gl)
            else:
                gr = turn(gr)
            parts = (
                jnp.where(low, gl, turn(ol)),
                turn(jnp.where(low, orr, ol)),
                jnp.where(low, turn(orr), gr),
            )
            for i, x in enumerate(parts):
                if a == 0:
                    strip[i, put, :] = x
                elif a == 3:
                    coef[2, i, at, :] = jnp.where(top_level, 0.0, x)
                else:
                    coef[a - 1, i, at, :] = x
        return 0

    lax.fori_loop(0, rows // step, gather, 0)

    def diffuse(n, _):
        at = pl.ds(pl.multiple_of(n * step, SUBL), step)
        put = pl.ds(pl.multiple_of(n * step + SUBL, SUBL), step)
        for i in range(3):
            x = strip[i, put, :]
            f = coef[2, i, at, :] * (pltpu.roll(x, LANES - 1, 1) - x)
            other[i, put, :] = x + f - pltpu.roll(f, 1, 1)
        return 0

    def advect(n, _):
        at = pl.ds(pl.multiple_of(n * step, SUBL), step)
        put = pl.ds(pl.multiple_of(n * step + SUBL, SUBL), step)
        mid = [other[i, put, :] for i in range(3)]
        nxt = [pltpu.roll(x, LANES - lev, 1) for x in mid]
        prv = [pltpu.roll(x, lev, 1) for x in mid]
        yps = (jnp.where(tail, nxt[1], nxt[0]), jnp.where(tail, nxt[2], nxt[1]), nxt[2])
        yms = (prv[0], jnp.where(head, prv[0], prv[1]), jnp.where(head, prv[1], prv[2]))
        for i in range(3):
            cu, cv = (coef[0, i, at, :], coef[1, i, at, :])
            wx = jnp.where(
                cu > 0,
                other[i, pl.ds(n * step + SUBL + 1, step), :],
                other[i, pl.ds(n * step + SUBL - 1, step), :],
            )
            wy = jnp.where(cv > 0, yps[i], yms[i])
            strip[i, put, :] = mid[i] + jnp.abs(cu) * (wx - mid[i]) + jnp.abs(cv) * (wy - mid[i])
        return 0

    for _ in range(ITERS):
        lax.fori_loop(0, rows // step, diffuse, 0)
        for i in range(3):
            other[i, SUBL - 1 : SUBL, :] = other[i, SUBL + rows - 1 : SUBL + rows, :]
            other[i, SUBL + rows : SUBL + rows + 1, :] = other[i, SUBL : SUBL + 1, :]
        lax.fori_loop(0, rows // step, advect, 0)

    out_l[...] = strip[0, SUBL : SUBL + nx, :]
    out_r[...] = strip[2, SUBL : SUBL + nx, :]


def strips(own_l, own_r, got_l, got_r, lev):
    rows = own_l.shape[1]
    nx = rows - 2 * HALO
    out = jax.ShapeDtypeStruct((nx, LANES), F32)
    return pl.pallas_call(
        functools.partial(strips_kernel, lev=lev, nx=nx),
        out_shape=(out, out),
        in_specs=[VMEM] * 4,
        out_specs=(VMEM, VMEM),
        scratch_shapes=[
            pltpu.VMEM((3, rows + 2 * SUBL, LANES), F32),
            pltpu.VMEM((3, rows + 2 * SUBL, LANES), F32),
            pltpu.VMEM((3, 3, rows, LANES), F32),
        ],
        compiler_params=params(8),
        cost_estimate=cost(10 << 20, 3 << 20),
        name="strips",
    )(own_l, own_r, got_l, got_r)


def finish_kernel(
    me_ref, row, shift, pos, inj, prof, edge_l, edge_r, mid, state, send, field, weight, osem,
    *, lev, nx, nt, cap, procs, order,
):
    def spread(i, _):
        for l in range(lev):
            weight[i, l] = jnp.full((TB, LANES), prof[i, l], F32)
        return 0

    lax.fori_loop(0, lev, spread, 0)
    lane16 = lane_id((ROWS, LANES))
    width = HALO

    def patch(n, _):
        a = pl.ds(pl.multiple_of(n * ROWS, ROWS), ROWS)
        left, right = (edge_l[a, :], edge_r[a, :])
        for l in range(lev):
            take_l = (lane16 * lev + (LANES // 2 + l)) & (LANES - 1)
            take_r = ((lane16 - (LANES - width)) * lev + l) & (LANES - 1)
            b = pl.ds(pl.multiple_of((nt - 1) * nx + n * ROWS, ROWS), ROWS)
            field[l, a, :] = jnp.where(lane16 < width, jnp.take_along_axis(left, take_l, axis=1), field[l, a, :])
            field[l, b, :] = jnp.where(
                lane16 >= LANES - width, jnp.take_along_axis(right, take_r, axis=1), field[l, b, :]
            )
        return 0

    lax.fori_loop(0, nx // ROWS, patch, 0)
    puts = [
        pltpu.make_async_copy(
            field.at[:, pl.ds(j * nx, nx), :], state.at[:, :, pl.ds(j * LANES, LANES)], osem.at[j]
        )
        for j in range(nt)
    ]
    for c in puts:
        c.start()
    me = me_ref[0]
    slot_of = lane_id((TB, LANES)) // TB

    def handler(h, _):
        @pl.when(row[h, 0] >= 0)
        def _():
            out = jnp.zeros((TB, LANES), F32)
            apart = h ^ me
            source = 0
            for n, bit in enumerate(order):
                source = source + ((apart // bit) & 1) * (1 << n)
            for s in range(cap):
                at = pl.ds(pl.multiple_of(row[h, s], TB), TB)
                level = inj[source, pos[h, s]]
                terms = [weight[level, l] * field[l, at, :] for l in range(lev)]
                while len(terms) > 1:
                    terms = [x + y for x, y in zip(terms[::2], terms[1::2])]
                acc = terms[0]
                out = jnp.where(slot_of == s, pltpu.roll(acc, shift[h, s], 1), out)
            send[h] = out

        @pl.when(row[h, 0] < 0)
        def _():
            send[h] = jnp.zeros((TB, LANES), F32)

        return 0

    lax.fori_loop(0, procs, handler, 0)
    for c in puts:
        c.wait()


def finish(me, row, shift, pos, inj, prof, edge_l, edge_r, mid, cap, order):
    lev, nt, nx, _ = mid.shape
    procs = row.shape[0]
    mid = mid.reshape(lev, nt * nx, LANES)
    return pl.pallas_call(
        functools.partial(finish_kernel, lev=lev, nx=nx, nt=nt, cap=cap, procs=procs, order=order),
        out_shape=(
            jax.ShapeDtypeStruct((lev, nx, nt * LANES), F32),
            jax.ShapeDtypeStruct((procs, TB, LANES), F32),
            jax.ShapeDtypeStruct(mid.shape, F32),
        ),
        in_specs=[SMEM] * 6 + [VMEM] * 3,
        out_specs=(HBM, VMEM, VMEM),
        input_output_aliases={8: 2},
        scratch_shapes=[pltpu.VMEM((lev, lev, TB, LANES), F32), pltpu.SemaphoreType.DMA((nt,))],
        compiler_params=params(4),
        cost_estimate=cost(30 << 20, 20 << 20),
        name="finish",
    )(me, row, shift, pos, inj, prof, edge_l, edge_r, mid)


def split3(x):
    hi = x.astype(BF16)
    rest = x - hi.astype(F32)
    mid = rest.astype(BF16)
    return hi, mid, (rest - mid.astype(F32)).astype(BF16)


def gradient_kernel(src, slot, got, burn, out, cols, parts, *, cells):
    tiles, width = burn.shape
    procs = got.shape[0]
    step = pl.program_id(0)
    block = min(tiles, 8 * SUBL)

    @pl.when(step == 0)
    def _():
        for a in range(TB):
            parts[a] = jnp.concatenate(split3(got[:, a, :]), 0)
        lane = lane_id((block, LANES))
        low = lane < cells
        who = lane_id((block, 3 * procs)) % procs

        def rows(n, _):
            at = pl.ds(pl.multiple_of(n * block, block), block)
            pick = (who == src[at, :]).astype(F32).astype(BF16)
            keep = lane // TB == slot[at, :]
            t = [
                jnp.where(keep, jnp.dot(pick, parts[a], preferred_element_type=F32), 0.0)
                for a in range(TB)
            ]
            w = TB
            while len(t) > 1:
                even = lane & w == 0
                t = [
                    jnp.where(even, x, y) + pltpu.roll(jnp.where(even, y, x), w, 1)
                    for x, y in zip(t[::2], t[1::2])
                ]
                w *= 2
            col = t[0]
            while w < LANES:
                col = col + pltpu.roll(col, w, 1)
                w *= 2
            hi = col.astype(BF16).astype(F32)
            mid = (col - hi).astype(BF16).astype(F32)
            cols[at, :LANES] = jnp.where(low, hi, mid).astype(BF16)
            cols[at, LANES:] = jnp.where(low, col - hi - mid, 0.0).astype(BF16)
            return 0

        lax.fori_loop(0, tiles // block, rows, 0)

    q = step * width + lane_id((cells, width))
    c = lax.broadcasted_iota(I32, (cells, width), 0) * SUB
    spread = ((q >= c) & (q < c + SUB)).astype(F32).astype(BF16)
    wide = jnp.dot(
        cols[...], jnp.concatenate([spread] * (2 * LANES // cells), 0), preferred_element_type=F32
    )
    out[...] = (burn[...].astype(F32) * wide).astype(BF16)


def gradient(src, slot, got, burn):
    tiles, fire = burn.shape
    cells = TB * TB
    procs = got.shape[0]
    width = max(w for w in range(LANES, 11 * LANES, LANES) if fire % w == 0)
    block = pl.BlockSpec((tiles, width), lambda i: (0, i))
    return pl.pallas_call(
        functools.partial(gradient_kernel, cells=cells),
        grid=(fire // width,),
        out_shape=jax.ShapeDtypeStruct((tiles, fire), BF16),
        in_specs=[
            pl.BlockSpec((tiles, 1), lambda i: (0, 0)),
            pl.BlockSpec((tiles, 1), lambda i: (0, 0)),
            pl.BlockSpec(got.shape, lambda i: (0, 0, 0)),
            block,
        ],
        out_specs=block,
        scratch_shapes=[pltpu.VMEM((tiles, 2 * LANES), BF16), pltpu.VMEM((TB, 3 * procs, LANES), BF16)],
        compiler_params=params(16),
        cost_estimate=cost(2 * tiles * fire * 4 * cells, 7 << 20),
        name="gradient",
    )(src, slot, got, burn)


def shifts(axis):
    count = lax.axis_size(axis)
    up = [(i, i + 1) for i in range(count - 1)]
    return up, [(j, i) for i, j in up]


def bits(count):
    return [1 << n for n in range(count.bit_length() - 1)]


def on_device(
    adjoint_forcing,
    courant_x,
    courant_y,
    vertical_mix,
    tile_block,
    injection_level,
    plume_profile,
    burn_weight,
):
    lev, nx, ny = adjoint_forcing.shape
    gx, gy = (lax.axis_size("gx"), lax.axis_size("gy"))
    procs = gx * gy
    tiles = injection_level.shape[0]
    sources = min(tiles // 4, procs // 2)
    cap = tiles // sources
    me = lax.axis_index(("gx", "gy"))
    me1 = me.astype(I32).reshape(1)
    fields = tuple(
        pltpu.with_memory_space_constraint(x, pltpu.HBM)
        for x in (adjoint_forcing, courant_x, courant_y, vertical_mix)
    )

    steps = [("gx", b) for b in bits(gx)[::-1][:-1]] + [("gy", b) for b in bits(gy)[::-1]] + [("gx", 1)]
    order = tuple(b * gy if axis == "gx" else b for axis, b in steps)
    known = injection_level.reshape(1, tiles)

    def widen(known, step):
        axis, bit = step
        pairs = [(i, i ^ bit) for i in range(lax.axis_size(axis))]
        return jnp.concatenate([known, lax.ppermute(known, axis, pairs)], 0)

    up, down = pack_x(*fields)
    row, shift, pos, src, slot, up, down = lax.optimization_barrier(
        tuple(tile_indices(me1, tile_block, procs, cap, nx // TB, ny // TB, gy, nx)) + (up, down)
    )
    fwd, back = shifts("gx")
    above = lax.ppermute(down, "gx", fwd)
    below = lax.ppermute(up, "gx", back)
    arrays = fill(above, below, prepare(*fields))
    w, cu, cv, k, own_l, send_l, own_r, send_r = arrays
    fwd, back = shifts("gy")
    got_l = lax.ppermute(send_r, "gy", fwd)
    got_r = lax.ppermute(send_l, "gy", back)
    todo = list(steps)
    for n in range(ITERS):
        known, w = lax.optimization_barrier((known, w))
        share = len(todo[:-1]) // (ITERS - n) if n + 1 < ITERS else len(todo[:-1])
        for step in todo[:share]:
            known = widen(known, step)
        todo = todo[share:]
        w = sweep(w, cu, cv, k, n + 1 == ITERS)
    known, w, got_l, got_r = lax.optimization_barrier((known, w, got_l, got_r))
    for step in todo:
        known = widen(known, step)
    edge_l, edge_r = strips(own_l, own_r, got_l, got_r, lev)
    state, columns, _ = finish(
        me1, row, shift, pos, known, plume_profile, edge_l, edge_r, w, cap, order
    )
    columns = lax.all_to_all(columns, ("gx", "gy"), split_axis=0, concat_axis=0, tiled=True)
    return state, gradient(src, slot, columns, burn_weight)


def solution(mesh):
    return jax.shard_map(
        on_device,
        mesh=mesh,
        in_specs=(
            P(None, "gx", "gy"),
            P(None, "gx", "gy"),
            P(None, "gx", "gy"),
            P(None, "gx", "gy"),
            P(),
            P(("gx", "gy")),
            P(),
            P(("gx", "gy"), None),
        ),
        out_specs=(P(None, "gx", "gy"), P(("gx", "gy"), None)),
        check_vma=False,
    )
```

time: 113 us -> 78.1 us (0.69)
  local copies, waits for them, and re-layouts: 18.5 us -> 1.02 us
  Pallas kernels: 51.4 us -> 40.4 us
  waiting for transfers between devices: 4.02 us -> 0.02 us
  blocking collectives: 17.3 us -> 15.3 us
    unnamed x50 -> x8, local copies, waits for them, and re-layouts: 15.1 us -> 1.02 us
    pallas_call x1, Pallas kernels: 15.8 us -> 8.62 us  [finish(): pl.pallas_call(functools.partial(finish_kernel, lev=lev, nx=nx, nt=nt, ca...]
    pallas_call x4 -> x8, Pallas kernels: 29.2 us -> 23.7 us  [the longest x4 12.9 us: sweep(): pl.pallas_call(functools.partial(sweep_kernel, lev=lev, nx=nx, nt=nt, las...]
    ppermute x5, waiting for transfers between devices: 4.01 us -> 0.01 us  [widen(): return jnp.concatenate([known, lax.ppermute(known, axis, pairs)], 0)]
    concatenate x2 -> x0, local copies, waits for them, and re-layouts: 3.31 us -> none  [on_device(): jnp.concatenate([levels_all, lax.ppermute(levels_all, axis, pairs)], 0)]
    all_to_all x1, blocking collectives: 17.3 us -> 15.3 us  [on_device(): lax.all_to_all(columns, ('gx', 'gy'), split_axis=0, concat_axis=0, tiled=...]
    pallas_call x1, Pallas kernels: 0.3 us -> 1.64 us  [pack_x(): pl.pallas_call(pack_x_kernel, grid=(1,), out_shape=(out, out), in_specs=s...]
  transfers between devices with their start and end apart: 9 -> 9, of which waited for: 3 -> 0; matrix products, arithmetic and copies ran while one was open for 3% -> 0% of each run, Pallas kernels for 26% -> 29%
where the time goes in v1:
time: 78.1 us; the launch traced here: 78 us
  Pallas kernels  40.4 us (52%)
  starting transfers between devices  20.3 us (26%)
  blocking collectives  15.3 us (20%)
  local copies, waits for them, and re-layouts  1.02 us (1%)
  between operations  0.9 us (1%)
    all_to_all x1, blocking collectives, on_device(): lax.all_to_all(columns, ('gx', 'gy'), split_axis=0, concat_axis=0, tiled=...  15.3 us
    pallas_call x4, Pallas kernels, sweep(): pl.pallas_call(functools.partial(sweep_kernel, lev=lev, nx=nx, nt=nt, las...  12.9 us
    ppermute x5, starting transfers between devices, widen(): return jnp.concatenate([known, lax.ppermute(known, axis, pairs)], 0)  11.9 us
    pallas_call x1, Pallas kernels, finish(): pl.pallas_call(functools.partial(finish_kernel, lev=lev, nx=nx, nt=nt, ca...  8.62 us
    pallas_call x1, Pallas kernels, prepare(): pl.pallas_call(functools.partial(prepare_kernel, lev=lev, nx=nx, nt=nt, c...  7.53 us
    pallas_call x1, Pallas kernels, gradient(): pl.pallas_call(functools.partial(gradient_kernel, cells=cells), grid=(fir...  6.44 us
    ppermute x1, starting transfers between devices, on_device(): got_l = lax.ppermute(send_r, 'gy', fwd)  3.4 us
    pallas_call x1, Pallas kernels, strips(): pl.pallas_call(functools.partial(strips_kernel, lev=lev, nx=nx), out_shap...  2.43 us
  transfers between devices with their start and end apart: 9, of which 0 were waited for; matrix products, arithmetic and copies ran while one was open for 0% of the time, Pallas kernels for 29%

profile of v1, /device:TPU:0, one launch (start us, length us, event | category | flops | bytes accessed | tf_op | source)
XLA Modules:
  0.0 78.0 jit_solution(14422064265824434587)
XLA Ops:
  0.6 0.0 copy-start.1
  0.6 0.7 copy-done.1
  1.4 0.4 tile_indices.1
  1.8 1.6 %pack_x.1 = (f32[2,16,8,384]{3,2,1,0:T(8,128)S(1)}, f32[2,16,8,384]{3,2,1,0:T(8,128)S(1)}) custom-call(f32[16,192,384]{2,1,0:T(8,128)} %v_hbm.1, f32[16,192,384]{2,1,0:T(8,128)} %v_hbm.1, bf16[16,192,384]{2,1,0:T(8,128)(2,1)} %cu_hbm.1, bf16[16,192,384]{2,1,0:T(8,128)(2,1)} %cu_hbm.1, bf16[16,192,384]{2,1,0:T(8,128)(2,1)} %cv_hbm.1, ...), custom_call_target="tpu_custom_call" | custom-call | bytes 3145728 | tf_op jit(solution)/shard_map/pack_x/pallas_call | solution.py:68
  3.5 2.4 %collective-permute-start = (f32[2,16,8,384]{3,2,1,0:T(8,128)S(1)}, f32[2,16,8,384]{3,2,1,0:T(8,128)S(1)}, u32[]{:S(2)}, u32[]{:S(2)}) collective-permute-start(f32[2,16,8,384]{3,2,1,0:T(8,128)S(1)} %get-tuple-element.58), channel_id=1, source_target_pairs={{0,4},{4,8},{8,12},{12,16},{16,20},{20,24},{24,28},{1,5},{5,9},{9,... | collective-permute-start | bytes 1179656 | tf_op jit(solution)/shard_map/ppermute | solution.py:705
  5.9 1.3 %collective-permute-start.1 = (f32[2,16,8,384]{3,2,1,0:T(8,128)S(1)}, f32[2,16,8,384]{3,2,1,0:T(8,128)S(1)}, u32[]{:S(2)}, u32[]{:S(2)}) collective-permute-start(f32[2,16,8,384]{3,2,1,0:T(8,128)S(1)} %get-tuple-element.59), channel_id=1, source_target_pairs={{4,0},{8,4},{12,8},{16,12},{20,16},{24,20},{28,24},{5,1},{9,5},{13... | collective-permute-start | bytes 1179656 | tf_op jit(solution)/shard_map/ppermute | solution.py:706
  7.2 7.5 %prepare.1 = (f32[16,3,224,128]{3,2,1,0:T(8,128)S(1)}, f32[16,3,208,128]{3,2,1,0:T(8,128)S(1)}, f32[16,3,208,128]{3,2,1,0:T(8,128)S(1)}, f32[16,3,208,128]{3,2,1...) custom-call(f32[16,192,384]{2,1,0:T(8,128)} %v_hbm.1, ...), custom_call_target="tpu_custom_call" | custom-call | flops 23592960 | bytes 35651584 | tf_op jit(solution)/shard_map/prepare/pallas_call | solution.py:197
  14.8 0.0 collective-permute-done.above
  14.8 0.0 collective-permute-done.1.below
  14.8 0.0 copy-start.3
  14.8 0.4 fill.1
  15.2 0.3 copy-done.3
  15.5 5.9 %collective-permute-start.2 = (s32[1,256]{1,0:T(1,128)S(1)}, s32[1,256]{1,0:T(1,128)S(1)}, u32[]{:S(2)}, u32[]{:S(2)}) collective-permute-start(s32[1,256]{1,0:T(1,128)S(1)} %bitcast.6), channel_id=1, source_target_pairs={{0,16},{4,20},{8,24},{12,28},{16,0},{20,4},{24,8},{28,12},{1,17},{... | collective-permute-start | bytes 3080 | tf_op jit(solution)/shard_map/ppermute | solution.py:698
  21.4 3.1 %sweep.3.src = f32[16,3,224,128]{3,2,1,0:T(8,128)S(1)} custom-call(f32[16,3,224,128]{3,2,1,0:T(8,128)S(1)} %get-tuple-element.70.src, f32[16,3,208,128]{3,2,1,0:T(8,128)S(1)} %get-tuple-element.71.cuf, f32[16,3,208,128]{3,2,1,0:T(8,128)S(1)} %get-tuple-element.72.cvf, f32[16,3,208,128]{3,2,1,0:T(8,128)S(1)} %get-tuple-element.73.refs_0_), custom_call_target="tpu_custom_call" | custom-call | flops 21233664 | bytes 16777216 | tf_op jit(solution)/shard_map/sweep/pallas_call | solution.py:321
  24.5 0.0 collective-permute-done.2
  24.5 1.6 %collective-permute-start.3 = (s32[2,256]{1,0:T(2,128)S(1)}, s32[2,256]{1,0:T(2,128)S(1)}, u32[]{:S(2)}, u32[]{:S(2)}) collective-permute-start(s32[2,256]{1,0:T(2,128)S(1)} %pad_add_fusion.4), channel_id=1, source_target_pairs={{0,8},{4,12},{8,0},{12,4},{16,24},{20,28},{24,16},{28,20},{1,9},{5... | collective-permute-start | bytes 6152 | tf_op jit(solution)/shard_map/ppermute | solution.py:698
  26.2 3.1 %sweep.4.src = f32[16,3,224,128]{3,2,1,0:T(8,128)S(1)} custom-call(f32[16,3,224,128]{3,2,1,0:T(8,128)S(1)} %sweep.3.src, f32[16,3,208,128]{3,2,1,0:T(8,128)S(1)} %get-tuple-element.71.cuf, f32[16,3,208,128]{3,2,1,0:T(8,128)S(1)} %get-tuple-element.72.cvf, f32[16,3,208,128]{3,2,1,0:T(8,128)S(1)} %get-tuple-element.73.refs_0_), custom_call_target="tpu_custom_call" | custom-call | flops 21233664 | bytes 16777216 | tf_op jit(solution)/shard_map/sweep/pallas_call | solution.py:321
  29.3 0.0 collective-permute-done.3
  29.4 1.6 %collective-permute-start.4 = (s32[4,256]{1,0:T(4,128)S(1)}, s32[4,256]{1,0:T(4,128)S(1)}, u32[]{:S(2)}, u32[]{:S(2)}) collective-permute-start(s32[4,256]{1,0:T(4,128)S(1)} %pad_add_fusion.3), channel_id=1, source_target_pairs={{0,2},{1,3},{2,0},{3,1},{4,6},{5,7},{6,4},{7,5},{8,10},{9,11},{10,... | collective-permute-start | bytes 12296 | tf_op jit(solution)/shard_map/ppermute | solution.py:698
  30.9 3.4 %collective-permute-start.6 = (f32[2,200,128]{2,1,0:T(8,128)S(1)}, f32[2,200,128]{2,1,0:T(8,128)S(1)}, u32[]{:S(2)}, u32[]{:S(2)}) collective-permute-start(f32[2,200,128]{2,1,0:T(8,128)S(1)} %get-tuple-element.80), channel_id=1, source_target_pairs={{0,1},{1,2},{2,3},{4,5},{5,6},{6,7},{8,9},{9,10},{10,11},{12,13},{... | collective-permute-start | bytes 614408 | tf_op jit(solution)/shard_map/ppermute | solution.py:710
  34.4 1.3 %collective-permute-start.7 = (f32[2,200,128]{2,1,0:T(8,128)S(1)}, f32[2,200,128]{2,1,0:T(8,128)S(1)}, u32[]{:S(2)}, u32[]{:S(2)}) collective-permute-start(f32[2,200,128]{2,1,0:T(8,128)S(1)} %get-tuple-element.81), channel_id=1, source_target_pairs={{1,0},{2,1},{3,2},{5,4},{6,5},{7,6},{9,8},{10,9},{11,10},{13,12},{... | collective-permute-start | bytes 614408 | tf_op jit(solution)/shard_map/ppermute | solution.py:711
  35.7 3.9 %sweep.5.src = f32[16,3,224,128]{3,2,1,0:T(8,128)S(1)} custom-call(f32[16,3,224,128]{3,2,1,0:T(8,128)S(1)} %sweep.4.src, f32[16,3,208,128]{3,2,1,0:T(8,128)S(1)} %get-tuple-element.71.cuf, f32[16,3,208,128]{3,2,1,0:T(8,128)S(1)} %get-tuple-element.72.cvf, f32[16,3,208,128]{3,2,1,0:T(8,128)S(1)} %get-tuple-element.73.refs_0_), custom_call_target="tpu_custom_call" | custom-call | flops 21233664 | bytes 16777216 | tf_op jit(solution)/shard_map/sweep/pallas_call | solution.py:321
  39.6 0.0 collective-permute-done.4
  39.6 0.0 copy-start.2
  39.6 2.7 %collective-permute-start.5 = (s32[8,256]{1,0:T(8,128)S(1)}, s32[8,256]{1,0:T(8,128)S(1)}, u32[]{:S(2)}, u32[]{:S(2)}) collective-permute-start(s32[8,256]{1,0:T(8,128)S(1)} %pad_add_fusion.2), channel_id=1, source_target_pairs={{0,1},{1,0},{2,3},{3,2},{4,5},{5,4},{6,7},{7,6},{8,9},{9,8},{10,11... | collective-permute-start | bytes 24584 | tf_op jit(solution)/shard_map/ppermute | solution.py:698
  42.3 2.6 %sweep_last.1 = f32[16,3,192,128]{3,2,1,0:T(8,128)S(1)} custom-call(f32[16,3,224,128]{3,2,1,0:T(8,128)S(1)} %sweep.5.src, f32[16,3,208,128]{3,2,1,0:T(8,128)S(1)} %get-tuple-element.71.cuf, f32[16,3,208,128]{3,2,1,0:T(8,128)S(1)} %get-tuple-element.72.cvf), custom_call_target="tpu_custom_call" | custom-call | flops 21233664 | bytes 16777216 | tf_op jit(solution)/shard_map/sweep_last/pallas_call | solution.py:321
  45.0 0.0 copy-start
  45.0 0.0 collective-permute-done.5
  45.0 0.0 collective-permute-done.6.got_l
  45.0 0.0 collective-permute-done.7.got_r
  45.0 0.1 collective-permute-start.8
  45.1 2.4 %strips.1 = (f32[192,128]{1,0:T(8,128)S(1)}, f32[192,128]{1,0:T(8,128)S(1)}) custom-call(f32[4,200,128]{2,1,0:T(8,128)S(1)} %get-tuple-element.83.own_l, f32[4,200,128]{2,1,0:T(8,128)S(1)} %get-tuple-element.84.own_r, f32[2,200,128]{2,1,0:T(8,128)S(1)} %collective-permute-done.6.got_l, f32[2,200,128]{2,1,0:T(8,128)S(1)} %collective-permute-done.7.got_r), custom_call_target="tpu_custom_call" | custom-call | flops 10485760 | bytes 3145728 | tf_op jit(solution)/shard_map/strips/pallas_call | solution.py:472
  47.6 0.0 collective-permute-done.8
  47.6 0.0 copy-done.2
  47.6 8.6 %finish.1 = (f32[16,192,384]{2,1,0:T(8,128)}, f32[32,8,128]{2,1,0:T(8,128)S(1)}, f32[16,576,128]{2,1,0:T(8,128)S(1)}) custom-call(s32[1]{0:T(128)} %bitcast.me_ref, s32[32,128]{1,0:T(8,128)S(1)} %get-tuple-element.55.row, s32[32,128]{1,0:T(8,128)S(1)} %get-tuple-element.56.shift, ...), custom_call_target="tpu_custom_call", output_to_operand_aliasing={{2}: (8, {})} | custom-call | flops 31457280 | bytes 20971520 | tf_op jit(solution)/shard_map/finish/pallas_call | solution.py:559
  56.2 15.3 %all_to_all.5.got = f32[32,8,128]{2,1,0:T(8,128)S(1)} all-to-all(f32[32,8,128]{2,1,0:T(8,128)S(1)} %get-tuple-element.93), channel_id=1, replica_groups=mesh['gx'=8,'gy'=4] {'gx','gy'}, dimensions={0} | all-to-all | bytes 262144 | tf_op jit(solution)/shard_map/all_to_all | solution.py:727
  71.5 0.0 copy-done
  71.5 6.4 %gradient.1 = bf16[256,6400]{1,0:T(8,128)(2,1)} custom-call(s32[256,1]{1,0:T(8,128)S(1)} %get-tuple-element.91.src, s32[256,1]{1,0:T(8,128)S(1)} %get-tuple-element.92.slot, f32[32,8,128]{2,1,0:T(8,128)S(1)} %all_to_all.5.got, bf16[256,6400]{1,0:T(8,128)(2,1)S(1)} %copy-done), custom_call_target="tpu_custom_call" | custom-call | flops 838860800 | bytes 7340032 | tf_op jit(solution)/shard_map/gradient/pallas_call | solution.py:640
  (5 shorter events, 0.0 us)
Async XLA Ops:
  0.6 0.8 copy-start.1
  3.5 11.3 %collective-permute-start = (f32[2,16,8,384]{3,2,1,0:T(8,128)S(1)}, f32[2,16,8,384]{3,2,1,0:T(8,128)S(1)}, u32[]{:S(2)}, u32[]{:S(2)}) collective-permute-start(f32[2,16,8,384]{3,2,1,0:T(8,128)S(1)} %get-tuple-element.58), channel_id=1, source_target_pairs={{0,4},{4,8},{8,12},{12,16},{16,20},{20,24},{24,28},{1,5},{5,9},{9,... | collective-permute-start | bytes 1179656 | tf_op jit(solution)/shard_map/ppermute | solution.py:705
  5.9 8.9 %collective-permute-start.1 = (f32[2,16,8,384]{3,2,1,0:T(8,128)S(1)}, f32[2,16,8,384]{3,2,1,0:T(8,128)S(1)}, u32[]{:S(2)}, u32[]{:S(2)}) collective-permute-start(f32[2,16,8,384]{3,2,1,0:T(8,128)S(1)} %get-tuple-element.59), channel_id=1, source_target_pairs={{4,0},{8,4},{12,8},{16,12},{20,16},{24,20},{28,24},{5,1},{9,5},{13... | collective-permute-start | bytes 1179656 | tf_op jit(solution)/shard_map/ppermute | solution.py:706
  14.8 0.7 copy-start.3
  15.5 9.1 %collective-permute-start.2 = (s32[1,256]{1,0:T(1,128)S(1)}, s32[1,256]{1,0:T(1,128)S(1)}, u32[]{:S(2)}, u32[]{:S(2)}) collective-permute-start(s32[1,256]{1,0:T(1,128)S(1)} %bitcast.6), channel_id=1, source_target_pairs={{0,16},{4,20},{8,24},{12,28},{16,0},{20,4},{24,8},{28,12},{1,17},{... | collective-permute-start | bytes 3080 | tf_op jit(solution)/shard_map/ppermute | solution.py:698
  24.5 4.8 %collective-permute-start.3 = (s32[2,256]{1,0:T(2,128)S(1)}, s32[2,256]{1,0:T(2,128)S(1)}, u32[]{:S(2)}, u32[]{:S(2)}) collective-permute-start(s32[2,256]{1,0:T(2,128)S(1)} %pad_add_fusion.4), channel_id=1, source_target_pairs={{0,8},{4,12},{8,0},{12,4},{16,24},{20,28},{24,16},{28,20},{1,9},{5... | collective-permute-start | bytes 6152 | tf_op jit(solution)/shard_map/ppermute | solution.py:698
  29.4 10.2 %collective-permute-start.4 = (s32[4,256]{1,0:T(4,128)S(1)}, s32[4,256]{1,0:T(4,128)S(1)}, u32[]{:S(2)}, u32[]{:S(2)}) collective-permute-start(s32[4,256]{1,0:T(4,128)S(1)} %pad_add_fusion.3), channel_id=1, source_target_pairs={{0,2},{1,3},{2,0},{3,1},{4,6},{5,7},{6,4},{7,5},{8,10},{9,11},{10,... | collective-permute-start | bytes 12296 | tf_op jit(solution)/shard_map/ppermute | solution.py:698
  30.9 14.1 %collective-permute-start.6 = (f32[2,200,128]{2,1,0:T(8,128)S(1)}, f32[2,200,128]{2,1,0:T(8,128)S(1)}, u32[]{:S(2)}, u32[]{:S(2)}) collective-permute-start(f32[2,200,128]{2,1,0:T(8,128)S(1)} %get-tuple-element.80), channel_id=1, source_target_pairs={{0,1},{1,2},{2,3},{4,5},{5,6},{6,7},{8,9},{9,10},{10,11},{12,13},{... | collective-permute-start | bytes 614408 | tf_op jit(solution)/shard_map/ppermute | solution.py:710
  34.4 10.7 %collective-permute-start.7 = (f32[2,200,128]{2,1,0:T(8,128)S(1)}, f32[2,200,128]{2,1,0:T(8,128)S(1)}, u32[]{:S(2)}, u32[]{:S(2)}) collective-permute-start(f32[2,200,128]{2,1,0:T(8,128)S(1)} %get-tuple-element.81), channel_id=1, source_target_pairs={{1,0},{2,1},{3,2},{5,4},{6,5},{7,6},{9,8},{10,9},{11,10},{13,12},{... | collective-permute-start | bytes 614408 | tf_op jit(solution)/shard_map/ppermute | solution.py:711
  39.6 8.0 %copy-start.2 = (f32[16,16]{1,0:T(8,128)S(1)}, f32[16,16]{1,0:T(8,128)}, u32[]{:S(2)}) copy-start(f32[16,16]{1,0:T(8,128)} %prof.1) | copy-start | bytes 3076
  39.6 5.4 %collective-permute-start.5 = (s32[8,256]{1,0:T(8,128)S(1)}, s32[8,256]{1,0:T(8,128)S(1)}, u32[]{:S(2)}, u32[]{:S(2)}) collective-permute-start(s32[8,256]{1,0:T(8,128)S(1)} %pad_add_fusion.2), channel_id=1, source_target_pairs={{0,1},{1,0},{2,3},{3,2},{4,5},{5,4},{6,7},{7,6},{8,9},{9,8},{10,11... | collective-permute-start | bytes 24584 | tf_op jit(solution)/shard_map/ppermute | solution.py:698
  45.0 26.5 %copy-start = (bf16[256,6400]{1,0:T(8,128)(2,1)S(1)}, bf16[256,6400]{1,0:T(8,128)(2,1)}, u32[]{:S(2)}) copy-start(bf16[256,6400]{1,0:T(8,128)(2,1)} %burn.1) | copy-start | bytes 9830404
  45.0 2.5 %collective-permute-start.8 = (s32[16,256]{1,0:T(8,128)S(1)}, s32[16,256]{1,0:T(8,128)S(1)}, u32[]{:S(2)}, u32[]{:S(2)}) collective-permute-start(s32[16,256]{1,0:T(8,128)S(1)} %pad_add_fusion.1), channel_id=1, source_target_pairs={{0,4},{4,0},{8,12},{12,8},{16,20},{20,16},{24,28},{28,24},{1,5},{5... | collective-permute-start | bytes 49160 | tf_op jit(solution)/shard_map/ppermute | solution.py:698

commit v2 on v1

--- a/solution.py
+++ b/solution.py
@@ -39,20 +39,33 @@
     return lax.broadcasted_iota(I32, shape, 1)
 
 
-def pack_x_kernel(vt, vb, cut, cub, cvt, cvb, kt, kb, up, dn):
+def pack_x_kernel(odd, vt, vb, cut, cub, cvt, cvb, kt, kb, inj, near, far):
     h, b = (HALO, ROWS)
-
-    def level(l, _):
-        up[0, l] = jnp.concatenate([vt[l, :h], cut[l].astype(F32)[:h]], 0)
-        up[1, l] = jnp.concatenate([cvt[l].astype(F32)[:h], kt[l].astype(F32)[:h]], 0)
-        dn[0, l] = jnp.concatenate([vb[l, SUBL - h :], cub[l].astype(F32)[b - h :]], 0)
-        dn[1, l] = jnp.concatenate([cvb[l].astype(F32)[b - h :], kb[l].astype(F32)[b - h :]], 0)
-        return 0
-
-    lax.fori_loop(0, vt.shape[0], level, 0)
-
-
-def pack_x(v, cu, cv, k):
+    lev = vt.shape[0]
+
+    def pack(up, dn):
+        def level(l, _):
+            up[l] = jnp.concatenate([vt[l, :h], cut[l].astype(F32)[:h]], 0)
+            up[lev + l] = jnp.concatenate([cvt[l].astype(F32)[:h], kt[l].astype(F32)[:h]], 0)
+            dn[l] = jnp.concatenate([vb[l, SUBL - h :], cub[l].astype(F32)[b - h :]], 0)
+            dn[lev + l] = jnp.concatenate([cvb[l].astype(F32)[b - h :], kb[l].astype(F32)[b - h :]], 0)
+            return 0
+
+        lax.fori_loop(0, lev, level, 0)
+
+    @pl.when(odd[0] == 0)
+    def _():
+        pack(far, near)
+
+    @pl.when(odd[0] != 0)
+    def _():
+        pack(near, far)
+
+    near[2 * lev] = jnp.zeros(near.shape[1:], F32)
+    near[2 * lev, : inj.shape[0], :LANES] = inj[...].astype(F32)
+
+
+def pack_x(odd, v, cu, cv, k, inj):
     lev, nx, ny = v.shape
 
     def ends(x, rows):
@@ -63,18 +76,18 @@
         )
 
     specs = [s for x, r in ((v, SUBL), (cu, ROWS), (cv, ROWS), (k, ROWS)) for s in ends(x, r)]
-    out = jax.ShapeDtypeStruct((2, lev, 2 * HALO, ny), F32)
-    whole = pl.BlockSpec((2, lev, 2 * HALO, ny), lambda i: (0, 0, 0, 0))
+    near = (2 * lev + 1, 2 * HALO, ny)
+    far = (2 * lev, 2 * HALO, ny)
     return pl.pallas_call(
         pack_x_kernel,
         grid=(1,),
-        out_shape=(out, out),
-        in_specs=specs,
-        out_specs=(whole, whole),
+        out_shape=(jax.ShapeDtypeStruct(near, F32), jax.ShapeDtypeStruct(far, F32)),
+        in_specs=[SMEM] + specs + [pl.BlockSpec(inj.shape, lambda i: (0, 0))],
+        out_specs=(pl.BlockSpec(near, lambda i: (0, 0, 0)), pl.BlockSpec(far, lambda i: (0, 0, 0))),
         compiler_params=params(12),
         cost_estimate=cost(0, 3 << 20),
         name="pack_x",
-    )(v, v, cu, cu, cv, cv, k, k)
+    )(odd, v, v, cu, cu, cv, cv, k, k, inj)
 
 
 def edge_lanes(rows, lev, right):
@@ -92,17 +105,20 @@
     return acc
 
 
-def store_edges(packed, own, send, at, right):
-    v, cu, cv, k = packed
-    for i, x in enumerate(packed):
-        own[i, at, :] = x
-    low = lane_id(v.shape) < LANES // 2
+def store_edges(packed, owns, near, far, at, odd):
     half = LANES // 2
-    for i, (a, b) in enumerate(((v, cu), (cv, k))):
-        if right:
-            send[i, at, :] = jnp.where(low, pltpu.roll(a, half, 1), b)
-        else:
-            send[i, at, :] = jnp.where(low, a, pltpu.roll(b, half, 1))
+    low = lane_id(packed[0][0].shape) < half
+    rows = owns[0].shape[1]
+    for own, arrays in zip(owns, packed):
+        for i, x in enumerate(arrays):
+            own[i, at, :] = x
+    for i in range(2):
+        a, b = packed[0][2 * i : 2 * i + 2]
+        left = jnp.where(low, a, pltpu.roll(b, half, 1))
+        a, b = packed[1][2 * i : 2 * i + 2]
+        right = jnp.where(low, pltpu.roll(a, half, 1), b)
+        near[i, at, :] = jnp.where(odd, left, right)
+        far[i, at, :] = jnp.where(odd, right, left)
 
 
 def load_group(ref, l, j, g, off=0):
@@ -133,7 +149,7 @@
 
 
 def prepare_kernel(
-    v_hbm, cu_hbm, cv_hbm, k_hbm, w, cuf, cvf, kf, own_l, send_l, own_r, send_r, vs, cus, cvs, ks, sem,
+    odd_ref, v_hbm, cu_hbm, cv_hbm, k_hbm, w, cuf, cvf, kf, own_l, own_r, near, far, vs, cus, cvs, ks, sem,
     *, lev, nx, nt, chunks,
 ):
     part = nx // chunks
@@ -157,13 +173,22 @@
         put = pl.ds(pl.multiple_of(r * ROWS + EDGE, SUBL), ROWS)
         here = pl.ds(pl.multiple_of(r * ROWS + FRONT, SUBL), ROWS)
         lanes = [slice(LANES * j, LANES * (j + 1)) for j in range(nt)]
-        for l in range(lev):
-            for j in range(nt):
-                for buf, raw in ((cuf, cus), (cvf, cvs), (kf, ks)):
-                    buf[l, j, put, :] = raw[l, at, lanes[j]].astype(F32)
+        raws = (vs, cus, cvs, ks)
+        bufs = (None, cuf, cvf, kf)
+        packed = [[None] * 4, [None] * 4]
 
         def store(l, j, x):
             w[l, j, here, :] = x
+            for i in range(4):
+                wide = raws[i][l, at, lanes[j]].astype(F32)
+                if i:
+                    bufs[i][l, j, put, :] = wide
+                for side in range(2):
+                    if j == (nt - 1) * side:
+                        take, level = takes[side]
+                        got = jnp.take_along_axis(wide, take, axis=1)
+                        old = packed[side][i]
+                        packed[side][i] = got if old is None else jnp.where(level == l, got, old)
 
         diffuse(
             lambda l: [vs[l, at, lanes[j]] for j in range(nt)],
@@ -172,13 +197,7 @@
             lev,
             nt,
         )
-        for side, (own, send) in enumerate(((own_l, send_l), (own_r, send_r))):
-            edge = lanes[-1] if side else lanes[0]
-            packed = [
-                pack_edge([x[l, at, edge].astype(F32) for l in range(lev)], *takes[side])
-                for x in (vs, cus, cvs, ks)
-            ]
-            store_edges(packed, own, send, at, side == 1)
+        store_edges(packed, (own_l, own_r), near, far, at, odd_ref[0] != 0)
         return 0
 
     for c in range(chunks):
@@ -187,17 +206,18 @@
         lax.fori_loop(c * part // ROWS, (c + 1) * part // ROWS, rows, 0)
 
 
-def prepare(v, cu, cv, k):
+def prepare(odd, v, cu, cv, k):
     lev, nx, ny = v.shape
     nt = ny // LANES
     chunks = max(c for c in (1, 2, 3, 4) if nx % (c * ROWS) == 0)
     wide = jax.ShapeDtypeStruct((lev, nt, nx + 2 * EDGE, LANES), F32)
     own = jax.ShapeDtypeStruct((4, nx + SUBL, LANES), F32)
-    send = jax.ShapeDtypeStruct((2, nx + SUBL, LANES), F32)
+    near = jax.ShapeDtypeStruct((2, nx + 2 * SUBL, LANES), F32)
+    far = jax.ShapeDtypeStruct((2, nx + SUBL, LANES), F32)
     return pl.pallas_call(
         functools.partial(prepare_kernel, lev=lev, nx=nx, nt=nt, chunks=chunks),
-        out_shape=(jax.ShapeDtypeStruct((lev, nt, nx + 2 * FRONT, LANES), F32), wide, wide, wide, own, send, own, send),
-        in_specs=[HBM] * 4,
+        out_shape=(jax.ShapeDtypeStruct((lev, nt, nx + 2 * FRONT, LANES), F32), wide, wide, wide, own, own, near, far),
+        in_specs=[SMEM] + [HBM] * 4,
         out_specs=(VMEM,) * 8,
         scratch_shapes=[pltpu.VMEM((lev, nx, ny), F32)]
         + [pltpu.VMEM((lev, nx, ny), BF16)] * 3
@@ -205,18 +225,22 @@
         compiler_params=params(14),
         cost_estimate=cost(20 * lev * nx * ny, 34 << 20),
         name="prepare",
-    )(v, cu, cv, k)
-
-
-def fill_kernel(above, below, *refs, lev, nx, nt):
-    w, cuf, cvf, kf = refs[8:12]
-    outs = refs[12:]
+    )(odd, v, cu, cv, k)
+
+
+def fill_kernel(odd_x, odd_y, inj, got_near, got_far, *refs, lev, nx, nt):
+    w, cuf, cvf, kf, own_l, own_r, near, far, known = refs[8:]
     rest = jnp.zeros((SUBL - HALO, LANES), F32)
+    flip = odd_x[0] != 0
+
+    def ends(l, j, q, o):
+        at = (q * lev + l, slice(o, o + HALO), slice(LANES * j, LANES * (j + 1)))
+        x, y = (got_near[at], got_far[at])
+        return jnp.where(flip, x, y), jnp.where(flip, y, x)
 
     def pair(l, j, q, o):
-        lanes = slice(LANES * j, LANES * (j + 1))
-        top = jnp.concatenate([rest, above[q, l, o : o + HALO, lanes]], 0)
-        return top, jnp.concatenate([below[q, l, o : o + HALO, lanes], rest], 0)
+        top, low = ends(l, j, q, o)
+        return jnp.concatenate([rest, top], 0), jnp.concatenate([low, rest], 0)
 
     for end in range(2):
         to = (FRONT + nx) if end else (FRONT - SUBL)
@@ -236,33 +260,38 @@
             for j in range(nt):
                 for buf, q, o in ((cuf, 0, HALO), (cvf, 1, 0), (kf, 1, HALO)):
                     buf[l, j, at : at + SUBL, :] = pair(l, j, q, o)[end]
+    packed = []
     for side in range(2):
         take, level = edge_lanes(SUBL, lev, side == 1)
-        lanes = slice(LANES * (nt - 1), LANES * nt) if side else slice(0, LANES)
-        packed = []
+        packed.append([])
         for q, o in ((0, 0), (0, HALO), (1, 0), (1, HALO)):
-            slabs = [
-                jnp.concatenate([below[q, l, o : o + HALO, lanes], above[q, l, o : o + HALO, lanes]], 0)
-                for l in range(lev)
-            ]
-            packed.append(pack_edge(slabs, take, level))
-        store_edges(packed, outs[2 * side], outs[2 * side + 1], slice(nx, nx + SUBL), side == 1)
-
-
-def fill(above, below, arrays):
-    lev, _, _, ny = above.shape
-    nt = ny // LANES
+            slabs = [jnp.concatenate(ends(l, (nt - 1) * side, q, o)[::-1], 0) for l in range(lev)]
+            packed[-1].append(pack_edge(slabs, take, level))
+    store_edges(packed, (own_l, own_r), near, far, slice(nx, nx + SUBL), odd_y[0] != 0)
+    lines = inj.shape[0]
+    tail = nx + SUBL
+    known[:lines, :] = inj[...].astype(F32)
+    known[lines:, :] = got_near[2 * lev, :lines, :LANES]
+    for i in range(2):
+        near[i, tail:, :] = jnp.zeros((SUBL, LANES), F32)
+    near[0, tail : tail + 2 * lines, :] = known[...]
+
+
+def fill(odd_x, odd_y, inj, got_near, got_far, arrays):
+    lev = got_far.shape[0] // 2
+    nt = got_far.shape[2] // LANES
     nx = arrays[4].shape[1] - SUBL
+    known = jax.ShapeDtypeStruct((2 * inj.shape[0], LANES), F32)
     return pl.pallas_call(
-        functools.partial(fill_kernel, lev=above.shape[1], nx=nx, nt=nt),
-        out_shape=tuple(jax.ShapeDtypeStruct(x.shape, x.dtype) for x in arrays),
-        in_specs=[VMEM] * 10,
-        out_specs=(VMEM,) * 8,
-        input_output_aliases={2 + i: i for i in range(8)},
+        functools.partial(fill_kernel, lev=lev, nx=nx, nt=nt),
+        out_shape=tuple(jax.ShapeDtypeStruct(x.shape, x.dtype) for x in arrays) + (known,),
+        in_specs=[SMEM] * 2 + [VMEM] * 11,
+        out_specs=(VMEM,) * 9,
+        input_output_aliases={5 + i: i for i in range(8)},
         compiler_params=params(3),
         cost_estimate=cost(0, 4 << 20),
         name="fill",
-    )(above, below, *arrays)
+    )(odd_x, odd_y, inj, got_near, got_far, *arrays)
 
 
 def sweep_kernel(src, cuf, cvf, *refs, lev, nx, nt, last_step):
@@ -358,9 +387,9 @@
         found = jnp.where(lane == s, one, found)
     value = found - 1
     spot = value // tiles
-    row[...] = jnp.where(found > 0, spot // per_tile, -1)
+    row[...] = jnp.where(found > 0, spot // per_tile, 0)
     shift[...] = (lane * TB - spot % per_tile * TB) & (LANES - 1)
-    pos[...] = value % tiles
+    pos[...] = jnp.where(found > 0, value % tiles, 0)
     own = owner(lines(me * per, 1, 1))[0]
     i = lax.broadcasted_iota(I32, (tiles, tiles), 0)
     j = lane_id((tiles, tiles))
@@ -387,7 +416,7 @@
     )(me, blocks)
 
 
-def strips_kernel(own_l, own_r, got_l, got_r, out_l, out_r, strip, other, coef, *, lev, nx):
+def strips_kernel(odd, own_l, own_r, got_near, got_far, out_l, out_r, strip, other, coef, *, lev, nx):
     rows = nx + 2 * HALO
     step = rows
     half = LANES // 2
@@ -405,7 +434,8 @@
         for a in range(4):
             q = a // 2
             ol, orr = (own_l[a, at, :], own_r[a, at, :])
-            gl, gr = (got_l[q, at, :], got_r[q, at, :])
+            x, y = (got_near[q, at, :], got_far[q, at, :])
+            gl, gr = (jnp.where(odd[0] != 0, x, y), jnp.where(odd[0] != 0, y, x))
             if a % 2:
                 gl = turn(gl)
             else:
@@ -465,14 +495,14 @@
     out_r[...] = strip[2, SUBL : SUBL + nx, :]
 
 
-def strips(own_l, own_r, got_l, got_r, lev):
+def strips(odd, own_l, own_r, got_near, got_far, lev):
     rows = own_l.shape[1]
     nx = rows - 2 * HALO
     out = jax.ShapeDtypeStruct((nx, LANES), F32)
     return pl.pallas_call(
         functools.partial(strips_kernel, lev=lev, nx=nx),
         out_shape=(out, out),
-        in_specs=[VMEM] * 4,
+        in_specs=[SMEM] + [VMEM] * 4,
         out_specs=(VMEM, VMEM),
         scratch_shapes=[
             pltpu.VMEM((3, rows + 2 * SUBL, LANES), F32),
@@ -482,7 +512,7 @@
         compiler_params=params(8),
         cost_estimate=cost(10 << 20, 3 << 20),
         name="strips",
-    )(own_l, own_r, got_l, got_r)
+    )(odd, own_l, own_r, got_near, got_far)
 
 
 def finish_kernel(
@@ -495,23 +525,26 @@
         return 0
 
     lax.fori_loop(0, lev, spread, 0)
-    lane16 = lane_id((ROWS, LANES))
+    lane8 = lane_id((SUBL, LANES))
     width = HALO
+    outer, inner = (lane8 < width, lane8 >= LANES - width)
+    base = (nt - 1) * nx
 
     def patch(n, _):
-        a = pl.ds(pl.multiple_of(n * ROWS, ROWS), ROWS)
-        left, right = (edge_l[a, :], edge_r[a, :])
-        for l in range(lev):
-            take_l = (lane16 * lev + (LANES // 2 + l)) & (LANES - 1)
-            take_r = ((lane16 - (LANES - width)) * lev + l) & (LANES - 1)
-            b = pl.ds(pl.multiple_of((nt - 1) * nx + n * ROWS, ROWS), ROWS)
-            field[l, a, :] = jnp.where(lane16 < width, jnp.take_along_axis(left, take_l, axis=1), field[l, a, :])
-            field[l, b, :] = jnp.where(
-                lane16 >= LANES - width, jnp.take_along_axis(right, take_r, axis=1), field[l, b, :]
-            )
-        return 0
-
-    lax.fori_loop(0, nx // ROWS, patch, 0)
+        for m in range(2):
+            l = 2 * n + m
+            take_l = (lane8 * lev + (LANES // 2 + l)) & (LANES - 1)
+            take_r = ((lane8 - (LANES - width)) * lev + l) & (LANES - 1)
+            for g in range(0, nx, SUBL):
+                x, y = (edge_l[g : g + SUBL, :], edge_r[g : g + SUBL, :])
+                x = jnp.take_along_axis(x, take_l, axis=1)
+                field[l, g : g + SUBL, :] = jnp.where(outer, x, field[l, g : g + SUBL, :])
+                y = jnp.take_along_axis(y, take_r, axis=1)
+                g = base + g
+                field[l, g : g + SUBL, :] = jnp.where(inner, y, field[l, g : g + SUBL, :])
+        return 0
+
+    lax.fori_loop(0, lev // 2, patch, 0)
     puts = [
         pltpu.make_async_copy(
             field.at[:, pl.ds(j * nx, nx), :], state.at[:, :, pl.ds(j * LANES, LANES)], osem.at[j]
@@ -521,33 +554,31 @@
     for c in puts:
         c.start()
     me = me_ref[0]
-    slot_of = lane_id((TB, LANES)) // TB
-
-    def handler(h, _):
-        @pl.when(row[h, 0] >= 0)
-        def _():
-            out = jnp.zeros((TB, LANES), F32)
-            apart = h ^ me
-            source = 0
-            for n, bit in enumerate(order):
-                source = source + ((apart // bit) & 1) * (1 << n)
-            for s in range(cap):
-                at = pl.ds(pl.multiple_of(row[h, s], TB), TB)
-                level = inj[source, pos[h, s]]
-                terms = [weight[level, l] * field[l, at, :] for l in range(lev)]
-                while len(terms) > 1:
-                    terms = [x + y for x, y in zip(terms[::2], terms[1::2])]
-                acc = terms[0]
-                out = jnp.where(slot_of == s, pltpu.roll(acc, shift[h, s], 1), out)
-            send[h] = out
-
-        @pl.when(row[h, 0] < 0)
-        def _():
-            send[h] = jnp.zeros((TB, LANES), F32)
-
-        return 0
-
-    lax.fori_loop(0, procs, handler, 0)
+    slot_of = lane_id((TB, LANES)) >> TB.bit_length() - 1
+
+    def handler(h):
+        out = jnp.zeros((TB, LANES), F32)
+        apart = h ^ me
+        source = 0
+        lines = inj.shape[0] // procs
+        for n, bit in enumerate(order):
+            source = source | (apart >> bit.bit_length() - 1 & 1) << n
+        for s in range(cap):
+            at = pl.ds(pl.multiple_of(row[h, s], TB), TB)
+            tile = pos[h, s]
+            level = inj[source * lines + (tile >> LANES.bit_length() - 1), tile & (LANES - 1)]
+            terms = [weight[level, l] * field[l, at, :] for l in range(lev)]
+            while len(terms) > 1:
+                terms = [x + y for x, y in zip(terms[::2], terms[1::2])]
+            out = jnp.where(slot_of == s, pltpu.roll(terms[0], shift[h, s], 1), out)
+        send[h] = out
+
+    def handlers(n, _):
+        for m in range(2):
+            handler(2 * n + m)
+        return 0
+
+    lax.fori_loop(0, procs // 2, handlers, 0)
     for c in puts:
         c.wait()
 
@@ -580,55 +611,62 @@
     return hi, mid, (rest - mid.astype(F32)).astype(BF16)
 
 
-def gradient_kernel(src, slot, got, burn, out, cols, parts, *, cells):
-    tiles, width = burn.shape
+def gradient_kernel(src, slot, got, burn, out, cols, parts, wide, sem, *, cells, width):
+    tiles, fire = burn.shape
     procs = got.shape[0]
-    step = pl.program_id(0)
     block = min(tiles, 8 * SUBL)
-
-    @pl.when(step == 0)
-    def _():
-        for a in range(TB):
-            parts[a] = jnp.concatenate(split3(got[:, a, :]), 0)
-        lane = lane_id((block, LANES))
-        low = lane < cells
-        who = lane_id((block, 3 * procs)) % procs
-
-        def rows(n, _):
-            at = pl.ds(pl.multiple_of(n * block, block), block)
-            pick = (who == src[at, :]).astype(F32).astype(BF16)
-            keep = lane // TB == slot[at, :]
+    for a in range(TB):
+        parts[a] = jnp.concatenate(split3(got[:, a, :]), 0)
+    lane = lane_id((block, LANES))
+    low = lane < cells
+    which = lane >> TB.bit_length() - 1
+    third = lane_id((block, 3 * procs))
+    who = jnp.where(third >= procs, third - procs, third)
+    who = jnp.where(who >= procs, who - procs, who)
+
+    def rows(n, _):
+        at = pl.ds(pl.multiple_of(n * block, block), block)
+        pick = jnp.where(who == src[at, :], 1.0, 0.0).astype(BF16)
+        keep = which == slot[at, :]
+        t = [
+            jnp.where(keep, jnp.dot(pick, parts[a], preferred_element_type=F32), 0.0)
+            for a in range(TB)
+        ]
+        w = TB
+        while len(t) > 1:
+            even = lane & w == 0
             t = [
-                jnp.where(keep, jnp.dot(pick, parts[a], preferred_element_type=F32), 0.0)
-                for a in range(TB)
+                jnp.where(even, x, y) + pltpu.roll(jnp.where(even, y, x), w, 1)
+                for x, y in zip(t[::2], t[1::2])
             ]
-            w = TB
-            while len(t) > 1:
-                even = lane & w == 0
-                t = [
-                    jnp.where(even, x, y) + pltpu.roll(jnp.where(even, y, x), w, 1)
-                    for x, y in zip(t[::2], t[1::2])
-                ]
-                w *= 2
-            col = t[0]
-            while w < LANES:
-                col = col + pltpu.roll(col, w, 1)
-                w *= 2
-            hi = col.astype(BF16).astype(F32)
-            mid = (col - hi).astype(BF16).astype(F32)
-            cols[at, :LANES] = jnp.where(low, hi, mid).astype(BF16)
-            cols[at, LANES:] = jnp.where(low, col - hi - mid, 0.0).astype(BF16)
-            return 0
-
-        lax.fori_loop(0, tiles // block, rows, 0)
-
-    q = step * width + lane_id((cells, width))
+            w *= 2
+        col = t[0]
+        while w < LANES:
+            col = col + pltpu.roll(col, w, 1)
+            w *= 2
+        hi = col.astype(BF16).astype(F32)
+        mid = (col - hi).astype(BF16).astype(F32)
+        cols[at, :LANES] = jnp.where(low, hi, mid).astype(BF16)
+        cols[at, LANES:] = jnp.where(low, col - hi - mid, 0.0).astype(BF16)
+        return 0
+
+    for n in range(tiles // block):
+        rows(n, 0)
     c = lax.broadcasted_iota(I32, (cells, width), 0) * SUB
-    spread = ((q >= c) & (q < c + SUB)).astype(F32).astype(BF16)
-    wide = jnp.dot(
-        cols[...], jnp.concatenate([spread] * (2 * LANES // cells), 0), preferred_element_type=F32
-    )
-    out[...] = (burn[...].astype(F32) * wide).astype(BF16)
+    lane = lane_id((cells, width)) - c
+    copies = []
+    for n in range(fire // width):
+        q = lane + n * width
+        spread = jnp.where((q >= 0) & (q < SUB), 1.0, 0.0).astype(BF16)
+        at = slice(n * width, (n + 1) * width)
+        full = jnp.dot(
+            cols[...], jnp.concatenate([spread] * (2 * LANES // cells), 0), preferred_element_type=F32
+        )
+        wide[:, at] = (burn[:, at].astype(F32) * full).astype(BF16)
+        copies.append(pltpu.make_async_copy(wide.at[:, at], out.at[:, at], sem.at[n]))
+        copies[-1].start()
+    for x in copies:
+        x.wait()
 
 
 def gradient(src, slot, got, burn):
@@ -636,29 +674,28 @@
     cells = TB * TB
     procs = got.shape[0]
     width = max(w for w in range(LANES, 11 * LANES, LANES) if fire % w == 0)
-    block = pl.BlockSpec((tiles, width), lambda i: (0, i))
     return pl.pallas_call(
-        functools.partial(gradient_kernel, cells=cells),
-        grid=(fire // width,),
+        functools.partial(gradient_kernel, cells=cells, width=width),
         out_shape=jax.ShapeDtypeStruct((tiles, fire), BF16),
-        in_specs=[
-            pl.BlockSpec((tiles, 1), lambda i: (0, 0)),
-            pl.BlockSpec((tiles, 1), lambda i: (0, 0)),
-            pl.BlockSpec(got.shape, lambda i: (0, 0, 0)),
-            block,
+        in_specs=[VMEM] * 4,
+        out_specs=HBM,
+        scratch_shapes=[
+            pltpu.VMEM((tiles, 2 * LANES), BF16),
+            pltpu.VMEM((TB, 3 * procs, LANES), BF16),
+            pltpu.VMEM((tiles, fire), BF16),
+            pltpu.SemaphoreType.DMA((fire // width,)),
         ],
-        out_specs=block,
-        scratch_shapes=[pltpu.VMEM((tiles, 2 * LANES), BF16), pltpu.VMEM((TB, 3 * procs, LANES), BF16)],
         compiler_params=params(16),
         cost_estimate=cost(2 * tiles * fire * 4 * cells, 7 << 20),
         name="gradient",
     )(src, slot, got, burn)
 
 
-def shifts(axis):
+def exchange(near, far, axis):
     count = lax.axis_size(axis)
-    up = [(i, i + 1) for i in range(count - 1)]
-    return up, [(j, i) for i, j in up]
+    first = lax.ppermute(near, axis, [(i, i ^ 1) for i in range(count)])
+    pairs = [(i, i + 1) for i in range(1, count - 1, 2)]
+    return first, lax.ppermute(far, axis, pairs + [(j, i) for i, j in pairs])
 
 
 def bits(count):
@@ -688,41 +725,43 @@
         for x in (adjoint_forcing, courant_x, courant_y, vertical_mix)
     )
 
-    steps = [("gx", b) for b in bits(gx)[::-1][:-1]] + [("gy", b) for b in bits(gy)[::-1]] + [("gx", 1)]
-    order = tuple(b * gy if axis == "gx" else b for axis, b in steps)
-    known = injection_level.reshape(1, tiles)
+    steps = [("gx", b) for b in bits(gx)[1:][::-1]] + [("gy", b) for b in bits(gy)[1:][::-1]]
+    order = (gy, 1) + tuple(b * gy if axis == "gx" else b for axis, b in steps)
+    inj = injection_level.reshape(-1, LANES)
 
     def widen(known, step):
         axis, bit = step
         pairs = [(i, i ^ bit) for i in range(lax.axis_size(axis))]
         return jnp.concatenate([known, lax.ppermute(known, axis, pairs)], 0)
 
-    up, down = pack_x(*fields)
-    row, shift, pos, src, slot, up, down = lax.optimization_barrier(
-        tuple(tile_indices(me1, tile_block, procs, cap, nx // TB, ny // TB, gy, nx)) + (up, down)
+    odd_x, odd_y = ((lax.axis_index(a).astype(I32) & 1).reshape(1) for a in ("gx", "gy"))
+    near, far = pack_x(odd_x, *fields, inj)
+    row, shift, pos, src, slot, near, far = lax.optimization_barrier(
+        tuple(tile_indices(me1, tile_block, procs, cap, nx // TB, ny // TB, gy, nx)) + (near, far)
     )
-    fwd, back = shifts("gx")
-    above = lax.ppermute(down, "gx", fwd)
-    below = lax.ppermute(up, "gx", back)
-    arrays = fill(above, below, prepare(*fields))
-    w, cu, cv, k, own_l, send_l, own_r, send_r = arrays
-    fwd, back = shifts("gy")
-    got_l = lax.ppermute(send_r, "gy", fwd)
-    got_r = lax.ppermute(send_l, "gy", back)
-    todo = list(steps)
+    got_near, got_far = exchange(near, far, "gx")
+    w, cu, cv, k, own_l, own_r, near, far, known = fill(
+        odd_x, odd_y, inj, got_near, got_far, prepare(odd_y, *fields)
+    )
+    got_near, got_far = exchange(near, far, "gy")
     for n in range(ITERS):
-        known, w = lax.optimization_barrier((known, w))
-        share = len(todo[:-1]) // (ITERS - n) if n + 1 < ITERS else len(todo[:-1])
-        for step in todo[:share]:
-            known = widen(known, step)
-        todo = todo[share:]
+        if n == ITERS // 2:
+            w, got_near = lax.optimization_barrier((w, got_near))
+            other = got_near[0, nx + SUBL : nx + SUBL + known.shape[0], :]
+            known = jnp.concatenate([known, other], 0)
+        if n >= ITERS // 2:
+            known, w = lax.optimization_barrier((known, w))
+            now = 1 if n + 1 < ITERS else len(steps) - 1
+            for step in steps[:now]:
+                known = widen(known, step)
+            steps = steps[now:]
         w = sweep(w, cu, cv, k, n + 1 == ITERS)
-    known, w, got_l, got_r = lax.optimization_barrier((known, w, got_l, got_r))
-    for step in todo:
+    known, w = lax.optimization_barrier((known, w))
+    for step in steps:
         known = widen(known, step)
-    edge_l, edge_r = strips(own_l, own_r, got_l, got_r, lev)
+    edge_l, edge_r = strips(odd_y, own_l, own_r, got_near, got_far, lev)
     state, columns, _ = finish(
-        me1, row, shift, pos, known, plume_profile, edge_l, edge_r, w, cap, order
+        me1, row, shift, pos, known.astype(I32), plume_profile, edge_l, edge_r, w, cap, order
     )
     columns = lax.all_to_all(columns, ("gx", "gy"), split_axis=0, concat_axis=0, tiled=True)
     return state, gradient(src, slot, columns, burn_weight)

time: 78.1 us -> 68.9 us (0.88)
  starting transfers between devices: 20.3 us -> 13.8 us
  blocking collectives: 15.3 us -> 10.8 us
  Pallas kernels: 40.4 us -> 41.5 us
    all_to_all x1, blocking collectives: 15.3 us -> 10.8 us  [on_device(): lax.all_to_all(columns, ('gx', 'gy'), split_axis=0, concat_axis=0, tiled=...]
    ppermute x4, starting transfers between devices: 8.4 us -> 4.46 us  [the longest x2 3.12 us: exchange(): first = lax.ppermute(near, axis, [(i, i ^ 1) for i in range(count)])]
    pallas_call x3, Pallas kernels: 8.49 us -> 5.45 us  [the longest x1 3.33 us: gradient(): pl.pallas_call(functools.partial(gradient_kernel, cells=cells, width=widt...]
    pallas_call x1, Pallas kernels: 8.62 us -> 11.3 us  [finish(): pl.pallas_call(functools.partial(finish_kernel, lev=lev, nx=nx, nt=nt, ca...]
    ppermute x5 -> x3, starting transfers between devices: 11.9 us -> 9.35 us  [widen(): return jnp.concatenate([known, lax.ppermute(known, axis, pairs)], 0)]
    pallas_call x4, Pallas kernels: 12.9 us -> 15 us  [sweep(): pl.pallas_call(functools.partial(sweep_kernel, lev=lev, nx=nx, nt=nt, las...]
  transfers between devices with their start and end apart: 9 -> 7, of which waited for: 0 -> 0; matrix products, arithmetic and copies ran while one was open for 0% -> 0% of each run, Pallas kernels for 29% -> 36%
where the time goes in v2:
time: 68.9 us; the launch traced here: 68.5 us
  Pallas kernels  41.5 us (60%)
  starting transfers between devices  13.8 us (20%)
  blocking collectives  10.8 us (16%)
  local copies, waits for them, and re-layouts  1.45 us (2%)
  between operations  0.88 us (1%)
    pallas_call x4, Pallas kernels, sweep(): pl.pallas_call(functools.partial(sweep_kernel, lev=lev, nx=nx, nt=nt, las...  15 us
    pallas_call x1, Pallas kernels, finish(): pl.pallas_call(functools.partial(finish_kernel, lev=lev, nx=nx, nt=nt, ca...  11.3 us
    all_to_all x1, blocking collectives, on_device(): lax.all_to_all(columns, ('gx', 'gy'), split_axis=0, concat_axis=0, tiled=...  10.8 us
    ppermute x3, starting transfers between devices, widen(): return jnp.concatenate([known, lax.ppermute(known, axis, pairs)], 0)  9.35 us
    pallas_call x1, Pallas kernels, prepare(): pl.pallas_call(functools.partial(prepare_kernel, lev=lev, nx=nx, nt=nt, c...  6.88 us
    pallas_call x1, Pallas kernels, gradient(): pl.pallas_call(functools.partial(gradient_kernel, cells=cells, width=widt...  3.33 us
    ppermute x2, starting transfers between devices, exchange(): first = lax.ppermute(near, axis, [(i, i ^ 1) for i in range(count)])  3.12 us
    pallas_call x1, Pallas kernels, strips(): pl.pallas_call(functools.partial(strips_kernel, lev=lev, nx=nx), out_shap...  2.43 us
  transfers between devices with their start and end apart: 7, of which 0 were waited for; matrix products, arithmetic and copies ran while one was open for 0% of the time, Pallas kernels for 36%

profile of v2, /device:TPU:0, one launch (start us, length us, event | category | flops | bytes accessed | tf_op | source)
XLA Modules:
  0.0 68.5 jit_solution(5617285321318179406)
XLA Ops:
  0.6 0.0 copy-start.1
  0.6 0.7 %copy-done.1 = s32[8192]{0:T(1024)S(1)} copy-done((s32[8192]{0:T(1024)S(1)}, s32[8192]{0:T(1024)}, u32[]{:S(2)}) %copy-start.1) | copy-done | bytes 32792
  1.4 0.4 tile_indices.1
  1.8 0.0 copy-start.3
  1.8 0.7 copy-done.3
  2.5 1.6 %pack_x.1 = (f32[33,8,384]{2,1,0:T(8,128)S(1)}, f32[32,8,384]{2,1,0:T(8,128)S(1)}) custom-call(s32[1]{0:T(128)} %bitcast.2.odd.odd_x, f32[16,192,384]{2,1,0:T(8,128)} %v_hbm.1, f32[16,192,384]{2,1,0:T(8,128)} %v_hbm.1, bf16[16,192,384]{2,1,0:T(8,128)(2,1)} %cu_hbm.1, bf16[16,192,384]{2,1,0:T(8,128)(2,1)} %cu_hbm.1, bf16[16,192,384]{2,1,0:T(8,128)(2,1)} %cv_hbm.1, ...), custom_call_target="tpu_custom_call" | custom-call | bytes 3145728 | tf_op jit(solution)/shard_map/pack_x/pallas_call | solution.py:81
  4.2 0.5 collective-permute-start
  4.7 0.7 collective-permute-start.1
  5.4 0.0 copy-start.4
  5.4 6.9 %prepare.1 = (f32[16,3,224,128]{3,2,1,0:T(8,128)S(1)}, f32[16,3,208,128]{3,2,1,0:T(8,128)S(1)}, f32[16,3,208,128]{3,2,1,0:T(8,128)S(1)}, f32[16,3,208,128]{3,2,1...) custom-call(s32[1]{0:T(128)} %bitcast.4.odd_ref.odd_y.odd, ...), custom_call_target="tpu_custom_call" | custom-call | flops 23592960 | bytes 35651584 | tf_op jit(solution)/shard_map/prepare/pallas_call | solution.py:217
  12.3 0.0 collective-permute-done.1.got_far
  12.3 0.0 collective-permute-done.got_near
  12.3 0.0 copy-done.4
  12.3 0.5 fill.1
  12.8 2.6 %collective-permute-start.2 = (f32[2,208,128]{2,1,0:T(8,128)S(1)}, f32[2,208,128]{2,1,0:T(8,128)S(1)}, u32[]{:S(2)}, u32[]{:S(2)}) collective-permute-start(f32[2,208,128]{2,1,0:T(8,128)S(1)} %get-tuple-element.70), channel_id=1, source_target_pairs={{0,1},{1,0},{2,3},{3,2},{4,5},{5,4},{6,7},{7,6},{8,9},{9,8},{10,11... | collective-permute-start | bytes 638984 | tf_op jit(solution)/shard_map/ppermute | solution.py:696
  15.4 4.1 %sweep.3.src = f32[16,3,224,128]{3,2,1,0:T(8,128)S(1)} custom-call(f32[16,3,224,128]{3,2,1,0:T(8,128)S(1)} %get-tuple-element.66.src, f32[16,3,208,128]{3,2,1,0:T(8,128)S(1)} %get-tuple-element.67.cuf, f32[16,3,208,128]{3,2,1,0:T(8,128)S(1)} %get-tuple-element.68.cvf, f32[16,3,208,128]{3,2,1,0:T(8,128)S(1)} %get-tuple-element.69.refs_0_), custom_call_target="tpu_custom_call" | custom-call | flops 21233664 | bytes 16777216 | tf_op jit(solution)/shard_map/sweep/pallas_call | solution.py:350
  19.5 3.8 %sweep.4.src = f32[16,3,224,128]{3,2,1,0:T(8,128)S(1)} custom-call(f32[16,3,224,128]{3,2,1,0:T(8,128)S(1)} %sweep.3.src, f32[16,3,208,128]{3,2,1,0:T(8,128)S(1)} %get-tuple-element.67.cuf, f32[16,3,208,128]{3,2,1,0:T(8,128)S(1)} %get-tuple-element.68.cvf, f32[16,3,208,128]{3,2,1,0:T(8,128)S(1)} %get-tuple-element.69.refs_0_), custom_call_target="tpu_custom_call" | custom-call | flops 21233664 | bytes 16777216 | tf_op jit(solution)/shard_map/sweep/pallas_call | solution.py:350
  23.3 0.0 collective-permute-done.2.got_near
  23.3 4.4 %collective-permute-start.3 = (f32[8,128]{1,0:T(8,128)S(1)}, f32[8,128]{1,0:T(8,128)S(1)}, u32[]{:S(2)}, u32[]{:S(2)}) collective-permute-start(f32[8,128]{1,0:T(8,128)S(1)} %pad_maximum_fusion.2), channel_id=1, source_target_pairs={{0,16},{4,20},{8,24},{12,28},{16,0},{20,4},{24,8},{28,12},{1,17},{... | collective-permute-start | bytes 12296 | tf_op jit(solution)/shard_map/ppermute | solution.py:735
  27.8 0.7 collective-permute-start.6
  28.4 4.1 %sweep.5.src = f32[16,3,224,128]{3,2,1,0:T(8,128)S(1)} custom-call(f32[16,3,224,128]{3,2,1,0:T(8,128)S(1)} %sweep.4.src, f32[16,3,208,128]{3,2,1,0:T(8,128)S(1)} %get-tuple-element.67.cuf, f32[16,3,208,128]{3,2,1,0:T(8,128)S(1)} %get-tuple-element.68.cvf, f32[16,3,208,128]{3,2,1,0:T(8,128)S(1)} %get-tuple-element.69.refs_0_), custom_call_target="tpu_custom_call" | custom-call | flops 21233664 | bytes 16777216 | tf_op jit(solution)/shard_map/sweep/pallas_call | solution.py:350
  32.5 0.0 collective-permute-done.3
  32.5 0.0 copy-start.2
  32.5 1.6 %collective-permute-start.4 = (f32[16,128]{1,0:T(8,128)S(1)}, f32[16,128]{1,0:T(8,128)S(1)}, u32[]{:S(2)}, u32[]{:S(2)}) collective-permute-start(f32[16,128]{1,0:T(8,128)S(1)} %pad_maximum_fusion.1), channel_id=1, source_target_pairs={{0,8},{4,12},{8,0},{12,4},{16,24},{20,28},{24,16},{28,20},{1,9},{5... | collective-permute-start | bytes 24584 | tf_op jit(solution)/shard_map/ppermute | solution.py:735
  34.2 3.1 %sweep_last.1 = f32[16,3,192,128]{3,2,1,0:T(8,128)S(1)} custom-call(f32[16,3,224,128]{3,2,1,0:T(8,128)S(1)} %sweep.5.src, f32[16,3,208,128]{3,2,1,0:T(8,128)S(1)} %get-tuple-element.67.cuf, f32[16,3,208,128]{3,2,1,0:T(8,128)S(1)} %get-tuple-element.68.cvf), custom_call_target="tpu_custom_call" | custom-call | flops 21233664 | bytes 16777216 | tf_op jit(solution)/shard_map/sweep_last/pallas_call | solution.py:350
  37.2 0.0 copy-start
  37.3 0.0 collective-permute-done.4
  37.3 3.3 %collective-permute-start.5 = (f32[32,128]{1,0:T(8,128)S(1)}, f32[32,128]{1,0:T(8,128)S(1)}, u32[]{:S(2)}, u32[]{:S(2)}) collective-permute-start(f32[32,128]{1,0:T(8,128)S(1)} %pad_maximum_fusion), channel_id=1, source_target_pairs={{0,2},{1,3},{2,0},{3,1},{4,6},{5,7},{6,4},{7,5},{8,10},{9,11},{10,... | collective-permute-start | bytes 49160 | tf_op jit(solution)/shard_map/ppermute | solution.py:735
  40.6 0.0 collective-permute-done.6.got_far
  40.6 2.4 %strips.1 = (f32[192,128]{1,0:T(8,128)S(1)}, f32[192,128]{1,0:T(8,128)S(1)}) custom-call(s32[1]{0:T(128)} %bitcast.4.odd_ref.odd_y.odd, f32[4,200,128]{2,1,0:T(8,128)S(1)} %get-tuple-element.78.own_l, f32[4,200,128]{2,1,0:T(8,128)S(1)} %get-tuple-element.79.own_r, f32[2,208,128]{2,1,0:T(8,128)S(1)} %collective-permute-done.2.got_near, ...), custom_call_target="tpu_custom_call" | custom-call | flops 10485760 | bytes 3145728 | tf_op jit(solution)/shard_map/strips/pallas_call | solution.py:502
  43.0 0.0 collective-permute-done.5
  43.1 0.0 copy-done.2
  43.1 11.3 %finish.1 = (f32[16,192,384]{2,1,0:T(8,128)}, f32[32,8,128]{2,1,0:T(8,128)S(1)}, f32[16,576,128]{2,1,0:T(8,128)S(1)}) custom-call(s32[1]{0:T(128)} %bitcast.me_ref, s32[32,128]{1,0:T(8,128)S(1)} %get-tuple-element.52.row, s32[32,128]{1,0:T(8,128)S(1)} %get-tuple-element.53.shift, ...), custom_call_target="tpu_custom_call", output_to_operand_aliasing={{2}: (8, {})} | custom-call | flops 31457280 | bytes 20971520 | tf_op jit(solution)/shard_map/finish/pallas_call | solution.py:590
  54.4 10.8 %all_to_all.5.got = f32[32,8,128]{2,1,0:T(8,128)S(1)} all-to-all(f32[32,8,128]{2,1,0:T(8,128)S(1)} %get-tuple-element.87), channel_id=1, replica_groups=mesh['gx'=8,'gy'=4] {'gx','gy'}, dimensions={0} | all-to-all | bytes 262144 | tf_op jit(solution)/shard_map/all_to_all | solution.py:766
  65.2 0.0 copy-done
  65.2 3.3 %gradient.1 = bf16[256,6400]{1,0:T(8,128)(2,1)} custom-call(s32[256,1]{1,0:T(8,128)S(1)} %get-tuple-element.85.src, s32[256,1]{1,0:T(8,128)S(1)} %get-tuple-element.86.slot, f32[32,8,128]{2,1,0:T(8,128)S(1)} %all_to_all.5.got, bf16[256,6400]{1,0:T(8,128)(2,1)S(1)} %copy-done), custom_call_target="tpu_custom_call" | custom-call | flops 838860800 | bytes 7340032 | tf_op jit(solution)/shard_map/gradient/pallas_call | solution.py:677
  (5 shorter events, 0.0 us)
Async XLA Ops:
  0.6 0.8 %copy-start.1 = (s32[8192]{0:T(1024)S(1)}, s32[8192]{0:T(1024)}, u32[]{:S(2)}) copy-start(s32[8192]{0:T(1024)} %param.12) | copy-start | bytes 98308
  1.8 0.7 copy-start.3
  4.2 8.1 %collective-permute-start = (f32[33,8,384]{2,1,0:T(8,128)S(1)}, f32[33,8,384]{2,1,0:T(8,128)S(1)}, u32[]{:S(2)}, u32[]{:S(2)}) collective-permute-start(f32[33,8,384]{2,1,0:T(8,128)S(1)} %get-tuple-element.55), channel_id=1, source_target_pairs={{0,4},{4,0},{8,12},{12,8},{16,20},{20,16},{24,28},{28,24},{1,5},{5... | collective-permute-start | bytes 1216520 | tf_op jit(solution)/shard_map/ppermute | solution.py:696
  4.7 7.6 %collective-permute-start.1 = (f32[32,8,384]{2,1,0:T(8,128)S(1)}, f32[32,8,384]{2,1,0:T(8,128)S(1)}, u32[]{:S(2)}, u32[]{:S(2)}) collective-permute-start(f32[32,8,384]{2,1,0:T(8,128)S(1)} %get-tuple-element.56), channel_id=1, source_target_pairs={{4,8},{12,16},{20,24},{8,4},{16,12},{24,20},{5,9},{13,17},{21,25},... | collective-permute-start | bytes 1179656 | tf_op jit(solution)/shard_map/ppermute | solution.py:698
  5.4 6.9 %copy-start.4 = (s32[256]{0:T(256)S(1)}, s32[256]{0:T(256)}, u32[]{:S(2)}) copy-start(s32[256]{0:T(256)} %param.13) | copy-start | bytes 3076
  12.8 10.5 %collective-permute-start.2 = (f32[2,208,128]{2,1,0:T(8,128)S(1)}, f32[2,208,128]{2,1,0:T(8,128)S(1)}, u32[]{:S(2)}, u32[]{:S(2)}) collective-permute-start(f32[2,208,128]{2,1,0:T(8,128)S(1)} %get-tuple-element.70), channel_id=1, source_target_pairs={{0,1},{1,0},{2,3},{3,2},{4,5},{5,4},{6,7},{7,6},{8,9},{9,8},{10,11... | collective-permute-start | bytes 638984 | tf_op jit(solution)/shard_map/ppermute | solution.py:696
  23.3 9.2 %collective-permute-start.3 = (f32[8,128]{1,0:T(8,128)S(1)}, f32[8,128]{1,0:T(8,128)S(1)}, u32[]{:S(2)}, u32[]{:S(2)}) collective-permute-start(f32[8,128]{1,0:T(8,128)S(1)} %pad_maximum_fusion.2), channel_id=1, source_target_pairs={{0,16},{4,20},{8,24},{12,28},{16,0},{20,4},{24,8},{28,12},{1,17},{... | collective-permute-start | bytes 12296 | tf_op jit(solution)/shard_map/ppermute | solution.py:735
  27.8 12.8 %collective-permute-start.6 = (f32[2,200,128]{2,1,0:T(8,128)S(1)}, f32[2,200,128]{2,1,0:T(8,128)S(1)}, u32[]{:S(2)}, u32[]{:S(2)}) collective-permute-start(f32[2,200,128]{2,1,0:T(8,128)S(1)} %get-tuple-element.80), channel_id=1, source_target_pairs={{1,2},{2,1},{5,6},{6,5},{9,10},{10,9},{13,14},{14,13},{17,18},{18,... | collective-permute-start | bytes 614408 | tf_op jit(solution)/shard_map/ppermute | solution.py:698
  32.5 10.5 %copy-start.2 = (f32[16,16]{1,0:T(8,128)S(1)}, f32[16,16]{1,0:T(8,128)}, u32[]{:S(2)}) copy-start(f32[16,16]{1,0:T(8,128)} %prof.1) | copy-start | bytes 3076
  32.5 4.7 %collective-permute-start.4 = (f32[16,128]{1,0:T(8,128)S(1)}, f32[16,128]{1,0:T(8,128)S(1)}, u32[]{:S(2)}, u32[]{:S(2)}) collective-permute-start(f32[16,128]{1,0:T(8,128)S(1)} %pad_maximum_fusion.1), channel_id=1, source_target_pairs={{0,8},{4,12},{8,0},{12,4},{16,24},{20,28},{24,16},{28,20},{1,9},{5... | collective-permute-start | bytes 24584 | tf_op jit(solution)/shard_map/ppermute | solution.py:735
  37.2 27.9 %copy-start = (bf16[256,6400]{1,0:T(8,128)(2,1)S(1)}, bf16[256,6400]{1,0:T(8,128)(2,1)}, u32[]{:S(2)}) copy-start(bf16[256,6400]{1,0:T(8,128)(2,1)} %burn.1) | copy-start | bytes 9830404
  37.3 5.7 %collective-permute-start.5 = (f32[32,128]{1,0:T(8,128)S(1)}, f32[32,128]{1,0:T(8,128)S(1)}, u32[]{:S(2)}, u32[]{:S(2)}) collective-permute-start(f32[32,128]{1,0:T(8,128)S(1)} %pad_maximum_fusion), channel_id=1, source_target_pairs={{0,2},{1,3},{2,0},{3,1},{4,6},{5,7},{6,4},{7,5},{8,10},{9,11},{10,... | collective-permute-start | bytes 49160 | tf_op jit(solution)/shard_map/ppermute | solution.py:735

commit v3 on v2

--- a/solution.py
+++ b/solution.py
@@ -148,10 +148,54 @@
         cur, below = (nxt, flux)
 
 
+def index_kernel(me_ref, blocks, row, shift, pos, src_col, slot_col, *, tiles, per_x, per_y, gy, cap, nx):
+    per = tiles // LANES
+    procs = blocks.shape[0] // per
+    me = me_ref[0]
+    per_tile = LANES // TB
+
+    def lines(start, count, stride):
+        return jnp.concatenate([blocks[pl.ds(start + i, count, stride), :] for i in range(per)], 1)
+
+    def owner(b):
+        br, bc = (b // (per_y * gy), b % (per_y * gy))
+        return br // per_x * gy + bc // per_y, br % per_x, bc % per_y
+
+    src, lr, lc = owner(lines(0, procs, per))
+    mine = src == me
+    t = lane_id((procs, tiles))
+    upper = lax.broadcasted_iota(I32, (tiles, tiles), 0) <= lane_id((tiles, tiles))
+    rank = jnp.dot(
+        mine.astype(F32).astype(BF16), upper.astype(F32).astype(BF16), preferred_element_type=F32
+    ).astype(I32)
+    code = ((lc // per_tile * (nx // TB) + lr) * per_tile + lc % per_tile) * tiles + t + 1
+    lane = lane_id((procs, LANES))
+    found = jnp.zeros((procs, LANES), I32)
+    for s in range(cap):
+        hit = mine & (rank == s + 1)
+        one = jnp.sum(jnp.where(hit, code, 0).astype(F32), axis=1, keepdims=True).astype(I32)
+        found = jnp.where(lane == s, one, found)
+    value = found - 1
+    spot = value // tiles
+    row[...] = jnp.where(found > 0, spot // per_tile, 0)
+    shift[...] = (lane * TB - spot % per_tile * TB) & (LANES - 1)
+    pos[...] = jnp.where(found > 0, value % tiles, 0)
+    own = owner(lines(me * per, 1, 1))[0]
+    i = lax.broadcasted_iota(I32, (tiles, tiles), 0)
+    j = lane_id((tiles, tiles))
+    own_all = jnp.broadcast_to(own, (tiles, tiles)).astype(F32)
+    col = jnp.sum(jnp.where(i == j, own_all, 0.0), axis=1, keepdims=True)
+    same = (own_all == col) & (j < i)
+    src_col[...] = col.astype(I32)
+    slot_col[...] = jnp.sum(jnp.where(same, 1.0, 0.0), axis=1, keepdims=True).astype(I32)
+
+
 def prepare_kernel(
-    odd_ref, v_hbm, cu_hbm, cv_hbm, k_hbm, w, cuf, cvf, kf, own_l, own_r, near, far, vs, cus, cvs, ks, sem,
-    *, lev, nx, nt, chunks,
+    odd_ref, me_ref, blocks_hbm, v_hbm, cu_hbm, cv_hbm, k_hbm, w, cuf, cvf, kf, own_l, own_r, near, far,
+    row, shift, pos, src_col, slot_col, vs, cus, cvs, ks, blocks, sem, bsem, *, lev, nx, nt, chunks, index,
 ):
+    table = pltpu.make_async_copy(blocks_hbm, blocks, bsem)
+    table.start()
     part = nx // chunks
     copies = []
     for c in range(chunks):
@@ -200,32 +244,46 @@
         store_edges(packed, (own_l, own_r), near, far, at, odd_ref[0] != 0)
         return 0
 
+    def two(n, _):
+        rows(2 * n, 0)
+        return rows(2 * n + 1, 0)
+
     for c in range(chunks):
         for x in copies[c]:
             x.wait()
         lax.fori_loop(c * part // ROWS, (c + 1) * part // ROWS, rows, 0)
 
-
-def prepare(odd, v, cu, cv, k):
+    table.wait()
+    index_kernel(me_ref, blocks, row, shift, pos, src_col, slot_col, nx=nx, **index)
+
+
+def prepare(odd, me, tile_block, procs, cap, gy, v, cu, cv, k):
     lev, nx, ny = v.shape
     nt = ny // LANES
     chunks = max(c for c in (1, 2, 3, 4) if nx % (c * ROWS) == 0)
+    tiles = tile_block.shape[0] // procs
+    blocks = pltpu.with_memory_space_constraint(tile_block.reshape(-1, LANES), pltpu.HBM)
+    index = dict(tiles=tiles, per_x=nx // TB, per_y=ny // TB, gy=gy, cap=cap)
+    table = jax.ShapeDtypeStruct((procs, LANES), I32)
+    column = jax.ShapeDtypeStruct((tiles, 1), I32)
     wide = jax.ShapeDtypeStruct((lev, nt, nx + 2 * EDGE, LANES), F32)
     own = jax.ShapeDtypeStruct((4, nx + SUBL, LANES), F32)
     near = jax.ShapeDtypeStruct((2, nx + 2 * SUBL, LANES), F32)
     far = jax.ShapeDtypeStruct((2, nx + SUBL, LANES), F32)
     return pl.pallas_call(
-        functools.partial(prepare_kernel, lev=lev, nx=nx, nt=nt, chunks=chunks),
-        out_shape=(jax.ShapeDtypeStruct((lev, nt, nx + 2 * FRONT, LANES), F32), wide, wide, wide, own, own, near, far),
-        in_specs=[SMEM] + [HBM] * 4,
-        out_specs=(VMEM,) * 8,
+        functools.partial(prepare_kernel, lev=lev, nx=nx, nt=nt, chunks=chunks, index=index),
+        out_shape=(jax.ShapeDtypeStruct((lev, nt, nx + 2 * FRONT, LANES), F32), wide, wide, wide, own, own, near, far)
+        + (table,) * 3
+        + (column,) * 2,
+        in_specs=[SMEM] * 2 + [HBM] * 5,
+        out_specs=(VMEM,) * 13,
         scratch_shapes=[pltpu.VMEM((lev, nx, ny), F32)]
         + [pltpu.VMEM((lev, nx, ny), BF16)] * 3
-        + [pltpu.SemaphoreType.DMA((chunks, 4))],
+        + [pltpu.VMEM(blocks.shape, I32), pltpu.SemaphoreType.DMA((chunks, 4)), pltpu.SemaphoreType.DMA],
         compiler_params=params(14),
         cost_estimate=cost(20 * lev * nx * ny, 34 << 20),
         name="prepare",
-    )(odd, v, cu, cv, k)
+    )(odd, me, blocks, v, cu, cv, k)
 
 
 def fill_kernel(odd_x, odd_y, inj, got_near, got_far, *refs, lev, nx, nt):
@@ -315,10 +373,9 @@
 
     def body(g, _):
         if last_step:
-            at = pl.ds(pl.multiple_of(g * SUBL - EDGE, SUBL), SUBL)
             for l in range(lev):
                 for j, x in enumerate(advect(l, g)):
-                    dst[l, j, at, :] = x
+                    dst[j * (nx // SUBL) + g - 1, l] = x
             return 0
         at = pl.ds(pl.multiple_of(g * SUBL + (FRONT - EDGE), SUBL), SUBL)
 
@@ -346,7 +403,7 @@
     lev, nt, rows, _ = src.shape
     nx = rows - 2 * FRONT
     ins = (src, cuf, cvf) if last_step else (src, cuf, cvf, kf)
-    shape = (lev, nt, nx, LANES) if last_step else src.shape
+    shape = (nt * nx // SUBL, lev, SUBL, LANES) if last_step else src.shape
     return pl.pallas_call(
         functools.partial(sweep_kernel, lev=lev, nx=nx, nt=nt, last_step=last_step),
         out_shape=jax.ShapeDtypeStruct(shape, F32),
@@ -356,64 +413,6 @@
         cost_estimate=cost(18 * lev * nt * nx * LANES, 16 << 20),
         name="sweep_last" if last_step else "sweep",
     )(*ins)
-
-
-def index_kernel(me_ref, blocks, row, shift, pos, src_col, slot_col, *, tiles, per_x, per_y, gy, cap, nx):
-    per = tiles // LANES
-    procs = blocks.shape[0] // per
-    me = me_ref[0]
-    per_tile = LANES // TB
-
-    def lines(start, count, stride):
-        return jnp.concatenate([blocks[pl.ds(start + i, count, stride), :] for i in range(per)], 1)
-
-    def owner(b):
-        br, bc = (b // (per_y * gy), b % (per_y * gy))
-        return br // per_x * gy + bc // per_y, br % per_x, bc % per_y
-
-    src, lr, lc = owner(lines(0, procs, per))
-    mine = src == me
-    t = lane_id((procs, tiles))
-    upper = lax.broadcasted_iota(I32, (tiles, tiles), 0) <= lane_id((tiles, tiles))
-    rank = jnp.dot(
-        mine.astype(F32).astype(BF16), upper.astype(F32).astype(BF16), preferred_element_type=F32
-    ).astype(I32)
-    code = ((lc // per_tile * nx + lr * TB) * per_tile + lc % per_tile) * tiles + t + 1
-    lane = lane_id((procs, LANES))
-    found = jnp.zeros((procs, LANES), I32)
-    for s in range(cap):
-        hit = mine & (rank == s + 1)
-        one = jnp.sum(jnp.where(hit, code, 0).astype(F32), axis=1, keepdims=True).astype(I32)
-        found = jnp.where(lane == s, one, found)
-    value = found - 1
-    spot = value // tiles
-    row[...] = jnp.where(found > 0, spot // per_tile, 0)
-    shift[...] = (lane * TB - spot % per_tile * TB) & (LANES - 1)
-    pos[...] = jnp.where(found > 0, value % tiles, 0)
-    own = owner(lines(me * per, 1, 1))[0]
-    i = lax.broadcasted_iota(I32, (tiles, tiles), 0)
-    j = lane_id((tiles, tiles))
-    own_all = jnp.broadcast_to(own, (tiles, tiles)).astype(F32)
-    col = jnp.sum(jnp.where(i == j, own_all, 0.0), axis=1, keepdims=True)
-    same = (own_all == col) & (j < i)
-    src_col[...] = col.astype(I32)
-    slot_col[...] = jnp.sum(jnp.where(same, 1.0, 0.0), axis=1, keepdims=True).astype(I32)
-
-
-def tile_indices(me, blocks, procs, cap, per_x, per_y, gy, nx):
-    tiles = blocks.shape[0] // procs
-    blocks = blocks.reshape(-1, LANES)
-    table = jax.ShapeDtypeStruct((procs, LANES), I32)
-    column = jax.ShapeDtypeStruct((tiles, 1), I32)
-    return pl.pallas_call(
-        functools.partial(index_kernel, tiles=tiles, per_x=per_x, per_y=per_y, gy=gy, cap=cap, nx=nx),
-        out_shape=(table, table, table, column, column),
-        in_specs=[SMEM, VMEM],
-        out_specs=(VMEM,) * 5,
-        compiler_params=params(8),
-        cost_estimate=cost(0, 1 << 20),
-        name="tile_indices",
-    )(me, blocks)
 
 
 def strips_kernel(odd, own_l, own_r, got_near, got_far, out_l, out_r, strip, other, coef, *, lev, nx):
@@ -528,7 +527,7 @@
     lane8 = lane_id((SUBL, LANES))
     width = HALO
     outer, inner = (lane8 < width, lane8 >= LANES - width)
-    base = (nt - 1) * nx
+    base = (nt - 1) * nx // SUBL
 
     def patch(n, _):
         for m in range(2):
@@ -538,18 +537,23 @@
             for g in range(0, nx, SUBL):
                 x, y = (edge_l[g : g + SUBL, :], edge_r[g : g + SUBL, :])
                 x = jnp.take_along_axis(x, take_l, axis=1)
-                field[l, g : g + SUBL, :] = jnp.where(outer, x, field[l, g : g + SUBL, :])
                 y = jnp.take_along_axis(y, take_r, axis=1)
-                g = base + g
-                field[l, g : g + SUBL, :] = jnp.where(inner, y, field[l, g : g + SUBL, :])
+                g //= SUBL
+                field[g, l] = jnp.where(outer, x, field[g, l])
+                g += base
+                field[g, l] = jnp.where(inner, y, field[g, l])
         return 0
 
     lax.fori_loop(0, lev // 2, patch, 0)
+    count = nx // SUBL
     puts = [
         pltpu.make_async_copy(
-            field.at[:, pl.ds(j * nx, nx), :], state.at[:, :, pl.ds(j * LANES, LANES)], osem.at[j]
+            field.at[pl.ds(j * count, count), l],
+            state.at[l, :, :, pl.ds(j * LANES, LANES)],
+            osem.at[j, l],
         )
         for j in range(nt)
+        for l in range(lev)
     ]
     for c in puts:
         c.start()
@@ -564,10 +568,10 @@
         for n, bit in enumerate(order):
             source = source | (apart >> bit.bit_length() - 1 & 1) << n
         for s in range(cap):
-            at = pl.ds(pl.multiple_of(row[h, s], TB), TB)
+            at = row[h, s]
             tile = pos[h, s]
             level = inj[source * lines + (tile >> LANES.bit_length() - 1), tile & (LANES - 1)]
-            terms = [weight[level, l] * field[l, at, :] for l in range(lev)]
+            terms = [weight[level, l] * field[at, l] for l in range(lev)]
             while len(terms) > 1:
                 terms = [x + y for x, y in zip(terms[::2], terms[1::2])]
             out = jnp.where(slot_of == s, pltpu.roll(terms[0], shift[h, s], 1), out)
@@ -584,24 +588,25 @@
 
 
 def finish(me, row, shift, pos, inj, prof, edge_l, edge_r, mid, cap, order):
-    lev, nt, nx, _ = mid.shape
+    lev, nx = (mid.shape[1], edge_l.shape[0])
+    nt = mid.shape[0] * SUBL // nx
     procs = row.shape[0]
-    mid = mid.reshape(lev, nt * nx, LANES)
-    return pl.pallas_call(
+    state, send, _ = pl.pallas_call(
         functools.partial(finish_kernel, lev=lev, nx=nx, nt=nt, cap=cap, procs=procs, order=order),
         out_shape=(
-            jax.ShapeDtypeStruct((lev, nx, nt * LANES), F32),
+            jax.ShapeDtypeStruct((lev, nx // SUBL, SUBL, nt * LANES), F32),
             jax.ShapeDtypeStruct((procs, TB, LANES), F32),
             jax.ShapeDtypeStruct(mid.shape, F32),
         ),
         in_specs=[SMEM] * 6 + [VMEM] * 3,
         out_specs=(HBM, VMEM, VMEM),
         input_output_aliases={8: 2},
-        scratch_shapes=[pltpu.VMEM((lev, lev, TB, LANES), F32), pltpu.SemaphoreType.DMA((nt,))],
+        scratch_shapes=[pltpu.VMEM((lev, lev, TB, LANES), F32), pltpu.SemaphoreType.DMA((nt, lev))],
         compiler_params=params(4),
         cost_estimate=cost(30 << 20, 20 << 20),
         name="finish",
     )(me, row, shift, pos, inj, prof, edge_l, edge_r, mid)
+    return state.reshape(lev, nx, nt * LANES), send
 
 
 def split3(x):
@@ -735,14 +740,11 @@
         return jnp.concatenate([known, lax.ppermute(known, axis, pairs)], 0)
 
     odd_x, odd_y = ((lax.axis_index(a).astype(I32) & 1).reshape(1) for a in ("gx", "gy"))
-    near, far = pack_x(odd_x, *fields, inj)
-    row, shift, pos, src, slot, near, far = lax.optimization_barrier(
-        tuple(tile_indices(me1, tile_block, procs, cap, nx // TB, ny // TB, gy, nx)) + (near, far)
-    )
+    near, far = pack_x(odd_x, *fields, pltpu.with_memory_space_constraint(inj, pltpu.HBM))
     got_near, got_far = exchange(near, far, "gx")
-    w, cu, cv, k, own_l, own_r, near, far, known = fill(
-        odd_x, odd_y, inj, got_near, got_far, prepare(odd_y, *fields)
-    )
+    ready = prepare(odd_y, me1, tile_block, procs, cap, gy, *fields)
+    row, shift, pos, src, slot = ready[8:]
+    w, cu, cv, k, own_l, own_r, near, far, known = fill(odd_x, odd_y, inj, got_near, got_far, ready[:8])
     got_near, got_far = exchange(near, far, "gy")
     for n in range(ITERS):
         if n == ITERS // 2:
@@ -760,7 +762,7 @@
     for step in steps:
         known = widen(known, step)
     edge_l, edge_r = strips(odd_y, own_l, own_r, got_near, got_far, lev)
-    state, columns, _ = finish(
+    state, columns = finish(
         me1, row, shift, pos, known.astype(I32), plume_profile, edge_l, edge_r, w, cap, order
     )
     columns = lax.all_to_all(columns, ("gx", "gy"), split_axis=0, concat_axis=0, tiled=True)

time: 68.9 us -> 64 us (0.929)
  Pallas kernels: 41.5 us -> 37.7 us
  local copies, waits for them, and re-layouts: 1.45 us -> 0.02 us
    pallas_call x1, Pallas kernels: 11.3 us -> 8.81 us  [finish(): pl.pallas_call(functools.partial(finish_kernel, lev=lev, nx=nx, nt=nt, ca...]
    unnamed x10 -> x6, local copies, waits for them, and re-layouts: 1.44 us -> 0.02 us
    pallas_call x4, Pallas kernels: 15 us -> 13.7 us  [sweep(): pl.pallas_call(functools.partial(sweep_kernel, lev=lev, nx=nx, nt=nt, las...]
  transfers between devices with their start and end apart: 7 -> 7, of which waited for: 0 -> 0; matrix products, arithmetic and copies ran while one was open for 0% -> 0% of each run, Pallas kernels for 36% -> 37%
where the time goes in v3:
time: 64 us; the launch traced here: 63.8 us
  Pallas kernels  37.7 us (59%)
  starting transfers between devices  13.8 us (22%)
  blocking collectives  11.3 us (18%)
  between operations  0.86 us (1%)
    pallas_call x4, Pallas kernels, sweep(): pl.pallas_call(functools.partial(sweep_kernel, lev=lev, nx=nx, nt=nt, las...  13.7 us
    all_to_all x1, blocking collectives, on_device(): lax.all_to_all(columns, ('gx', 'gy'), split_axis=0, concat_axis=0, tiled=...  11.3 us
    ppermute x3, starting transfers between devices, widen(): return jnp.concatenate([known, lax.ppermute(known, axis, pairs)], 0)  9.36 us
    pallas_call x1, Pallas kernels, finish(): pl.pallas_call(functools.partial(finish_kernel, lev=lev, nx=nx, nt=nt, ca...  8.81 us
    pallas_call x1, Pallas kernels, prepare(): pl.pallas_call(functools.partial(prepare_kernel, lev=lev, nx=nx, nt=nt, c...  7.32 us
    pallas_call x1, Pallas kernels, gradient(): pl.pallas_call(functools.partial(gradient_kernel, cells=cells, width=widt...  3.32 us
    ppermute x2, starting transfers between devices, exchange(): first = lax.ppermute(near, axis, [(i, i ^ 1) for i in range(count)])  3.12 us
    pallas_call x1, Pallas kernels, strips(): pl.pallas_call(functools.partial(strips_kernel, lev=lev, nx=nx), out_shap...  2.43 us
  transfers between devices with their start and end apart: 7, of which 0 were waited for; matrix products, arithmetic and copies ran while one was open for 0% of the time, Pallas kernels for 37%

profile of v3, /device:TPU:0, one launch (start us, length us, event | category | flops | bytes accessed | tf_op | source)
XLA Modules:
  0.0 63.8 jit_solution(5754558427716501569)
XLA Ops:
  0.6 1.7 %pack_x.1 = (f32[33,8,384]{2,1,0:T(8,128)S(1)}, f32[32,8,384]{2,1,0:T(8,128)S(1)}) custom-call(s32[1]{0:T(128)} %bitcast.3.odd.odd_x, f32[16,192,384]{2,1,0:T(8,128)} %vb.1, f32[16,192,384]{2,1,0:T(8,128)} %vb.1, bf16[16,192,384]{2,1,0:T(8,128)(2,1)} %cub.1, bf16[16,192,384]{2,1,0:T(8,128)(2,1)} %cub.1, bf16[16,192,384]{2,1,0:T(8,128)(2,1)} %cvb.1, ...), custom_call_target="tpu_custom_call" | custom-call | bytes 3145728 | tf_op jit(solution)/shard_map/pack_x/pallas_call | solution.py:81
  2.3 0.5 collective-permute-start
  2.8 0.7 %collective-permute-start.1 = (f32[32,8,384]{2,1,0:T(8,128)S(1)}, f32[32,8,384]{2,1,0:T(8,128)S(1)}, u32[]{:S(2)}, u32[]{:S(2)}) collective-permute-start(f32[32,8,384]{2,1,0:T(8,128)S(1)} %get-tuple-element.42), channel_id=1, source_target_pairs={{4,8},{12,16},{20,24},{8,4},{16,12},{24,20},{5,9},{13,17},{21,25},... | collective-permute-start | bytes 1179656 | tf_op jit(solution)/shard_map/ppermute | solution.py:703
  3.5 0.0 copy-start.2
  3.6 7.3 %prepare.1 = (f32[16,3,224,128]{3,2,1,0:T(8,128)S(1)}, f32[16,3,208,128]{3,2,1,0:T(8,128)S(1)}, f32[16,3,208,128]{3,2,1,0:T(8,128)S(1)}, f32[16,3,208,128]{3,2,1...) custom-call(s32[1]{0:T(128)} %bitcast.1.odd_ref.odd_y.odd, ...), custom_call_target="tpu_custom_call" | custom-call | flops 23592960 | bytes 35651584 | tf_op jit(solution)/shard_map/prepare/pallas_call | solution.py:273
  10.9 0.0 collective-permute-done.1.got_far
  10.9 0.0 collective-permute-done.got_near
  10.9 0.0 copy-done.2
  10.9 0.5 fill.1
  11.4 2.6 %collective-permute-start.2 = (f32[2,208,128]{2,1,0:T(8,128)S(1)}, f32[2,208,128]{2,1,0:T(8,128)S(1)}, u32[]{:S(2)}, u32[]{:S(2)}) collective-permute-start(f32[2,208,128]{2,1,0:T(8,128)S(1)} %get-tuple-element.56), channel_id=1, source_target_pairs={{0,1},{1,0},{2,3},{3,2},{4,5},{5,4},{6,7},{7,6},{8,9},{9,8},{10,11... | collective-permute-start | bytes 638984 | tf_op jit(solution)/shard_map/ppermute | solution.py:701
  14.0 4.0 %sweep.3.src = f32[16,3,224,128]{3,2,1,0:T(8,128)S(1)} custom-call(f32[16,3,224,128]{3,2,1,0:T(8,128)S(1)} %get-tuple-element.52.src, f32[16,3,208,128]{3,2,1,0:T(8,128)S(1)} %get-tuple-element.53.cuf, f32[16,3,208,128]{3,2,1,0:T(8,128)S(1)} %get-tuple-element.54.cvf, f32[16,3,208,128]{3,2,1,0:T(8,128)S(1)} %get-tuple-element.55.refs_0_), custom_call_target="tpu_custom_call" | custom-call | flops 21233664 | bytes 16777216 | tf_op jit(solution)/shard_map/sweep/pallas_call | solution.py:407
  17.9 3.1 %sweep.4.src = f32[16,3,224,128]{3,2,1,0:T(8,128)S(1)} custom-call(f32[16,3,224,128]{3,2,1,0:T(8,128)S(1)} %sweep.3.src, f32[16,3,208,128]{3,2,1,0:T(8,128)S(1)} %get-tuple-element.53.cuf, f32[16,3,208,128]{3,2,1,0:T(8,128)S(1)} %get-tuple-element.54.cvf, f32[16,3,208,128]{3,2,1,0:T(8,128)S(1)} %get-tuple-element.55.refs_0_), custom_call_target="tpu_custom_call" | custom-call | flops 21233664 | bytes 16777216 | tf_op jit(solution)/shard_map/sweep/pallas_call | solution.py:407
  21.1 0.0 collective-permute-done.2.got_near
  21.1 4.4 %collective-permute-start.3 = (f32[8,128]{1,0:T(8,128)S(1)}, f32[8,128]{1,0:T(8,128)S(1)}, u32[]{:S(2)}, u32[]{:S(2)}) collective-permute-start(f32[8,128]{1,0:T(8,128)S(1)} %pad_maximum_fusion.2), channel_id=1, source_target_pairs={{0,16},{4,20},{8,24},{12,28},{16,0},{20,4},{24,8},{28,12},{1,17},{... | collective-permute-start | bytes 12296 | tf_op jit(solution)/shard_map/ppermute | solution.py:740
  25.6 0.7 %collective-permute-start.6 = (f32[2,200,128]{2,1,0:T(8,128)S(1)}, f32[2,200,128]{2,1,0:T(8,128)S(1)}, u32[]{:S(2)}, u32[]{:S(2)}) collective-permute-start(f32[2,200,128]{2,1,0:T(8,128)S(1)} %get-tuple-element.66), channel_id=1, source_target_pairs={{1,2},{2,1},{5,6},{6,5},{9,10},{10,9},{13,14},{14,13},{17,18},{18,... | collective-permute-start | bytes 614408 | tf_op jit(solution)/shard_map/ppermute | solution.py:703
  26.2 3.9 %sweep.5.src = f32[16,3,224,128]{3,2,1,0:T(8,128)S(1)} custom-call(f32[16,3,224,128]{3,2,1,0:T(8,128)S(1)} %sweep.4.src, f32[16,3,208,128]{3,2,1,0:T(8,128)S(1)} %get-tuple-element.53.cuf, f32[16,3,208,128]{3,2,1,0:T(8,128)S(1)} %get-tuple-element.54.cvf, f32[16,3,208,128]{3,2,1,0:T(8,128)S(1)} %get-tuple-element.55.refs_0_), custom_call_target="tpu_custom_call" | custom-call | flops 21233664 | bytes 16777216 | tf_op jit(solution)/shard_map/sweep/pallas_call | solution.py:407
  30.2 0.0 collective-permute-done.3
  30.2 0.0 copy-start.1
  30.2 1.6 %collective-permute-start.4 = (f32[16,128]{1,0:T(8,128)S(1)}, f32[16,128]{1,0:T(8,128)S(1)}, u32[]{:S(2)}, u32[]{:S(2)}) collective-permute-start(f32[16,128]{1,0:T(8,128)S(1)} %pad_maximum_fusion.1), channel_id=1, source_target_pairs={{0,8},{4,12},{8,0},{12,4},{16,24},{20,28},{24,16},{28,20},{1,9},{5... | collective-permute-start | bytes 24584 | tf_op jit(solution)/shard_map/ppermute | solution.py:740
  31.8 2.6 %sweep_last.1.mid = f32[72,16,8,128]{3,2,1,0:T(8,128)S(1)} custom-call(f32[16,3,224,128]{3,2,1,0:T(8,128)S(1)} %sweep.5.src, f32[16,3,208,128]{3,2,1,0:T(8,128)S(1)} %get-tuple-element.53.cuf, f32[16,3,208,128]{3,2,1,0:T(8,128)S(1)} %get-tuple-element.54.cvf), custom_call_target="tpu_custom_call" | custom-call | flops 21233664 | bytes 16777216 | tf_op jit(solution)/shard_map/sweep_last/pallas_call | solution.py:407
  34.5 0.0 copy-start
  34.5 0.0 collective-permute-done.4
  34.5 3.3 %collective-permute-start.5 = (f32[32,128]{1,0:T(8,128)S(1)}, f32[32,128]{1,0:T(8,128)S(1)}, u32[]{:S(2)}, u32[]{:S(2)}) collective-permute-start(f32[32,128]{1,0:T(8,128)S(1)} %pad_maximum_fusion), channel_id=1, source_target_pairs={{0,2},{1,3},{2,0},{3,1},{4,6},{5,7},{6,4},{7,5},{8,10},{9,11},{10,... | collective-permute-start | bytes 49160 | tf_op jit(solution)/shard_map/ppermute | solution.py:740
  37.8 0.0 collective-permute-done.6.got_far
  37.8 2.4 %strips.1 = (f32[192,128]{1,0:T(8,128)S(1)}, f32[192,128]{1,0:T(8,128)S(1)}) custom-call(s32[1]{0:T(128)} %bitcast.1.odd_ref.odd_y.odd, f32[4,200,128]{2,1,0:T(8,128)S(1)} %get-tuple-element.64.own_l, f32[4,200,128]{2,1,0:T(8,128)S(1)} %get-tuple-element.65.own_r, f32[2,208,128]{2,1,0:T(8,128)S(1)} %collective-permute-done.2.got_near, ...), custom_call_target="tpu_custom_call" | custom-call | flops 10485760 | bytes 3145728 | tf_op jit(solution)/shard_map/strips/pallas_call | solution.py:501
  40.3 0.0 collective-permute-done.5
  40.3 0.0 copy-done.1
  40.3 8.8 %finish.1 = (f32[16,24,8,384]{3,2,1,0:T(8,128)}, f32[32,8,128]{2,1,0:T(8,128)S(1)}, f32[72,16,8,128]{3,2,1,0:T(8,128)S(1)}) custom-call(s32[1]{0:T(128)} %bitcast.me_ref, s32[32,128]{1,0:T(8,128)S(1)} %get-tuple-element.38.row, s32[32,128]{1,0:T(8,128)S(1)} %get-tuple-element.39.shift, ...), custom_call_target="tpu_custom_call", output_to_operand_aliasing={{2}: (8, {})} | custom-call | flops 31457280 | bytes 20971520 | tf_op jit(solution)/shard_map/finish/pallas_call | solution.py:594
  49.1 11.3 %all_to_all.5.got = f32[32,8,128]{2,1,0:T(8,128)S(1)} all-to-all(f32[32,8,128]{2,1,0:T(8,128)S(1)} %get-tuple-element.73), channel_id=1, replica_groups=mesh['gx'=8,'gy'=4] {'gx','gy'}, dimensions={0} | all-to-all | bytes 262144 | tf_op jit(solution)/shard_map/all_to_all | solution.py:768
  60.5 0.0 copy-done
  60.5 3.3 %gradient.1 = bf16[256,6400]{1,0:T(8,128)(2,1)} custom-call(s32[256,1]{1,0:T(8,128)S(1)} %get-tuple-element.71.src, s32[256,1]{1,0:T(8,128)S(1)} %get-tuple-element.72.slot, f32[32,8,128]{2,1,0:T(8,128)S(1)} %all_to_all.5.got, bf16[256,6400]{1,0:T(8,128)(2,1)S(1)} %copy-done), custom_call_target="tpu_custom_call" | custom-call | flops 838860800 | bytes 7340032 | tf_op jit(solution)/shard_map/gradient/pallas_call | solution.py:682
  (5 shorter events, 0.0 us)
Async XLA Ops:
  2.3 8.6 %collective-permute-start = (f32[33,8,384]{2,1,0:T(8,128)S(1)}, f32[33,8,384]{2,1,0:T(8,128)S(1)}, u32[]{:S(2)}, u32[]{:S(2)}) collective-permute-start(f32[33,8,384]{2,1,0:T(8,128)S(1)} %get-tuple-element.41), channel_id=1, source_target_pairs={{0,4},{4,0},{8,12},{12,8},{16,20},{20,16},{24,28},{28,24},{1,5},{5... | collective-permute-start | bytes 1216520 | tf_op jit(solution)/shard_map/ppermute | solution.py:701
  2.8 8.0 %collective-permute-start.1 = (f32[32,8,384]{2,1,0:T(8,128)S(1)}, f32[32,8,384]{2,1,0:T(8,128)S(1)}, u32[]{:S(2)}, u32[]{:S(2)}) collective-permute-start(f32[32,8,384]{2,1,0:T(8,128)S(1)} %get-tuple-element.42), channel_id=1, source_target_pairs={{4,8},{12,16},{20,24},{8,4},{16,12},{24,20},{5,9},{13,17},{21,25},... | collective-permute-start | bytes 1179656 | tf_op jit(solution)/shard_map/ppermute | solution.py:703
  3.5 7.4 %copy-start.2 = (s32[256]{0:T(256)S(1)}, s32[256]{0:T(256)}, u32[]{:S(2)}) copy-start(s32[256]{0:T(256)} %param.13) | copy-start | bytes 3076
  11.4 9.7 %collective-permute-start.2 = (f32[2,208,128]{2,1,0:T(8,128)S(1)}, f32[2,208,128]{2,1,0:T(8,128)S(1)}, u32[]{:S(2)}, u32[]{:S(2)}) collective-permute-start(f32[2,208,128]{2,1,0:T(8,128)S(1)} %get-tuple-element.56), channel_id=1, source_target_pairs={{0,1},{1,0},{2,3},{3,2},{4,5},{5,4},{6,7},{7,6},{8,9},{9,8},{10,11... | collective-permute-start | bytes 638984 | tf_op jit(solution)/shard_map/ppermute | solution.py:701
  21.1 9.0 %collective-permute-start.3 = (f32[8,128]{1,0:T(8,128)S(1)}, f32[8,128]{1,0:T(8,128)S(1)}, u32[]{:S(2)}, u32[]{:S(2)}) collective-permute-start(f32[8,128]{1,0:T(8,128)S(1)} %pad_maximum_fusion.2), channel_id=1, source_target_pairs={{0,16},{4,20},{8,24},{12,28},{16,0},{20,4},{24,8},{28,12},{1,17},{... | collective-permute-start | bytes 12296 | tf_op jit(solution)/shard_map/ppermute | solution.py:740
  25.6 12.3 %collective-permute-start.6 = (f32[2,200,128]{2,1,0:T(8,128)S(1)}, f32[2,200,128]{2,1,0:T(8,128)S(1)}, u32[]{:S(2)}, u32[]{:S(2)}) collective-permute-start(f32[2,200,128]{2,1,0:T(8,128)S(1)} %get-tuple-element.66), channel_id=1, source_target_pairs={{1,2},{2,1},{5,6},{6,5},{9,10},{10,9},{13,14},{14,13},{17,18},{18,... | collective-permute-start | bytes 614408 | tf_op jit(solution)/shard_map/ppermute | solution.py:703
  30.2 10.1 %copy-start.1 = (f32[16,16]{1,0:T(8,128)S(1)}, f32[16,16]{1,0:T(8,128)}, u32[]{:S(2)}) copy-start(f32[16,16]{1,0:T(8,128)} %prof.1) | copy-start | bytes 3076
  30.2 4.3 %collective-permute-start.4 = (f32[16,128]{1,0:T(8,128)S(1)}, f32[16,128]{1,0:T(8,128)S(1)}, u32[]{:S(2)}, u32[]{:S(2)}) collective-permute-start(f32[16,128]{1,0:T(8,128)S(1)} %pad_maximum_fusion.1), channel_id=1, source_target_pairs={{0,8},{4,12},{8,0},{12,4},{16,24},{20,28},{24,16},{28,20},{1,9},{5... | collective-permute-start | bytes 24584 | tf_op jit(solution)/shard_map/ppermute | solution.py:740
  34.5 26.0 %copy-start = (bf16[256,6400]{1,0:T(8,128)(2,1)S(1)}, bf16[256,6400]{1,0:T(8,128)(2,1)}, u32[]{:S(2)}) copy-start(bf16[256,6400]{1,0:T(8,128)(2,1)} %burn.1) | copy-start | bytes 9830404
  34.5 5.8 %collective-permute-start.5 = (f32[32,128]{1,0:T(8,128)S(1)}, f32[32,128]{1,0:T(8,128)S(1)}, u32[]{:S(2)}, u32[]{:S(2)}) collective-permute-start(f32[32,128]{1,0:T(8,128)S(1)} %pad_maximum_fusion), channel_id=1, source_target_pairs={{0,2},{1,3},{2,0},{3,1},{4,6},{5,7},{6,4},{7,5},{8,10},{9,11},{10,... | collective-permute-start | bytes 49160 | tf_op jit(solution)/shard_map/ppermute | solution.py:740

commit v4 on v3

--- a/solution.py
+++ b/solution.py
@@ -578,11 +578,11 @@
         send[h] = out
 
     def handlers(n, _):
-        for m in range(2):
-            handler(2 * n + m)
-        return 0
-
-    lax.fori_loop(0, procs // 2, handlers, 0)
+        for m in range(4):
+            handler(4 * n + m)
+        return 0
+
+    lax.fori_loop(0, procs // 4, handlers, 0)
     for c in puts:
         c.wait()
 

time: 64 us -> 63.4 us (level)
  no operation moved by 1% of the time
where the time goes in v4:
time: 63.4 us; the launch traced here: 63.2 us
  Pallas kernels  37.1 us (59%)
  starting transfers between devices  13.8 us (22%)
  blocking collectives  11.3 us (18%)
  between operations  0.86 us (1%)
    pallas_call x4, Pallas kernels, sweep(): pl.pallas_call(functools.partial(sweep_kernel, lev=lev, nx=nx, nt=nt, las...  13.7 us
    all_to_all x1, blocking collectives, on_device(): lax.all_to_all(columns, ('gx', 'gy'), split_axis=0, concat_axis=0, tiled=...  11.3 us
    ppermute x3, starting transfers between devices, widen(): return jnp.concatenate([known, lax.ppermute(known, axis, pairs)], 0)  9.36 us
    pallas_call x1, Pallas kernels, finish(): pl.pallas_call(functools.partial(finish_kernel, lev=lev, nx=nx, nt=nt, ca...  8.23 us
    pallas_call x1, Pallas kernels, prepare(): pl.pallas_call(functools.partial(prepare_kernel, lev=lev, nx=nx, nt=nt, c...  7.32 us
    pallas_call x1, Pallas kernels, gradient(): pl.pallas_call(functools.partial(gradient_kernel, cells=cells, width=widt...  3.32 us
    ppermute x2, starting transfers between devices, exchange(): first = lax.ppermute(near, axis, [(i, i ^ 1) for i in range(count)])  3.12 us
    pallas_call x1, Pallas kernels, strips(): pl.pallas_call(functools.partial(strips_kernel, lev=lev, nx=nx), out_shap...  2.43 us
  transfers between devices with their start and end apart: 7, of which 0 were waited for; matrix products, arithmetic and copies ran while one was open for 0% of the time, Pallas kernels for 37%

profile of v4, /device:TPU:0, one launch (start us, length us, event | category | flops | bytes accessed | tf_op | source)
XLA Modules:
  0.0 63.2 jit_solution(14203408083954141313)
XLA Ops:
  0.6 1.7 %pack_x.1 = (f32[33,8,384]{2,1,0:T(8,128)S(1)}, f32[32,8,384]{2,1,0:T(8,128)S(1)}) custom-call(s32[1]{0:T(128)} %bitcast.3.odd.odd_x, f32[16,192,384]{2,1,0:T(8,128)} %vb.1, f32[16,192,384]{2,1,0:T(8,128)} %vb.1, bf16[16,192,384]{2,1,0:T(8,128)(2,1)} %cub.1, bf16[16,192,384]{2,1,0:T(8,128)(2,1)} %cub.1, bf16[16,192,384]{2,1,0:T(8,128)(2,1)} %cvb.1, ...), custom_call_target="tpu_custom_call" | custom-call | bytes 3145728 | tf_op jit(solution)/shard_map/pack_x/pallas_call | solution.py:81
  2.3 0.5 collective-permute-start
  2.8 0.7 %collective-permute-start.1 = (f32[32,8,384]{2,1,0:T(8,128)S(1)}, f32[32,8,384]{2,1,0:T(8,128)S(1)}, u32[]{:S(2)}, u32[]{:S(2)}) collective-permute-start(f32[32,8,384]{2,1,0:T(8,128)S(1)} %get-tuple-element.42), channel_id=1, source_target_pairs={{4,8},{12,16},{20,24},{8,4},{16,12},{24,20},{5,9},{13,17},{21,25},... | collective-permute-start | bytes 1179656 | tf_op jit(solution)/shard_map/ppermute | solution.py:703
  3.5 0.0 copy-start.2
  3.6 7.3 %prepare.1 = (f32[16,3,224,128]{3,2,1,0:T(8,128)S(1)}, f32[16,3,208,128]{3,2,1,0:T(8,128)S(1)}, f32[16,3,208,128]{3,2,1,0:T(8,128)S(1)}, f32[16,3,208,128]{3,2,1...) custom-call(s32[1]{0:T(128)} %bitcast.1.odd_ref.odd_y.odd, ...), custom_call_target="tpu_custom_call" | custom-call | flops 23592960 | bytes 35651584 | tf_op jit(solution)/shard_map/prepare/pallas_call | solution.py:273
  10.9 0.0 collective-permute-done.1.got_far
  10.9 0.0 collective-permute-done.got_near
  10.9 0.0 copy-done.2
  10.9 0.5 fill.1
  11.4 2.6 %collective-permute-start.2 = (f32[2,208,128]{2,1,0:T(8,128)S(1)}, f32[2,208,128]{2,1,0:T(8,128)S(1)}, u32[]{:S(2)}, u32[]{:S(2)}) collective-permute-start(f32[2,208,128]{2,1,0:T(8,128)S(1)} %get-tuple-element.56), channel_id=1, source_target_pairs={{0,1},{1,0},{2,3},{3,2},{4,5},{5,4},{6,7},{7,6},{8,9},{9,8},{10,11... | collective-permute-start | bytes 638984 | tf_op jit(solution)/shard_map/ppermute | solution.py:701
  14.0 4.0 %sweep.3.src = f32[16,3,224,128]{3,2,1,0:T(8,128)S(1)} custom-call(f32[16,3,224,128]{3,2,1,0:T(8,128)S(1)} %get-tuple-element.52.src, f32[16,3,208,128]{3,2,1,0:T(8,128)S(1)} %get-tuple-element.53.cuf, f32[16,3,208,128]{3,2,1,0:T(8,128)S(1)} %get-tuple-element.54.cvf, f32[16,3,208,128]{3,2,1,0:T(8,128)S(1)} %get-tuple-element.55.refs_0_), custom_call_target="tpu_custom_call" | custom-call | flops 21233664 | bytes 16777216 | tf_op jit(solution)/shard_map/sweep/pallas_call | solution.py:407
  17.9 3.1 %sweep.4.src = f32[16,3,224,128]{3,2,1,0:T(8,128)S(1)} custom-call(f32[16,3,224,128]{3,2,1,0:T(8,128)S(1)} %sweep.3.src, f32[16,3,208,128]{3,2,1,0:T(8,128)S(1)} %get-tuple-element.53.cuf, f32[16,3,208,128]{3,2,1,0:T(8,128)S(1)} %get-tuple-element.54.cvf, f32[16,3,208,128]{3,2,1,0:T(8,128)S(1)} %get-tuple-element.55.refs_0_), custom_call_target="tpu_custom_call" | custom-call | flops 21233664 | bytes 16777216 | tf_op jit(solution)/shard_map/sweep/pallas_call | solution.py:407
  21.1 0.0 collective-permute-done.2.got_near
  21.1 4.4 %collective-permute-start.3 = (f32[8,128]{1,0:T(8,128)S(1)}, f32[8,128]{1,0:T(8,128)S(1)}, u32[]{:S(2)}, u32[]{:S(2)}) collective-permute-start(f32[8,128]{1,0:T(8,128)S(1)} %pad_maximum_fusion.2), channel_id=1, source_target_pairs={{0,16},{4,20},{8,24},{12,28},{16,0},{20,4},{24,8},{28,12},{1,17},{... | collective-permute-start | bytes 12296 | tf_op jit(solution)/shard_map/ppermute | solution.py:740
  25.6 0.7 %collective-permute-start.6 = (f32[2,200,128]{2,1,0:T(8,128)S(1)}, f32[2,200,128]{2,1,0:T(8,128)S(1)}, u32[]{:S(2)}, u32[]{:S(2)}) collective-permute-start(f32[2,200,128]{2,1,0:T(8,128)S(1)} %get-tuple-element.66), channel_id=1, source_target_pairs={{1,2},{2,1},{5,6},{6,5},{9,10},{10,9},{13,14},{14,13},{17,18},{18,... | collective-permute-start | bytes 614408 | tf_op jit(solution)/shard_map/ppermute | solution.py:703
  26.2 3.9 %sweep.5.src = f32[16,3,224,128]{3,2,1,0:T(8,128)S(1)} custom-call(f32[16,3,224,128]{3,2,1,0:T(8,128)S(1)} %sweep.4.src, f32[16,3,208,128]{3,2,1,0:T(8,128)S(1)} %get-tuple-element.53.cuf, f32[16,3,208,128]{3,2,1,0:T(8,128)S(1)} %get-tuple-element.54.cvf, f32[16,3,208,128]{3,2,1,0:T(8,128)S(1)} %get-tuple-element.55.refs_0_), custom_call_target="tpu_custom_call" | custom-call | flops 21233664 | bytes 16777216 | tf_op jit(solution)/shard_map/sweep/pallas_call | solution.py:407
  30.2 0.0 collective-permute-done.3
  30.2 0.0 copy-start.1
  30.2 1.6 %collective-permute-start.4 = (f32[16,128]{1,0:T(8,128)S(1)}, f32[16,128]{1,0:T(8,128)S(1)}, u32[]{:S(2)}, u32[]{:S(2)}) collective-permute-start(f32[16,128]{1,0:T(8,128)S(1)} %pad_maximum_fusion.1), channel_id=1, source_target_pairs={{0,8},{4,12},{8,0},{12,4},{16,24},{20,28},{24,16},{28,20},{1,9},{5... | collective-permute-start | bytes 24584 | tf_op jit(solution)/shard_map/ppermute | solution.py:740
  31.8 2.6 %sweep_last.1.mid = f32[72,16,8,128]{3,2,1,0:T(8,128)S(1)} custom-call(f32[16,3,224,128]{3,2,1,0:T(8,128)S(1)} %sweep.5.src, f32[16,3,208,128]{3,2,1,0:T(8,128)S(1)} %get-tuple-element.53.cuf, f32[16,3,208,128]{3,2,1,0:T(8,128)S(1)} %get-tuple-element.54.cvf), custom_call_target="tpu_custom_call" | custom-call | flops 21233664 | bytes 16777216 | tf_op jit(solution)/shard_map/sweep_last/pallas_call | solution.py:407
  34.5 0.0 copy-start
  34.5 0.0 collective-permute-done.4
  34.5 3.3 %collective-permute-start.5 = (f32[32,128]{1,0:T(8,128)S(1)}, f32[32,128]{1,0:T(8,128)S(1)}, u32[]{:S(2)}, u32[]{:S(2)}) collective-permute-start(f32[32,128]{1,0:T(8,128)S(1)} %pad_maximum_fusion), channel_id=1, source_target_pairs={{0,2},{1,3},{2,0},{3,1},{4,6},{5,7},{6,4},{7,5},{8,10},{9,11},{10,... | collective-permute-start | bytes 49160 | tf_op jit(solution)/shard_map/ppermute | solution.py:740
  37.8 0.0 collective-permute-done.6.got_far
  37.8 2.4 %strips.1 = (f32[192,128]{1,0:T(8,128)S(1)}, f32[192,128]{1,0:T(8,128)S(1)}) custom-call(s32[1]{0:T(128)} %bitcast.1.odd_ref.odd_y.odd, f32[4,200,128]{2,1,0:T(8,128)S(1)} %get-tuple-element.64.own_l, f32[4,200,128]{2,1,0:T(8,128)S(1)} %get-tuple-element.65.own_r, f32[2,208,128]{2,1,0:T(8,128)S(1)} %collective-permute-done.2.got_near, ...), custom_call_target="tpu_custom_call" | custom-call | flops 10485760 | bytes 3145728 | tf_op jit(solution)/shard_map/strips/pallas_call | solution.py:501
  40.3 0.0 collective-permute-done.5
  40.3 0.0 copy-done.1
  40.3 8.2 %finish.1 = (f32[16,24,8,384]{3,2,1,0:T(8,128)}, f32[32,8,128]{2,1,0:T(8,128)S(1)}, f32[72,16,8,128]{3,2,1,0:T(8,128)S(1)}) custom-call(s32[1]{0:T(128)} %bitcast.me_ref, s32[32,128]{1,0:T(8,128)S(1)} %get-tuple-element.38.row, s32[32,128]{1,0:T(8,128)S(1)} %get-tuple-element.39.shift, ...), custom_call_target="tpu_custom_call", output_to_operand_aliasing={{2}: (8, {})} | custom-call | flops 31457280 | bytes 20971520 | tf_op jit(solution)/shard_map/finish/pallas_call | solution.py:594
  48.5 11.3 %all_to_all.5.got = f32[32,8,128]{2,1,0:T(8,128)S(1)} all-to-all(f32[32,8,128]{2,1,0:T(8,128)S(1)} %get-tuple-element.73), channel_id=1, replica_groups=mesh['gx'=8,'gy'=4] {'gx','gy'}, dimensions={0} | all-to-all | bytes 262144 | tf_op jit(solution)/shard_map/all_to_all | solution.py:768
  59.9 0.0 copy-done
  59.9 3.3 %gradient.1 = bf16[256,6400]{1,0:T(8,128)(2,1)} custom-call(s32[256,1]{1,0:T(8,128)S(1)} %get-tuple-element.71.src, s32[256,1]{1,0:T(8,128)S(1)} %get-tuple-element.72.slot, f32[32,8,128]{2,1,0:T(8,128)S(1)} %all_to_all.5.got, bf16[256,6400]{1,0:T(8,128)(2,1)S(1)} %copy-done), custom_call_target="tpu_custom_call" | custom-call | flops 838860800 | bytes 7340032 | tf_op jit(solution)/shard_map/gradient/pallas_call | solution.py:682
  (5 shorter events, 0.0 us)
Async XLA Ops:
  2.3 8.6 %collective-permute-start = (f32[33,8,384]{2,1,0:T(8,128)S(1)}, f32[33,8,384]{2,1,0:T(8,128)S(1)}, u32[]{:S(2)}, u32[]{:S(2)}) collective-permute-start(f32[33,8,384]{2,1,0:T(8,128)S(1)} %get-tuple-element.41), channel_id=1, source_target_pairs={{0,4},{4,0},{8,12},{12,8},{16,20},{20,16},{24,28},{28,24},{1,5},{5... | collective-permute-start | bytes 1216520 | tf_op jit(solution)/shard_map/ppermute | solution.py:701
  2.8 8.0 %collective-permute-start.1 = (f32[32,8,384]{2,1,0:T(8,128)S(1)}, f32[32,8,384]{2,1,0:T(8,128)S(1)}, u32[]{:S(2)}, u32[]{:S(2)}) collective-permute-start(f32[32,8,384]{2,1,0:T(8,128)S(1)} %get-tuple-element.42), channel_id=1, source_target_pairs={{4,8},{12,16},{20,24},{8,4},{16,12},{24,20},{5,9},{13,17},{21,25},... | collective-permute-start | bytes 1179656 | tf_op jit(solution)/shard_map/ppermute | solution.py:703
  3.5 7.4 %copy-start.2 = (s32[256]{0:T(256)S(1)}, s32[256]{0:T(256)}, u32[]{:S(2)}) copy-start(s32[256]{0:T(256)} %param.13) | copy-start | bytes 3076
  11.4 9.7 %collective-permute-start.2 = (f32[2,208,128]{2,1,0:T(8,128)S(1)}, f32[2,208,128]{2,1,0:T(8,128)S(1)}, u32[]{:S(2)}, u32[]{:S(2)}) collective-permute-start(f32[2,208,128]{2,1,0:T(8,128)S(1)} %get-tuple-element.56), channel_id=1, source_target_pairs={{0,1},{1,0},{2,3},{3,2},{4,5},{5,4},{6,7},{7,6},{8,9},{9,8},{10,11... | collective-permute-start | bytes 638984 | tf_op jit(solution)/shard_map/ppermute | solution.py:701
  21.1 9.0 %collective-permute-start.3 = (f32[8,128]{1,0:T(8,128)S(1)}, f32[8,128]{1,0:T(8,128)S(1)}, u32[]{:S(2)}, u32[]{:S(2)}) collective-permute-start(f32[8,128]{1,0:T(8,128)S(1)} %pad_maximum_fusion.2), channel_id=1, source_target_pairs={{0,16},{4,20},{8,24},{12,28},{16,0},{20,4},{24,8},{28,12},{1,17},{... | collective-permute-start | bytes 12296 | tf_op jit(solution)/shard_map/ppermute | solution.py:740
  25.6 12.3 %collective-permute-start.6 = (f32[2,200,128]{2,1,0:T(8,128)S(1)}, f32[2,200,128]{2,1,0:T(8,128)S(1)}, u32[]{:S(2)}, u32[]{:S(2)}) collective-permute-start(f32[2,200,128]{2,1,0:T(8,128)S(1)} %get-tuple-element.66), channel_id=1, source_target_pairs={{1,2},{2,1},{5,6},{6,5},{9,10},{10,9},{13,14},{14,13},{17,18},{18,... | collective-permute-start | bytes 614408 | tf_op jit(solution)/shard_map/ppermute | solution.py:703
  30.2 10.1 %copy-start.1 = (f32[16,16]{1,0:T(8,128)S(1)}, f32[16,16]{1,0:T(8,128)}, u32[]{:S(2)}) copy-start(f32[16,16]{1,0:T(8,128)} %prof.1) | copy-start | bytes 3076
  30.2 4.3 %collective-permute-start.4 = (f32[16,128]{1,0:T(8,128)S(1)}, f32[16,128]{1,0:T(8,128)S(1)}, u32[]{:S(2)}, u32[]{:S(2)}) collective-permute-start(f32[16,128]{1,0:T(8,128)S(1)} %pad_maximum_fusion.1), channel_id=1, source_target_pairs={{0,8},{4,12},{8,0},{12,4},{16,24},{20,28},{24,16},{28,20},{1,9},{5... | collective-permute-start | bytes 24584 | tf_op jit(solution)/shard_map/ppermute | solution.py:740
  34.5 25.4 %copy-start = (bf16[256,6400]{1,0:T(8,128)(2,1)S(1)}, bf16[256,6400]{1,0:T(8,128)(2,1)}, u32[]{:S(2)}) copy-start(bf16[256,6400]{1,0:T(8,128)(2,1)} %burn.1) | copy-start | bytes 9830404
  34.5 5.8 %collective-permute-start.5 = (f32[32,128]{1,0:T(8,128)S(1)}, f32[32,128]{1,0:T(8,128)S(1)}, u32[]{:S(2)}, u32[]{:S(2)}) collective-permute-start(f32[32,128]{1,0:T(8,128)S(1)} %pad_maximum_fusion), channel_id=1, source_target_pairs={{0,2},{1,3},{2,0},{3,1},{4,6},{5,7},{6,4},{7,5},{8,10},{9,11},{10,... | collective-permute-start | bytes 49160 | tf_op jit(solution)/shard_map/ppermute | solution.py:740

commit v5 on v4

--- a/solution.py
+++ b/solution.py
@@ -530,8 +530,8 @@
     base = (nt - 1) * nx // SUBL
 
     def patch(n, _):
-        for m in range(2):
-            l = 2 * n + m
+        for m in range(4):
+            l = 4 * n + m
             take_l = (lane8 * lev + (LANES // 2 + l)) & (LANES - 1)
             take_r = ((lane8 - (LANES - width)) * lev + l) & (LANES - 1)
             for g in range(0, nx, SUBL):
@@ -544,7 +544,7 @@
                 field[g, l] = jnp.where(inner, y, field[g, l])
         return 0
 
-    lax.fori_loop(0, lev // 2, patch, 0)
+    lax.fori_loop(0, lev // 4, patch, 0)
     count = nx // SUBL
     puts = [
         pltpu.make_async_copy(

time: 63.4 us -> 63.3 us (level)
  no operation moved by 1% of the time
where the time goes in v5:
time: 63.3 us; the launch traced here: 63.1 us
  Pallas kernels  37 us (58%)
  starting transfers between devices  13.8 us (22%)
  blocking collectives  11.3 us (18%)
  between operations  0.86 us (1%)
    pallas_call x4, Pallas kernels, sweep(): pl.pallas_call(functools.partial(sweep_kernel, lev=lev, nx=nx, nt=nt, las...  13.7 us
    all_to_all x1, blocking collectives, on_device(): lax.all_to_all(columns, ('gx', 'gy'), split_axis=0, concat_axis=0, tiled=...  11.3 us
    ppermute x3, starting transfers between devices, widen(): return jnp.concatenate([known, lax.ppermute(known, axis, pairs)], 0)  9.36 us
    pallas_call x1, Pallas kernels, finish(): pl.pallas_call(functools.partial(finish_kernel, lev=lev, nx=nx, nt=nt, ca...  8.13 us
    pallas_call x1, Pallas kernels, prepare(): pl.pallas_call(functools.partial(prepare_kernel, lev=lev, nx=nx, nt=nt, c...  7.32 us
    pallas_call x1, Pallas kernels, gradient(): pl.pallas_call(functools.partial(gradient_kernel, cells=cells, width=widt...  3.32 us
    ppermute x2, starting transfers between devices, exchange(): first = lax.ppermute(near, axis, [(i, i ^ 1) for i in range(count)])  3.12 us
    pallas_call x1, Pallas kernels, strips(): pl.pallas_call(functools.partial(strips_kernel, lev=lev, nx=nx), out_shap...  2.43 us
  transfers between devices with their start and end apart: 7, of which 0 were waited for; matrix products, arithmetic and copies ran while one was open for 0% of the time, Pallas kernels for 37%

profile of v5, /device:TPU:0, one launch (start us, length us, event | category | flops | bytes accessed | tf_op | source)
XLA Modules:
  0.0 63.1 jit_solution(17609996924433797670)
XLA Ops:
  0.6 1.7 %pack_x.1 = (f32[33,8,384]{2,1,0:T(8,128)S(1)}, f32[32,8,384]{2,1,0:T(8,128)S(1)}) custom-call(s32[1]{0:T(128)} %bitcast.3.odd.odd_x, f32[16,192,384]{2,1,0:T(8,128)} %vb.1, f32[16,192,384]{2,1,0:T(8,128)} %vb.1, bf16[16,192,384]{2,1,0:T(8,128)(2,1)} %cub.1, bf16[16,192,384]{2,1,0:T(8,128)(2,1)} %cub.1, bf16[16,192,384]{2,1,0:T(8,128)(2,1)} %cvb.1, ...), custom_call_target="tpu_custom_call" | custom-call | bytes 3145728 | tf_op jit(solution)/shard_map/pack_x/pallas_call | solution.py:81
  2.3 0.5 collective-permute-start
  2.8 0.7 %collective-permute-start.1 = (f32[32,8,384]{2,1,0:T(8,128)S(1)}, f32[32,8,384]{2,1,0:T(8,128)S(1)}, u32[]{:S(2)}, u32[]{:S(2)}) collective-permute-start(f32[32,8,384]{2,1,0:T(8,128)S(1)} %get-tuple-element.42), channel_id=1, source_target_pairs={{4,8},{12,16},{20,24},{8,4},{16,12},{24,20},{5,9},{13,17},{21,25},... | collective-permute-start | bytes 1179656 | tf_op jit(solution)/shard_map/ppermute | solution.py:703
  3.5 0.0 copy-start.2
  3.6 7.3 %prepare.1 = (f32[16,3,224,128]{3,2,1,0:T(8,128)S(1)}, f32[16,3,208,128]{3,2,1,0:T(8,128)S(1)}, f32[16,3,208,128]{3,2,1,0:T(8,128)S(1)}, f32[16,3,208,128]{3,2,1...) custom-call(s32[1]{0:T(128)} %bitcast.1.odd_ref.odd_y.odd, ...), custom_call_target="tpu_custom_call" | custom-call | flops 23592960 | bytes 35651584 | tf_op jit(solution)/shard_map/prepare/pallas_call | solution.py:273
  10.9 0.0 collective-permute-done.1.got_far
  10.9 0.0 collective-permute-done.got_near
  10.9 0.0 copy-done.2
  10.9 0.5 fill.1
  11.4 2.6 %collective-permute-start.2 = (f32[2,208,128]{2,1,0:T(8,128)S(1)}, f32[2,208,128]{2,1,0:T(8,128)S(1)}, u32[]{:S(2)}, u32[]{:S(2)}) collective-permute-start(f32[2,208,128]{2,1,0:T(8,128)S(1)} %get-tuple-element.56), channel_id=1, source_target_pairs={{0,1},{1,0},{2,3},{3,2},{4,5},{5,4},{6,7},{7,6},{8,9},{9,8},{10,11... | collective-permute-start | bytes 638984 | tf_op jit(solution)/shard_map/ppermute | solution.py:701
  14.0 4.0 %sweep.3.src = f32[16,3,224,128]{3,2,1,0:T(8,128)S(1)} custom-call(f32[16,3,224,128]{3,2,1,0:T(8,128)S(1)} %get-tuple-element.52.src, f32[16,3,208,128]{3,2,1,0:T(8,128)S(1)} %get-tuple-element.53.cuf, f32[16,3,208,128]{3,2,1,0:T(8,128)S(1)} %get-tuple-element.54.cvf, f32[16,3,208,128]{3,2,1,0:T(8,128)S(1)} %get-tuple-element.55.refs_0_), custom_call_target="tpu_custom_call" | custom-call | flops 21233664 | bytes 16777216 | tf_op jit(solution)/shard_map/sweep/pallas_call | solution.py:407
  17.9 3.1 %sweep.4.src = f32[16,3,224,128]{3,2,1,0:T(8,128)S(1)} custom-call(f32[16,3,224,128]{3,2,1,0:T(8,128)S(1)} %sweep.3.src, f32[16,3,208,128]{3,2,1,0:T(8,128)S(1)} %get-tuple-element.53.cuf, f32[16,3,208,128]{3,2,1,0:T(8,128)S(1)} %get-tuple-element.54.cvf, f32[16,3,208,128]{3,2,1,0:T(8,128)S(1)} %get-tuple-element.55.refs_0_), custom_call_target="tpu_custom_call" | custom-call | flops 21233664 | bytes 16777216 | tf_op jit(solution)/shard_map/sweep/pallas_call | solution.py:407
  21.1 0.0 collective-permute-done.2.got_near
  21.1 4.4 %collective-permute-start.3 = (f32[8,128]{1,0:T(8,128)S(1)}, f32[8,128]{1,0:T(8,128)S(1)}, u32[]{:S(2)}, u32[]{:S(2)}) collective-permute-start(f32[8,128]{1,0:T(8,128)S(1)} %pad_maximum_fusion.2), channel_id=1, source_target_pairs={{0,16},{4,20},{8,24},{12,28},{16,0},{20,4},{24,8},{28,12},{1,17},{... | collective-permute-start | bytes 12296 | tf_op jit(solution)/shard_map/ppermute | solution.py:740
  25.6 0.7 %collective-permute-start.6 = (f32[2,200,128]{2,1,0:T(8,128)S(1)}, f32[2,200,128]{2,1,0:T(8,128)S(1)}, u32[]{:S(2)}, u32[]{:S(2)}) collective-permute-start(f32[2,200,128]{2,1,0:T(8,128)S(1)} %get-tuple-element.66), channel_id=1, source_target_pairs={{1,2},{2,1},{5,6},{6,5},{9,10},{10,9},{13,14},{14,13},{17,18},{18,... | collective-permute-start | bytes 614408 | tf_op jit(solution)/shard_map/ppermute | solution.py:703
  26.2 3.9 %sweep.5.src = f32[16,3,224,128]{3,2,1,0:T(8,128)S(1)} custom-call(f32[16,3,224,128]{3,2,1,0:T(8,128)S(1)} %sweep.4.src, f32[16,3,208,128]{3,2,1,0:T(8,128)S(1)} %get-tuple-element.53.cuf, f32[16,3,208,128]{3,2,1,0:T(8,128)S(1)} %get-tuple-element.54.cvf, f32[16,3,208,128]{3,2,1,0:T(8,128)S(1)} %get-tuple-element.55.refs_0_), custom_call_target="tpu_custom_call" | custom-call | flops 21233664 | bytes 16777216 | tf_op jit(solution)/shard_map/sweep/pallas_call | solution.py:407
  30.2 0.0 collective-permute-done.3
  30.2 0.0 copy-start.1
  30.2 1.6 %collective-permute-start.4 = (f32[16,128]{1,0:T(8,128)S(1)}, f32[16,128]{1,0:T(8,128)S(1)}, u32[]{:S(2)}, u32[]{:S(2)}) collective-permute-start(f32[16,128]{1,0:T(8,128)S(1)} %pad_maximum_fusion.1), channel_id=1, source_target_pairs={{0,8},{4,12},{8,0},{12,4},{16,24},{20,28},{24,16},{28,20},{1,9},{5... | collective-permute-start | bytes 24584 | tf_op jit(solution)/shard_map/ppermute | solution.py:740
  31.8 2.6 %sweep_last.1.mid = f32[72,16,8,128]{3,2,1,0:T(8,128)S(1)} custom-call(f32[16,3,224,128]{3,2,1,0:T(8,128)S(1)} %sweep.5.src, f32[16,3,208,128]{3,2,1,0:T(8,128)S(1)} %get-tuple-element.53.cuf, f32[16,3,208,128]{3,2,1,0:T(8,128)S(1)} %get-tuple-element.54.cvf), custom_call_target="tpu_custom_call" | custom-call | flops 21233664 | bytes 16777216 | tf_op jit(solution)/shard_map/sweep_last/pallas_call | solution.py:407
  34.5 0.0 copy-start
  34.5 0.0 collective-permute-done.4
  34.5 3.3 %collective-permute-start.5 = (f32[32,128]{1,0:T(8,128)S(1)}, f32[32,128]{1,0:T(8,128)S(1)}, u32[]{:S(2)}, u32[]{:S(2)}) collective-permute-start(f32[32,128]{1,0:T(8,128)S(1)} %pad_maximum_fusion), channel_id=1, source_target_pairs={{0,2},{1,3},{2,0},{3,1},{4,6},{5,7},{6,4},{7,5},{8,10},{9,11},{10,... | collective-permute-start | bytes 49160 | tf_op jit(solution)/shard_map/ppermute | solution.py:740
  37.8 0.0 collective-permute-done.6.got_far
  37.8 2.4 %strips.1 = (f32[192,128]{1,0:T(8,128)S(1)}, f32[192,128]{1,0:T(8,128)S(1)}) custom-call(s32[1]{0:T(128)} %bitcast.1.odd_ref.odd_y.odd, f32[4,200,128]{2,1,0:T(8,128)S(1)} %get-tuple-element.64.own_l, f32[4,200,128]{2,1,0:T(8,128)S(1)} %get-tuple-element.65.own_r, f32[2,208,128]{2,1,0:T(8,128)S(1)} %collective-permute-done.2.got_near, ...), custom_call_target="tpu_custom_call" | custom-call | flops 10485760 | bytes 3145728 | tf_op jit(solution)/shard_map/strips/pallas_call | solution.py:501
  40.3 0.0 collective-permute-done.5
  40.3 0.0 copy-done.1
  40.3 8.1 %finish.1 = (f32[16,24,8,384]{3,2,1,0:T(8,128)}, f32[32,8,128]{2,1,0:T(8,128)S(1)}, f32[72,16,8,128]{3,2,1,0:T(8,128)S(1)}) custom-call(s32[1]{0:T(128)} %bitcast.me_ref, s32[32,128]{1,0:T(8,128)S(1)} %get-tuple-element.38.row, s32[32,128]{1,0:T(8,128)S(1)} %get-tuple-element.39.shift, ...), custom_call_target="tpu_custom_call", output_to_operand_aliasing={{2}: (8, {})} | custom-call | flops 31457280 | bytes 20971520 | tf_op jit(solution)/shard_map/finish/pallas_call | solution.py:594
  48.4 11.3 %all_to_all.5.got = f32[32,8,128]{2,1,0:T(8,128)S(1)} all-to-all(f32[32,8,128]{2,1,0:T(8,128)S(1)} %get-tuple-element.73), channel_id=1, replica_groups=mesh['gx'=8,'gy'=4] {'gx','gy'}, dimensions={0} | all-to-all | bytes 262144 | tf_op jit(solution)/shard_map/all_to_all | solution.py:768
  59.8 0.0 copy-done
  59.8 3.3 %gradient.1 = bf16[256,6400]{1,0:T(8,128)(2,1)} custom-call(s32[256,1]{1,0:T(8,128)S(1)} %get-tuple-element.71.src, s32[256,1]{1,0:T(8,128)S(1)} %get-tuple-element.72.slot, f32[32,8,128]{2,1,0:T(8,128)S(1)} %all_to_all.5.got, bf16[256,6400]{1,0:T(8,128)(2,1)S(1)} %copy-done), custom_call_target="tpu_custom_call" | custom-call | flops 838860800 | bytes 7340032 | tf_op jit(solution)/shard_map/gradient/pallas_call | solution.py:682
  (5 shorter events, 0.0 us)
Async XLA Ops:
  2.3 8.6 %collective-permute-start = (f32[33,8,384]{2,1,0:T(8,128)S(1)}, f32[33,8,384]{2,1,0:T(8,128)S(1)}, u32[]{:S(2)}, u32[]{:S(2)}) collective-permute-start(f32[33,8,384]{2,1,0:T(8,128)S(1)} %get-tuple-element.41), channel_id=1, source_target_pairs={{0,4},{4,0},{8,12},{12,8},{16,20},{20,16},{24,28},{28,24},{1,5},{5... | collective-permute-start | bytes 1216520 | tf_op jit(solution)/shard_map/ppermute | solution.py:701
  2.8 8.0 %collective-permute-start.1 = (f32[32,8,384]{2,1,0:T(8,128)S(1)}, f32[32,8,384]{2,1,0:T(8,128)S(1)}, u32[]{:S(2)}, u32[]{:S(2)}) collective-permute-start(f32[32,8,384]{2,1,0:T(8,128)S(1)} %get-tuple-element.42), channel_id=1, source_target_pairs={{4,8},{12,16},{20,24},{8,4},{16,12},{24,20},{5,9},{13,17},{21,25},... | collective-permute-start | bytes 1179656 | tf_op jit(solution)/shard_map/ppermute | solution.py:703
  3.5 7.4 %copy-start.2 = (s32[256]{0:T(256)S(1)}, s32[256]{0:T(256)}, u32[]{:S(2)}) copy-start(s32[256]{0:T(256)} %param.13) | copy-start | bytes 3076
  11.4 9.7 %collective-permute-start.2 = (f32[2,208,128]{2,1,0:T(8,128)S(1)}, f32[2,208,128]{2,1,0:T(8,128)S(1)}, u32[]{:S(2)}, u32[]{:S(2)}) collective-permute-start(f32[2,208,128]{2,1,0:T(8,128)S(1)} %get-tuple-element.56), channel_id=1, source_target_pairs={{0,1},{1,0},{2,3},{3,2},{4,5},{5,4},{6,7},{7,6},{8,9},{9,8},{10,11... | collective-permute-start | bytes 638984 | tf_op jit(solution)/shard_map/ppermute | solution.py:701
  21.1 9.0 %collective-permute-start.3 = (f32[8,128]{1,0:T(8,128)S(1)}, f32[8,128]{1,0:T(8,128)S(1)}, u32[]{:S(2)}, u32[]{:S(2)}) collective-permute-start(f32[8,128]{1,0:T(8,128)S(1)} %pad_maximum_fusion.2), channel_id=1, source_target_pairs={{0,16},{4,20},{8,24},{12,28},{16,0},{20,4},{24,8},{28,12},{1,17},{... | collective-permute-start | bytes 12296 | tf_op jit(solution)/shard_map/ppermute | solution.py:740
  25.6 12.3 %collective-permute-start.6 = (f32[2,200,128]{2,1,0:T(8,128)S(1)}, f32[2,200,128]{2,1,0:T(8,128)S(1)}, u32[]{:S(2)}, u32[]{:S(2)}) collective-permute-start(f32[2,200,128]{2,1,0:T(8,128)S(1)} %get-tuple-element.66), channel_id=1, source_target_pairs={{1,2},{2,1},{5,6},{6,5},{9,10},{10,9},{13,14},{14,13},{17,18},{18,... | collective-permute-start | bytes 614408 | tf_op jit(solution)/shard_map/ppermute | solution.py:703
  30.2 10.1 %copy-start.1 = (f32[16,16]{1,0:T(8,128)S(1)}, f32[16,16]{1,0:T(8,128)}, u32[]{:S(2)}) copy-start(f32[16,16]{1,0:T(8,128)} %prof.1) | copy-start | bytes 3076
  30.2 4.3 %collective-permute-start.4 = (f32[16,128]{1,0:T(8,128)S(1)}, f32[16,128]{1,0:T(8,128)S(1)}, u32[]{:S(2)}, u32[]{:S(2)}) collective-permute-start(f32[16,128]{1,0:T(8,128)S(1)} %pad_maximum_fusion.1), channel_id=1, source_target_pairs={{0,8},{4,12},{8,0},{12,4},{16,24},{20,28},{24,16},{28,20},{1,9},{5... | collective-permute-start | bytes 24584 | tf_op jit(solution)/shard_map/ppermute | solution.py:740
  34.5 25.3 %copy-start = (bf16[256,6400]{1,0:T(8,128)(2,1)S(1)}, bf16[256,6400]{1,0:T(8,128)(2,1)}, u32[]{:S(2)}) copy-start(bf16[256,6400]{1,0:T(8,128)(2,1)} %burn.1) | copy-start | bytes 9830404
  34.5 5.8 %collective-permute-start.5 = (f32[32,128]{1,0:T(8,128)S(1)}, f32[32,128]{1,0:T(8,128)S(1)}, u32[]{:S(2)}, u32[]{:S(2)}) collective-permute-start(f32[32,128]{1,0:T(8,128)S(1)} %pad_maximum_fusion), channel_id=1, source_target_pairs={{0,2},{1,3},{2,0},{3,1},{4,6},{5,7},{6,4},{7,5},{8,10},{9,11},{10,... | collective-permute-start | bytes 49160 | tf_op jit(solution)/shard_map/ppermute | solution.py:740
